TPU v7x, 256 devices: a whole 4x4x8 slice. The times are simulated.
256 devices in a mesh: tbl: 64 (over z, x, core), hst: 4 (over y).
Axes of the slice: x: 4, y: 4, z: 8, core: 2. Of those that a mesh axis runs over, the one named last changes fastest.
Arguments:
- pooled: bfloat16 [32768, 1024], P('tbl'), may hold values from -16 to 16
- w_up: bfloat16 [1024, 4096], P(None, 'hst'), may hold values from -0.1875 to 0.1875
- grad_out: bfloat16 [32768, 4096], P('tbl', 'hst'), may hold values from -6 to 6
- owners: int32 [8, 32768, 8], P('hst', 'tbl'), may hold values from 0 to 63, all different within a row; in each aligned block of 512 rows (0 to 511, 512 to 1023, ..., all dimensions but the last counted through in order) at most 128 rows name the same one
- rows: int32 [8, 32768, 8], P('hst', 'tbl'), may hold values from 0 to 1023
- lookup_weight: bfloat16 [8, 32768, 8], P('hst', 'tbl'), may hold values from 0.25 to 2
- lens: int32 [8, 32768], P('hst', 'tbl'), may hold values from 4 to 8
- slot_map: int32 [64, 4, 2048], P('tbl', 'hst'), may hold values from 0 to 2047, each once within a row
- cache_weight: float32 [64, 4, 2048, 128], P('tbl', 'hst'), may hold values from -6 to 6
- cache_accum: float32 [64, 4, 2048], P('tbl', 'hst'), may hold values from 0.1 to 10
- evict_slots: int32 [64, 4, 256], P('tbl', 'hst'), may hold values from 0 to 2047, as said below
- evict_dest: int32 [64, 4, 256], P('tbl', 'hst'), may hold values from 0 to 3, as said below
- evict_count: int32 [64, 4], P('tbl', 'hst'), may hold values from 128 to 256
Outputs:
- grad_up: float32 [1024, 4096], P('tbl', 'hst')
- new_weight: float32 [64, 4, 2048, 128], P('tbl', 'hst')
- new_accum: float32 [64, 4, 2048], P('tbl', 'hst')
- held_rows: float32 [64, 4, 4, 128, 128], P('tbl', 'hst')
- held_accum: float32 [64, 4, 4, 128], P('tbl', 'hst')
Inputs may be any that keep to these rules, and one draw needn't show every extreme that they name: The 8 owners of one bag differ. Among the 512 samples of one index of tbl and one table, no owner is named by more than 128 lookup positions, used or not; some owner is named by exactly 128 in some such block. `evict_slots`: the 256 slots of one device's list differ. `evict_dest`: among the used entries of one device, no holder appears more than 128 times, and one holder appears exactly 128 times.
All inputs are finite; a program needn't handle non-finite values.
Results may differ from a plain program's by a relative error of at most 0.0029.
Values may be sent and summed in bfloat16 or wider, within the bound.
No kernel may reach another device: no remote copies, remote signals or barrier semaphores. Data moves between devices by JAX's collectives and lax.ppermute only.
A program may use at most 64 MiB of HBM per device.

v0:
```python
import functools

import jax
import jax.numpy as jnp
from jax import lax
from jax.experimental import pallas as pl
from jax.experimental.pallas import tpu as pltpu
from jax.sharding import Mesh
from jax.sharding import PartitionSpec as P

TBL = ("tbl_0", "tbl_1", "tbl_2")
Z, X, C, H = "tbl_0", "tbl_1", "tbl_2", "hst"

LEARN_RATE = 0.05
EPSILON = 1e-08
F32 = jnp.float32
BF16 = jnp.bfloat16
I32 = jnp.int32
VMEM = pl.BlockSpec(memory_space=pltpu.VMEM)
SMEM = pl.BlockSpec(memory_space=pltpu.SMEM)
MOST = 128
HELD = 136


def shifted(x, axis, step):
    size = lax.axis_size(axis)
    return lax.ppermute(x, axis, [(i, (i + step) % size) for i in range(size)])


def call(body, ins, outs, scratch, flops, moved, name):
    return pl.pallas_call(
        body,
        in_specs=ins,
        out_specs=[VMEM] * len(outs),
        out_shape=outs,
        scratch_shapes=scratch,
        compiler_params=pltpu.CompilerParams(vmem_limit_bytes=48 << 20),
        cost_estimate=pl.CostEstimate(flops=flops, bytes_accessed=moved, transcendentals=0),
        name=name,
    )


def top_kernel(pos, pooled, w_up, grad_out, delta, own, one, two, three, feature):
    width = 256

    def column(i, carry):
        at = pl.ds(pl.multiple_of(i * width, width), width)
        preact = jnp.dot(pooled[...], w_up[:, at], preferred_element_type=F32)
        s = jax.nn.sigmoid(preact)
        delta[:, at] = (grad_out[:, at].astype(F32) * s * (1.0 + preact * (1.0 - s))).astype(BF16)
        return carry

    lax.fori_loop(0, 4, column, 0)
    h = pos[3]

    def part(k, carry):
        row = pl.multiple_of(lax.rem(h + k, 4) * width, width)
        feature[k] = lax.dot_general(
            delta[...],
            w_up[pl.ds(row, width), :],
            (((1,), (1,)), ((), ())),
            preferred_element_type=F32,
        )
        return carry

    lax.fori_loop(0, 4, part, 0)
    bags = delta.shape[0]
    for k, ref in enumerate((own, one, two, three)):
        for t in range(2):
            ref[t * bags : (t + 1) * bags, :] = feature[k, :, t * 128 : (t + 1) * 128].astype(ref.dtype)


def code_kernel(pos, owner, value, lens, out):
    x, c = pos[1], pos[2]
    tables, bag, bags = owner.shape
    j = lax.broadcasted_iota(I32, (8, bags), 0)
    there = 2 * ((x + j) & 3) + ((c + (j >> 2)) & 1)
    for t in range(tables):
        used = [jnp.where(l < lens[t : t + 1, :], owner[t, l : l + 1, :], -1) for l in range(bag)]
        vals = [value[t, l : l + 1, :] for l in range(bag)]
        for k in range(out.shape[0]):
            ids = there + k * 8
            total = jnp.zeros((8, bags), I32)
            for l in range(bag):
                total = total + jnp.where(used[l] == ids, vals[l], 0)
            out[k, 8 * t : 8 * t + 8, :] = total


STEPS = (1, 2, 2, 2, 1)


def prep_kernel(order, pos, codes, *refs):
    ranks, sides, code_all, rank_all = refs[:5], refs[5:10], refs[10], refs[11]
    bags = code_all.shape[1]
    for s in range(8):
        code_all[16 * s : 16 * s + 16, :] = codes[lax.rem(pos[0] + 8 - order[s], 8)]
    earlier = (
        lax.broadcasted_iota(I32, (bags, bags), 0) < lax.broadcasted_iota(I32, (bags, bags), 1)
    )
    earlier = jnp.where(earlier, 1.0, 0.0).astype(BF16)
    present = code_all[...] > 0
    rank = jnp.dot(jnp.where(present, 1.0, 0.0).astype(BF16), earlier, preferred_element_type=F32)
    rank_all[...] = jnp.where(present, rank, 255.0)
    first = 0
    for step, count in enumerate(STEPS):

        def unit(i, carry):
            at = pl.ds(pl.multiple_of((first + i) * 8, 8), 8)
            code = code_all[at, :]
            ranks[step][i] = rank_all[at, :]
            row = lax.shift_right_logical(code, 11)
            fields = [
                lax.shift_right_logical(row, 2).astype(F32),
                (code & 2047).astype(F32) * (1.0 / 512.0),
                (row & 3).astype(F32),
                jnp.zeros((128 - 24, bags), F32),
            ]
            sides[step][i] = jnp.concatenate(fields, axis=0).T.astype(BF16)
            return carry

        lax.fori_loop(0, 2 * count, unit, 0)
        first += 2 * count


def pick_kernel(count, ranks, sides, *refs):
    blocks, refs = refs[:2], refs[2:]
    outs, bag_all, picks, rhs = refs[:12], refs[12], refs[13], refs[14]
    bags = bag_all.shape[2]
    if count == 1:
        for t in range(2):
            bag_all[0, t] = blocks[t][...]
    else:
        for s in range(2):
            for t in range(2):
                bag_all[s, t] = blocks[s][t * bags : (t + 1) * bags, :]
    place = lax.broadcasted_iota(I32, (MOST, bags), 0).astype(F32).astype(BF16)

    def source(s, carry):
        for t in range(2):
            rhs[t, :, :128] = bag_all[s, t]
            rhs[t, :, 128:] = sides[2 * s + t]
            rank = ranks[2 * s + t].astype(BF16)
            for o in range(8):
                line = jnp.broadcast_to(rank[o : o + 1, :], (MOST, bags))
                picks[t, o * MOST : (o + 1) * MOST, :] = jnp.where(
                    line == place, jnp.ones((), BF16), jnp.zeros((), BF16)
                )
        for t in range(2):
            for o in range(0, 8, 2):
                got2 = jnp.dot(
                    picks[t, o * MOST : (o + 2) * MOST, :], rhs[t], preferred_element_type=F32
                )
                for i in range(2):
                    q = o + i
                    got = got2[i * MOST : (i + 1) * MOST]
                    rows, low, meta = outs[3 * (2 * t + q // 4) : 3 * (2 * t + q // 4) + 3]
                    k = q % 4
                    rows[s, k] = got[:, :128].astype(BF16)
                    low[s, k] = jnp.broadcast_to(
                        got[:, 128 + 16 + q : 128 + 17 + q], (MOST, 128)
                    ).astype(BF16)
                    side = got[:, 128:].T
                    meta[s, k : k + 1, :] = side[q : q + 1]
                    meta[s, 4 + k : 5 + k, :] = side[8 + q : 9 + q]
        return carry

    lax.fori_loop(0, count, source, 0)


def spread_one(k, steps, onto, both):
    ids = lax.broadcasted_iota(I32, (256, MOST), 0).astype(F32).astype(BF16)
    s = 0
    for rows, low, meta in steps:
        for i in range(rows.shape[0]):
            at = slice(s * MOST, (s + 1) * MOST)
            high = jnp.broadcast_to(meta[i, pl.ds(k, 1), :].astype(BF16), (256, MOST))
            wt = jnp.broadcast_to(meta[i, pl.ds(k + 4, 1), :].astype(BF16), (256, MOST))
            onto[:, at] = jnp.where(high == ids, wt, jnp.zeros((), BF16))
            vec, bits = rows[i, k], low[i, k]
            for l in range(4):
                both[at, l * 128 : (l + 1) * 128] = jnp.where(
                    bits == jnp.full((), l, BF16), vec, jnp.zeros((), BF16)
                )
            s += 1
    return jnp.dot(onto[...], both[...], preferred_element_type=F32)


def send_kernel(*refs):
    steps = [refs[3 * i : 3 * i + 3] for i in range(5)]
    out, onto, both = refs[15:]

    def one(k, carry):
        out[k] = spread_one(k, steps, onto, both).astype(BF16)
        return carry

    lax.fori_loop(0, 4, one, 0)


def keep_kernel(other, *refs):
    steps = [refs[3 * i : 3 * i + 3] for i in range(5)]
    outs, onto, both, total = refs[15:19], refs[19], refs[20], refs[21]

    def one(k, carry):
        total[k] = spread_one(k, steps, onto, both) + other[k].astype(F32)
        return carry

    lax.fori_loop(0, 4, one, 0)
    for k in range(4):
        outs[k][...] = total[k].astype(outs[k].dtype)


def grad_kernel(pos, pooled, delta, keep, send, half):
    x, c = pos[1], pos[2]

    def piece(i, carry):
        at = pl.ds(pl.multiple_of(i * 512, 512), 512)
        half[...] = lax.dot_general(
            pooled[:, at], delta[...], (((0,), (0,)), ((), ())), preferred_element_type=F32
        )
        for j in range(4):
            kz = i * 4 + j
            for k in range(4):
                row = j * 128 + lax.rem(x + k, 4) * 32
                keep[k, kz] = half[pl.ds(pl.multiple_of(row + c * 16, 16), 16), :]
                send[k, kz] = half[pl.ds(pl.multiple_of(row + (1 - c) * 16, 16), 16), :]
        return carry

    lax.fori_loop(0, 2, piece, 0)


def update_kernel(pos, slots_s, goal_s, slot_map, weight, accum, *refs):
    parts, refs = refs[:8], refs[8:]
    new_weight, new_accum = refs[:2]
    held, refs = refs[2:6], refs[6:]
    rhs, acc_wide, hold, hold_acc = refs
    for t in range(2):
        own = parts[4 * t][...]
        for k in range(1, 4):
            own = own + parts[4 * t + k][...].astype(F32)
        high = own.astype(BF16)
        low = (own - high.astype(F32)).astype(BF16)
        for l in range(4):
            at = (4 * t + l) * 256
            rhs[at : at + 256, :128] = high[:, l * 128 : (l + 1) * 128]
            rhs[at : at + 256, 128:] = low[:, l * 128 : (l + 1) * 128]
    hold[...] = jnp.zeros_like(hold)
    hold_acc[...] = jnp.zeros_like(hold_acc)
    eye = lax.broadcasted_iota(I32, (128, 128), 0) == lax.broadcasted_iota(I32, (128, 128), 1)
    step = 256
    ids = lax.broadcasted_iota(I32, (step, 2048), 0).astype(F32).astype(BF16)
    slot_row = slot_map[...]

    def chunk(i, carry):
        at = pl.multiple_of(i * step, step)
        near = slot_row - at
        near = jnp.where((near >= 0) & (near < step), near, 2 * step).astype(F32).astype(BF16)
        pick = jnp.where(
            jnp.broadcast_to(near, (step, 2048)) == ids, jnp.ones((), BF16), jnp.zeros((), BF16)
        )
        both = jnp.dot(pick, rhs[...], preferred_element_type=F32)
        grad = both[:, :128] + both[:, 128:]
        for j in range(step // 128):
            g = grad[j * 128 : (j + 1) * 128]
            b = i * (step // 128) + j
            kept = jnp.sum(jnp.where(eye, accum[pl.ds(b, 1), :], 0.0), axis=1, keepdims=True)
            acc = kept + jnp.sum(g * g, axis=1, keepdims=True) * (1.0 / 128.0)
            wide = jnp.broadcast_to(acc, (128, 128))
            here = pl.ds(pl.multiple_of(at + j * 128, 128), 128)
            acc_wide[here, :] = wide
            new_accum[pl.ds(b, 1), :] = jnp.sum(jnp.where(eye, wide, 0.0), axis=0, keepdims=True)
            new_weight[here, :] = weight[here, :] - LEARN_RATE * g / (jnp.sqrt(acc) + EPSILON)
        return carry

    lax.fori_loop(0, 2048 // step, chunk, 0)

    def leave(i, carry):
        for j in range(8):
            slot, goal = slots_s[8 * i + j], goal_s[8 * i + j]
            hold[pl.ds(goal, 1), :] = new_weight[pl.ds(slot, 1), :]
            hold_acc[pl.ds(goal, 1), :] = acc_wide[pl.ds(slot, 1), :]
        return carry

    lax.fori_loop(0, slots_s.shape[0] // 8, leave, 0)
    for k in range(4):
        held[k][:128, :] = hold[k * 128 : (k + 1) * 128, :]
        line = jnp.sum(jnp.where(eye, hold_acc[k * 128 : (k + 1) * 128, :], 0.0), axis=0, keepdims=True)
        held[k][128:, :] = jnp.broadcast_to(line, (HELD - 128, 128))


def arrive_kernel(pos, b0, b1, b2, b3, rows, accum):
    h = pos[3]
    for k, ref in enumerate((b0, b1, b2, b3)):
        at = lax.rem(h + 4 - k, 4)
        rows[at] = ref[:128, :]
        accum[pl.ds(at, 1), :] = ref[128:129, :]


def together(*groups):
    flat = [a for g in groups for a in g]
    flat = lax.optimization_barrier(flat)
    out = []
    for g in groups:
        out.append(flat[: len(g)])
        flat = flat[len(g) :]
    return out


def on_device(
    pooled,
    w_up,
    grad_out,
    owners,
    rows,
    lookup_weight,
    lens,
    slot_map,
    cache_weight,
    cache_accum,
    evict_slots,
    evict_dest,
    evict_count,
):
    shape = jax.ShapeDtypeStruct
    bags = pooled.shape[0]
    z, x, c, h = (lax.axis_index(a) for a in (Z, X, C, H))
    pos = jnp.stack([z, x, c, h]).astype(I32)

    delta, *parts = call(
        top_kernel,
        [SMEM, VMEM, VMEM, VMEM],
        [shape((bags, 1024), BF16), shape((2 * bags, 128), F32)] + [shape((2 * bags, 128), BF16)] * 3,
        [pltpu.VMEM((4, bags, 256), F32)],
        2 << 30,
        6 << 20,
        "top",
    )(pos, pooled, w_up, grad_out)
    got = [shifted(parts[k], H, k) for k in (1, 2, 3)]

    (delta,), (owners, rows, lookup_weight, lens) = together(
        (delta,), (owners, rows, lookup_weight, lens)
    )
    value = rows * 2048 + (lookup_weight.astype(F32) * 512.0).astype(I32)
    (codes,) = call(
        code_kernel, [SMEM, VMEM, VMEM, VMEM], [shape((8, 16, bags), I32)], [], 1 << 22, 1 << 20, "codes"
    )(pos, jnp.swapaxes(owners, 1, 2), jnp.swapaxes(value, 1, 2), lens)
    codes = lax.all_to_all(codes, Z, split_axis=0, concat_axis=0, tiled=True)

    got, (codes,) = together(got, (codes,))
    own = parts[0] + got[0].astype(F32) + got[1].astype(F32) + got[2].astype(F32)
    own = own.astype(BF16)
    order = (0, 1, 7, 2, 6, 3, 5, 4)
    units = [2 * n for n in STEPS]
    prep = call(
        functools.partial(prep_kernel, order),
        [SMEM, VMEM],
        [shape((n, 8, bags), F32) for n in units] + [shape((n, bags, 128), BF16) for n in units],
        [pltpu.VMEM((128, bags), I32), pltpu.VMEM((128, bags), F32)],
        1 << 26,
        3 << 20,
        "prep",
    )(pos, codes)

    def pick(step, blocks):
        count = STEPS[step]
        outs = [
            shape((count, 4, MOST, 128), BF16),
            shape((count, 4, MOST, 128), BF16),
            shape((count, 8, 128), F32),
        ] * 4
        return call(
            functools.partial(pick_kernel, count),
            [VMEM] * 4,
            outs,
            [
                pltpu.VMEM((count, 2, bags, 128), BF16),
                pltpu.VMEM((2, 8 * MOST, bags), BF16),
                pltpu.VMEM((2, bags, 256), BF16),
            ],
            1 << 30,
            4 << 20,
            f"pick{step}",
        )(prep[step], prep[5 + step], *blocks)

    up, down = shifted(own, Z, 1), shifted(own, Z, -1)
    (delta,), (own,) = together((delta,), (own,))
    grad, there = call(
        grad_kernel,
        [SMEM, VMEM, VMEM],
        [shape((4, 8, 16, 1024), F32)] * 2,
        [pltpu.VMEM((512, 1024), F32)],
        1 << 30,
        6 << 20,
        "grad",
    )(pos, pooled, delta)
    near = (up, down)
    (up, down), (grad, there) = together((up, down), (grad, there))
    there = shifted(there, C, 1)
    up, down = shifted(up, Z, 1), shifted(down, Z, -1)
    picked = [pick(0, (own[:bags], own[bags:]))]
    mid = (up, down)
    (up, down), near, *picked = together((up, down), near, *picked)
    up, down = shifted(up, Z, 1), shifted(down, Z, -1)
    picked.append(pick(1, near))
    grad_x = grad + there
    total, blocks = grad_x[0], [grad_x[k].astype(BF16) for k in (1, 2, 3)]
    far = (up, down)
    (up, down), mid, (total,), blocks, picked[1] = together((up, down), mid, (total,), blocks, picked[1])
    last = (shifted(up[:bags], Z, 1), shifted(down[bags:], Z, -1))
    got_x = [shifted(blocks[k - 1], X, k) for k in (1, 2, 3)]
    picked.append(pick(2, mid))
    picked.append(pick(3, far))
    picked.append(pick(4, last))

    work = [pltpu.VMEM((256, 8 * MOST), BF16), pltpu.VMEM((8 * MOST, 512), BF16)]
    half = lambda t, side: [a for p in picked for a in p[3 * (2 * t + side) : 3 * (2 * t + side) + 3]]
    others = []
    for t in range(2):
        (out,) = call(
            send_kernel, [VMEM] * 15, [shape((4, 256, 512), BF16)], work, 4 << 30, 5 << 20, f"send{t}"
        )(*half(t, 1))
        others.append(shifted(out, C, 1))
    arrived = []
    for t in range(2):
        outs = call(
            keep_kernel,
            [VMEM] * 16,
            [shape((256, 512), F32)] + [shape((256, 512), BF16)] * 3,
            work + [pltpu.VMEM((4, 256, 512), F32)],
            4 << 30,
            5 << 20,
            f"keep{t}",
        )(others[t], *half(t, 0))
        arrived += [outs[0]] + [shifted(outs[k], X, k) for k in (1, 2, 3)]

    for block in got_x:
        total = total + block.astype(F32)
    keep_now, (total,) = together((arrived[4],), (total,))
    arrived[4] = keep_now[0]
    blocks = lax.all_to_all(total.astype(BF16), Z, split_axis=0, concat_axis=0, tiled=True)
    blocks = jnp.where(jnp.arange(8, dtype=I32)[:, None, None] == z, 0.0, blocks.astype(F32))
    grad_up = lax.dynamic_index_in_dim(total, z, 0, keepdims=False) + blocks.sum(axis=0)
    arrived, (grad_up,) = together(arrived, (grad_up,))

    list_len = evict_slots.shape[-1]
    departure = evict_dest[0, 0]
    list_ids = jnp.arange(list_len, dtype=I32)
    live = list_ids < evict_count[0, 0]
    picks = ((departure[:, None] == jnp.arange(4, dtype=I32)) & live[:, None]).astype(BF16)
    before = (list_ids[:, None] > list_ids[None, :]).astype(BF16)
    counted = jnp.dot(before, picks, preferred_element_type=F32)
    placed = jnp.sum(counted * picks.astype(F32), axis=-1).astype(I32)
    goal = jnp.where(live, lax.rem(departure + 4 - h, 4) * 128 + placed, 512)
    slot_rows = jnp.swapaxes(slot_map.reshape(2, 256, 4), 1, 2).reshape(1, 2048)
    new_weight, new_accum, *held = call(
        update_kernel,
        [SMEM] * 3 + [VMEM] * 11,
        [shape((2048, 128), F32), shape((16, 128), F32)] + [shape((HELD, 128), F32)] * 4,
        [
            pltpu.VMEM((2048, 256), BF16),
            pltpu.VMEM((2048, 128), F32),
            pltpu.VMEM((520, 128), F32),
            pltpu.VMEM((520, 128), F32),
        ],
        2 << 30,
        4 << 20,
        "update",
    )(
        pos,
        evict_slots.reshape(-1),
        goal,
        slot_rows,
        cache_weight[0, 0],
        cache_accum.reshape(16, 128),
        *arrived,
    )
    held = [held[0]] + [shifted(held[k], H, k) for k in (1, 2, 3)]
    held_rows, held_accum = call(
        arrive_kernel,
        [SMEM] + [VMEM] * 4,
        [shape((4, 128, 128), F32), shape((4, 128), F32)],
        [],
        1 << 10,
        1 << 19,
        "arrive",
    )(pos, *held)
    return (
        grad_up,
        new_weight[None, None],
        new_accum.reshape(1, 1, 2048),
        held_rows[None, None],
        held_accum[None, None],
    )


def solution(mesh):
    torus = Mesh(mesh.devices.reshape(8, 4, 2, mesh.shape["hst"]), (Z, X, C, H))
    in_specs = (
        P(TBL, None),
        P(None, "hst"),
        P(TBL, "hst"),
        P("hst", TBL, None),
        P("hst", TBL, None),
        P("hst", TBL, None),
        P("hst", TBL),
        P(TBL, "hst", None),
        P(TBL, "hst", None, None),
        P(TBL, "hst", None),
        P(TBL, "hst", None),
        P(TBL, "hst", None),
        P(TBL, "hst"),
    )
    out_specs = (
        P(TBL, "hst"),
        P(TBL, "hst", None, None),
        P(TBL, "hst", None),
        P(TBL, "hst", None, None, None),
        P(TBL, "hst", None, None),
    )
    return jax.shard_map(
        on_device, mesh=torus, in_specs=in_specs, out_specs=out_specs, check_vma=False
    )
```

profile of v0, /device:TPU:8, one launch (start us, length us, event | category | flops | bytes accessed | tf_op | source)
XLA Modules:
  0.0 168.2 jit_solution(1909612642167299390)
XLA Ops:
  0.7 1.2 copy-done.2
  1.9 1.2 copy-done.3
  3.2 5.6 %top.1 = (bf16[512,1024]{1,0:T(8,128)(2,1)S(1)}, f32[1024,128]{1,0:T(8,128)S(1)}, bf16[1024,128]{1,0:T(8,128)(2,1)S(1)}, bf16[1024,128]{1,0:T(8,128)(2,1)S(1)}, bf16[1024,128]{1,0:T(8,128)(2,1)S(1)}) custom-call(s32[4]{0:T(128)S(1)} %pad_add_fusion.pos, bf16[512,1024]{1,0:T(8,128)(2,1)S(1)} %copy-done.3, bf16[1024,1024]{1,0:T(8,128)(2,1)} %w_up.1, ...), custom_call_target="tpu_custom_call" | custom-call | flops 2147483648 | bytes 6291456 | tf_op jit(solution)/shard_map/top/pallas_call | solution.py:328
  9.8 1.5 codes.1
  11.3 8.5 %all-to-all-start = ((s32[8,16,512]{2,1,0:T(8,128)}), s32[8,16,512]{2,1,0:T(8,128)S(1)}, u32[]{:S(2)}, u32[]{:S(2)}) async-start(s32[8,16,512]{2,1,0:T(8,128)} %codes.1), calls=%async_computation | async-start | bytes 524288 | tf_op jit(solution)/shard_map/all_to_all | solution.py:346
  19.8 1.6 collective-permute-start
  22.3 2.4 %collective-permute-start.2 = (bf16[1024,128]{1,0:T(8,128)(2,1)S(1)}, bf16[1024,128]{1,0:T(8,128)(2,1)S(1)}, u32[]{:S(2)}, u32[]{:S(2)}) collective-permute-start(bf16[1024,128]{1,0:T(8,128)(2,1)S(1)} %get-tuple-element.163), channel_id=1, source_target_pairs={{0,3},{1,0},{2,1},{3,2},{4,7},{5,4},{6,5},{7,6},{8,11},{9,8},{10,9... | collective-permute-start | bytes 786440 | tf_op jit(solution)/shard_map/ppermute | solution.py:27
  24.7 4.3 %collective-permute-done = bf16[1024,128]{1,0:T(8,128)(2,1)S(1)} collective-permute-done((bf16[1024,128]{1,0:T(8,128)(2,1)S(1)}, bf16[1024,128]{1,0:T(8,128)(2,1)S(1)}, u32[]{:S(2)}, u32[]{:S(2)}) %collective-permute-start) | collective-permute-done | bytes 262176 | tf_op jit(solution)/shard_map/ppermute | solution.py:27
  29.0 3.1 %collective-permute-done.1 = bf16[1024,128]{1,0:T(8,128)(2,1)S(1)} collective-permute-done((bf16[1024,128]{1,0:T(8,128)(2,1)S(1)}, bf16[1024,128]{1,0:T(8,128)(2,1)S(1)}, u32[]{:S(2)}, u32[]{:S(2)}) %collective-permute-start.1) | collective-permute-done | bytes 262176 | tf_op jit(solution)/shard_map/ppermute | solution.py:27
  32.1 3.2 %collective-permute-done.2 = bf16[1024,128]{1,0:T(8,128)(2,1)S(1)} collective-permute-done((bf16[1024,128]{1,0:T(8,128)(2,1)S(1)}, bf16[1024,128]{1,0:T(8,128)(2,1)S(1)}, u32[]{:S(2)}, u32[]{:S(2)}) %collective-permute-start.2) | collective-permute-done | bytes 262176 | tf_op jit(solution)/shard_map/ppermute | solution.py:27
  35.4 1.7 %collective-permute-start.3 = (bf16[1024,128]{1,0:T(8,128)(2,1)S(1)}, bf16[1024,128]{1,0:T(8,128)(2,1)S(1)}, u32[]{:S(2)}, u32[]{:S(2)}) collective-permute-start(bf16[1024,128]{1,0:T(8,128)(2,1)S(1)} %add_convert_fusion), channel_id=1, source_target_pairs={{0,32},{32,64},{64,96},{96,128},{128,160},{160,192},{192,224},{224... | collective-permute-start | bytes 786440 | tf_op jit(solution)/shard_map/ppermute | solution.py:27
  37.2 1.6 collective-permute-start.4
  38.8 1.2 copy-done.10
  40.0 3.6 %grad.1 = (f32[4,8,16,1024]{3,2,1,0:T(8,128)S(1)}, f32[4,8,16,1024]{3,2,1,0:T(8,128)}) custom-call(s32[4]{0:T(128)S(1)} %pad_add_fusion.pos, bf16[512,1024]{1,0:T(8,128)(2,1)S(1)} %copy-done.4, bf16[512,1024]{1,0:T(8,128)(2,1)S(1)} %copy-done.10), custom_call_target="tpu_custom_call" | custom-call | flops 1073741824 | bytes 6291456 | tf_op jit(solution)/shard_map/grad/pallas_call | solution.py:386
  44.3 2.5 %prep.1 = (f32[2,8,512]{2,1,0:T(8,128)S(1)}, f32[4,8,512]{2,1,0:T(8,128)S(1)}, f32[4,8,512]{2,1,0:T(8,128)S(1)}, f32[4,8,512]{2,1,0:T(8,128)S(1)}, f32[2,8,512]{...) custom-call(s32[4]{0:T(128)S(1)} %pad_add_fusion.pos, ...), custom_call_target="tpu_custom_call" | custom-call | flops 67108864 | bytes 3145728 | tf_op jit(solution)/shard_map/prep/pallas_call | solution.py:353
  46.8 1.5 collective-permute-start.5
  48.3 1.8 %collective-permute-start.6 = (bf16[1024,128]{1,0:T(8,128)(2,1)S(1)}, bf16[1024,128]{1,0:T(8,128)(2,1)S(1)}, u32[]{:S(2)}, u32[]{:S(2)}) collective-permute-start(bf16[1024,128]{1,0:T(8,128)(2,1)S(1)} %collective-permute-done.4.refs_1_), channel_id=1, source_target_pairs={{0,224},{32,0},{64,32},{96,64},{128,96},{160,128},{192,160},{224,1... | collective-permute-start | bytes 786440 | tf_op jit(solution)/shard_map/ppermute | solution.py:27
  51.7 5.1 %collective-permute-done.5.refs_0_ = bf16[1024,128]{1,0:T(8,128)(2,1)S(1)} collective-permute-done((bf16[1024,128]{1,0:T(8,128)(2,1)S(1)}, bf16[1024,128]{1,0:T(8,128)(2,1)S(1)}, u32[]{:S(2)}, u32[]{:S(2)}) %collective-permute-start.5) | collective-permute-done | bytes 262176 | tf_op jit(solution)/shard_map/ppermute | solution.py:27
  57.4 3.0 %collective-permute-start.7 = (bf16[1024,128]{1,0:T(8,128)(2,1)S(1)}, bf16[1024,128]{1,0:T(8,128)(2,1)S(1)}, u32[]{:S(2)}, u32[]{:S(2)}) collective-permute-start(bf16[1024,128]{1,0:T(8,128)(2,1)S(1)} %collective-permute-done.5.refs_0_), channel_id=1, source_target_pairs={{0,32},{32,64},{64,96},{96,128},{128,160},{160,192},{192,224},{224... | collective-permute-start | bytes 786440 | tf_op jit(solution)/shard_map/ppermute | solution.py:27
  60.6 1.8 %pick1.1 = (bf16[2,4,128,128]{3,2,1,0:T(8,128)(2,1)S(1)}, bf16[2,4,128,128]{3,2,1,0:T(8,128)(2,1)S(1)}, f32[2,8,128]{2,1,0:T(8,128)S(1)}, bf16[2,4,128,128]{3,2,...) custom-call(f32[4,8,512]{2,1,0:T(8,128)S(1)} %get-tuple-element.201., ...), custom_call_target="tpu_custom_call" | custom-call | flops 1073741824 | bytes 4194304 | tf_op jit(solution)/shard_map/pick1/pallas_call | solution.py:370
  63.4 3.1 %collective-permute-done.7.refs_0_ = bf16[1024,128]{1,0:T(8,128)(2,1)S(1)} collective-permute-done((bf16[1024,128]{1,0:T(8,128)(2,1)S(1)}, bf16[1024,128]{1,0:T(8,128)(2,1)S(1)}, u32[]{:S(2)}, u32[]{:S(2)}) %collective-permute-start.7) | collective-permute-done | bytes 262176 | tf_op jit(solution)/shard_map/ppermute | solution.py:27
  66.5 1.5 collective-permute-done.8.refs_1_
  68.0 1.7 %collective-permute-start.10 = (bf16[512,128]{1,0:T(8,128)(2,1)S(1)}, bf16[512,128]{1,0:T(8,128)(2,1)S(1)}, u32[]{:S(2)}, u32[]{:S(2)}) collective-permute-start(bf16[512,128]{1,0:T(8,128)(2,1)S(1)} %slice.33), channel_id=1, source_target_pairs={{0,32},{32,64},{64,96},{96,128},{128,160},{160,192},{192,224},{224... | collective-permute-start | bytes 393224 | tf_op jit(solution)/shard_map/ppermute | solution.py:27
  69.7 1.9 %collective-permute-start.11 = (bf16[512,128]{1,0:T(8,128)(2,1)S(1)}, bf16[512,128]{1,0:T(8,128)(2,1)S(1)}, u32[]{:S(2)}, u32[]{:S(2)}) collective-permute-start(bf16[512,128]{1,0:T(8,128)(2,1)S(1)} %slice.34), channel_id=1, source_target_pairs={{0,224},{32,0},{64,32},{96,64},{128,96},{160,128},{192,160},{224,1... | collective-permute-start | bytes 393224 | tf_op jit(solution)/shard_map/ppermute | solution.py:27
  71.6 1.8 %pick3.1 = (bf16[2,4,128,128]{3,2,1,0:T(8,128)(2,1)S(1)}, bf16[2,4,128,128]{3,2,1,0:T(8,128)(2,1)S(1)}, f32[2,8,128]{2,1,0:T(8,128)S(1)}, bf16[2,4,128,128]{3,2,...) custom-call(f32[4,8,512]{2,1,0:T(8,128)S(1)} %get-tuple-element.227., ...), custom_call_target="tpu_custom_call" | custom-call | flops 1073741824 | bytes 4194304 | tf_op jit(solution)/shard_map/pick3/pallas_call | solution.py:370
  73.4 1.8 %pick2.1 = (bf16[2,4,128,128]{3,2,1,0:T(8,128)(2,1)S(1)}, bf16[2,4,128,128]{3,2,1,0:T(8,128)(2,1)S(1)}, f32[2,8,128]{2,1,0:T(8,128)S(1)}, bf16[2,4,128,128]{3,2,...) custom-call(f32[4,8,512]{2,1,0:T(8,128)S(1)} %get-tuple-element.220., ...), custom_call_target="tpu_custom_call" | custom-call | flops 1073741824 | bytes 4194304 | tf_op jit(solution)/shard_map/pick2/pallas_call | solution.py:370
  76.1 2.5 %send1.1 = bf16[4,256,512]{2,1,0:T(8,128)(2,1)S(1)} custom-call(bf16[1,4,128,128]{3,2,1,0:T(8,128)(2,1)S(1)} %get-tuple-element.258.refs_0_, bf16[1,4,128,128]{3,2,1,0:T(8,128)(2,1)S(1)} %get-tuple-element.259.refs_1_, f32[1,8,128]{2,1,0:T(8,128)S(1)} %get-tuple-element.260.refs_2_, bf16[2,4,128,128]{3,2,1,0:T(8,128)(2,1)S(1)} %get-tuple-element.261.refs_3_, ...), custom_call_target="tpu_custom_call" | custom-call | flops 4294967296 | bytes 5242880 | tf_op jit(solution)/shard_map/send1/pallas_call | solution.py:418
  78.8 2.5 %send0.1 = bf16[4,256,512]{2,1,0:T(8,128)(2,1)S(1)} custom-call(bf16[1,4,128,128]{3,2,1,0:T(8,128)(2,1)S(1)} %get-tuple-element.194.refs_0_, bf16[1,4,128,128]{3,2,1,0:T(8,128)(2,1)S(1)} %get-tuple-element.195.refs_1_, f32[1,8,128]{2,1,0:T(8,128)S(1)} %get-tuple-element.196.refs_2_, bf16[2,4,128,128]{3,2,1,0:T(8,128)(2,1)S(1)} %get-tuple-element.217.refs_3_, ...), custom_call_target="tpu_custom_call" | custom-call | flops 4294967296 | bytes 5242880 | tf_op jit(solution)/shard_map/send0/pallas_call | solution.py:418
  81.9 2.8 %collective-permute-start.19 = (bf16[8,16,1024]{2,1,0:T(8,128)(2,1)S(1)}, bf16[8,16,1024]{2,1,0:T(8,128)(2,1)S(1)}, u32[]{:S(2)}, u32[]{:S(2)}) collective-permute-start(bf16[8,16,1024]{2,1,0:T(8,128)(2,1)S(1)} %get-tuple-element.292), channel_id=1, source_target_pairs={{0,24},{8,0},{16,8},{24,16},{1,25},{9,1},{17,9},{25,17},{2,26},{10... | collective-permute-start | bytes 786440 | tf_op jit(solution)/shard_map/ppermute | solution.py:27
  87.2 8.9 %collective-permute-done.19 = bf16[8,16,1024]{2,1,0:T(8,128)(2,1)S(1)} collective-permute-done((bf16[8,16,1024]{2,1,0:T(8,128)(2,1)S(1)}, bf16[8,16,1024]{2,1,0:T(8,128)(2,1)S(1)}, u32[]{:S(2)}, u32[]{:S(2)}) %collective-permute-start.19) | collective-permute-done | bytes 262176 | tf_op jit(solution)/shard_map/ppermute | solution.py:27
  96.2 3.7 %collective-permute-done.17 = bf16[8,16,1024]{2,1,0:T(8,128)(2,1)S(1)} collective-permute-done((bf16[8,16,1024]{2,1,0:T(8,128)(2,1)S(1)}, bf16[8,16,1024]{2,1,0:T(8,128)(2,1)S(1)}, u32[]{:S(2)}, u32[]{:S(2)}) %collective-permute-start.17) | collective-permute-done | bytes 262176 | tf_op jit(solution)/shard_map/ppermute | solution.py:27
  100.0 2.6 %keep1.1 = (f32[256,512]{1,0:T(8,128)S(1)}, bf16[256,512]{1,0:T(8,128)(2,1)S(1)}, bf16[256,512]{1,0:T(8,128)(2,1)S(1)}, bf16[256,512]{1,0:T(8,128)(2,1)S(1)}) custom-call(bf16[4,256,512]{2,1,0:T(8,128)(2,1)S(1)} %collective-permute-done.16.other, bf16[1,4,128,128]{3,2,1,0:T(8,128)(2,1)S(1)} %get-tuple-element.273.refs_0_, ...), custom_call_target="tpu_custom_call" | custom-call | flops 4294967296 | bytes 5242880 | tf_op jit(solution)/shard_map/keep1/pallas_call | solution.py:424
  104.2 4.6 %all-to-all-start.1 = ((bf16[8,16,1024]{2,1,0:T(8,128)(2,1)}), bf16[8,16,1024]{2,1,0:T(8,128)(2,1)}, u32[]{:S(2)}, u32[]{:S(2)}) async-start(bf16[8,16,1024]{2,1,0:T(8,128)(2,1)} %convert_element_type.67), calls=%async_computation.1 | async-start | bytes 524288 | tf_op jit(solution)/shard_map/all_to_all | solution.py:439
  116.4 3.3 %keep0.1 = (f32[256,512]{1,0:T(8,128)S(1)}, bf16[256,512]{1,0:T(8,128)(2,1)}, bf16[256,512]{1,0:T(8,128)(2,1)S(1)}, bf16[256,512]{1,0:T(8,128)(2,1)S(1)}) custom-call(bf16[4,256,512]{2,1,0:T(8,128)(2,1)S(1)} %collective-permute-done.12.other, bf16[1,4,128,128]{3,2,1,0:T(8,128)(2,1)S(1)} %get-tuple-element.239.refs_0_, ...), custom_call_target="tpu_custom_call" | custom-call | flops 4294967296 | bytes 5242880 | tf_op jit(solution)/shard_map/keep0/pallas_call | solution.py:424
  122.8 2.1 %collective-permute-start.14 = (bf16[256,512]{1,0:T(8,128)(2,1)}, bf16[256,512]{1,0:T(8,128)(2,1)S(1)}, u32[]{:S(2)}, u32[]{:S(2)}) collective-permute-start(bf16[256,512]{1,0:T(8,128)(2,1)} %copy-done.6), channel_id=1, source_target_pairs={{0,16},{8,24},{16,0},{24,8},{1,17},{9,25},{17,1},{25,9},{2,18},{10... | collective-permute-start | bytes 786440 | tf_op jit(solution)/shard_map/ppermute | solution.py:27
  125.0 1.4 collective-permute-start.15
  127.0 2.1 %collective-permute-start.21 = (bf16[256,512]{1,0:T(8,128)(2,1)S(1)}, bf16[256,512]{1,0:T(8,128)(2,1)}, u32[]{:S(2)}, u32[]{:S(2)}) collective-permute-start(bf16[256,512]{1,0:T(8,128)(2,1)S(1)} %get-tuple-element.295), channel_id=1, source_target_pairs={{0,16},{8,24},{16,0},{24,8},{1,17},{9,25},{17,1},{25,9},{2,18},{10... | collective-permute-start | bytes 786440 | tf_op jit(solution)/shard_map/ppermute | solution.py:27
  129.1 8.4 %collective-permute-done.13.refs_1_ = bf16[256,512]{1,0:T(8,128)(2,1)S(1)} collective-permute-done((bf16[256,512]{1,0:T(8,128)(2,1)}, bf16[256,512]{1,0:T(8,128)(2,1)S(1)}, u32[]{:S(2)}, u32[]{:S(2)}) %collective-permute-start.13) | collective-permute-done | bytes 262176 | tf_op jit(solution)/shard_map/ppermute | solution.py:27
  137.5 1.1 select_reduce_fusion
  138.6 1.5 bitcast_add_fusion
  140.1 7.4 %collective-permute-done.20.refs_5_ = bf16[256,512]{1,0:T(8,128)(2,1)S(1)} collective-permute-done((bf16[256,512]{1,0:T(8,128)(2,1)S(1)}, bf16[256,512]{1,0:T(8,128)(2,1)S(1)}, u32[]{:S(2)}, u32[]{:S(2)}) %collective-permute-start.20) | collective-permute-done | bytes 262176 | tf_op jit(solution)/shard_map/ppermute | solution.py:27
  147.4 2.5 %collective-permute-done.22.refs_7_ = bf16[256,512]{1,0:T(8,128)(2,1)} collective-permute-done((bf16[256,512]{1,0:T(8,128)(2,1)S(1)}, bf16[256,512]{1,0:T(8,128)(2,1)}, u32[]{:S(2)}, u32[]{:S(2)}) %collective-permute-start.22) | collective-permute-done | bytes 262176 | tf_op jit(solution)/shard_map/ppermute | solution.py:27
  151.0 1.0 copy-done.26
  152.0 7.5 %update.1 = (f32[2048,128]{1,0:T(8,128)}, f32[16,128]{1,0:T(8,128)}, f32[136,128]{1,0:T(8,128)S(1)}, f32[136,128]{1,0:T(8,128)S(1)}, f32[136,128]{1,0:T(8,128)S(1)}, /*index=5*/f32[136,128]{1,0:T(8,128)S(1)}) custom-call(s32[4]{0:T(128)S(1)} %pad_add_fusion.pos, s32[256]{0:T(256)S(1)} %bitcast.32, s32[256]{0:T(256)S(1)} %fusion.9.goal_s, ...), custom_call_target="tpu_custom_call" | custom-call | flops 2147483648 | bytes 4194304 | tf_op jit(solution)/shard_map/update/pallas_call | solution.py:454
  160.3 1.6 collective-permute-start.24
  161.9 2.6 %collective-permute-start.25 = (f32[136,128]{1,0:T(8,128)S(1)}, f32[136,128]{1,0:T(8,128)S(1)}, u32[]{:S(2)}, u32[]{:S(2)}) collective-permute-start(f32[136,128]{1,0:T(8,128)S(1)} %get-tuple-element.312), channel_id=1, source_target_pairs={{0,3},{1,0},{2,1},{3,2},{4,7},{5,4},{6,5},{7,6},{8,11},{9,8},{10,9... | collective-permute-start | bytes 208904 | tf_op jit(solution)/shard_map/ppermute | solution.py:27
  164.5 1.7 %collective-permute-done.24.b2 = f32[136,128]{1,0:T(8,128)S(1)} collective-permute-done((f32[136,128]{1,0:T(8,128)S(1)}, f32[136,128]{1,0:T(8,128)S(1)}, u32[]{:S(2)}, u32[]{:S(2)}) %collective-permute-start.24) | collective-permute-done | bytes 69664 | tf_op jit(solution)/shard_map/ppermute | solution.py:27
  166.9 1.3 arrive.1
  (125 shorter events, 25.4 us)
Async XLA Ops:
  3.2 6.6 %copy-start.36 = (s32[2,512,8]{1,2,0:T(8,128)S(1)}, s32[2,512,8]{1,2,0:T(8,128)}, u32[]{:S(2)}) copy-start(s32[2,512,8]{1,2,0:T(8,128)} %param.17) | copy-start | bytes 98308
  3.2 6.6 %copy-start.37 = (bf16[2,512,8]{1,2,0:T(8,128)(2,1)S(1)}, bf16[2,512,8]{1,2,0:T(8,128)(2,1)}, u32[]{:S(2)}) copy-start(bf16[2,512,8]{1,2,0:T(8,128)(2,1)} %param.18) | copy-start | bytes 49156
  3.2 6.6 %copy-start = (s32[2,512,8]{1,2,0:T(8,128)S(1)}, s32[2,512,8]{1,2,0:T(8,128)}, u32[]{:S(2)}) copy-start(s32[2,512,8]{1,2,0:T(8,128)} %param.16) | copy-start | bytes 98308
  3.2 6.6 %copy-start.1 = (s32[2,512]{1,0:T(2,128)S(1)}, s32[2,512]{1,0:T(2,128)}, u32[]{:S(2)}) copy-start(s32[2,512]{1,0:T(2,128)} %lens) | copy-start | bytes 12292
  9.8 29.0 %copy-start.4 = (bf16[512,1024]{1,0:T(8,128)(2,1)S(1)}, bf16[512,1024]{1,0:T(8,128)(2,1)}, u32[]{:S(2)}) copy-start(bf16[512,1024]{1,0:T(8,128)(2,1)} %pooled.3) | copy-start | bytes 3145732
  11.3 24.0 %all-to-all-start = ((s32[8,16,512]{2,1,0:T(8,128)}), s32[8,16,512]{2,1,0:T(8,128)S(1)}, u32[]{:S(2)}, u32[]{:S(2)}) async-start(s32[8,16,512]{2,1,0:T(8,128)} %codes.1), calls=%async_computation | async-start | bytes 524288 | tf_op jit(solution)/shard_map/all_to_all | solution.py:346
  19.8 9.2 %collective-permute-start = (bf16[1024,128]{1,0:T(8,128)(2,1)S(1)}, bf16[1024,128]{1,0:T(8,128)(2,1)S(1)}, u32[]{:S(2)}, u32[]{:S(2)}) collective-permute-start(bf16[1024,128]{1,0:T(8,128)(2,1)S(1)} %get-tuple-element.161), channel_id=1, source_target_pairs={{0,1},{1,2},{2,3},{3,0},{4,5},{5,6},{6,7},{7,4},{8,9},{9,10},{10,1... | collective-permute-start | bytes 786440 | tf_op jit(solution)/shard_map/ppermute | solution.py:27
  21.4 10.7 %collective-permute-start.1 = (bf16[1024,128]{1,0:T(8,128)(2,1)S(1)}, bf16[1024,128]{1,0:T(8,128)(2,1)S(1)}, u32[]{:S(2)}, u32[]{:S(2)}) collective-permute-start(bf16[1024,128]{1,0:T(8,128)(2,1)S(1)} %get-tuple-element.162), channel_id=1, source_target_pairs={{0,2},{1,3},{2,0},{3,1},{4,6},{5,7},{6,4},{7,5},{8,10},{9,11},{10,... | collective-permute-start | bytes 786440 | tf_op jit(solution)/shard_map/ppermute | solution.py:27
  22.3 13.0 %collective-permute-start.2 = (bf16[1024,128]{1,0:T(8,128)(2,1)S(1)}, bf16[1024,128]{1,0:T(8,128)(2,1)S(1)}, u32[]{:S(2)}, u32[]{:S(2)}) collective-permute-start(bf16[1024,128]{1,0:T(8,128)(2,1)S(1)} %get-tuple-element.163), channel_id=1, source_target_pairs={{0,3},{1,0},{2,1},{3,2},{4,7},{5,4},{6,5},{7,6},{8,11},{9,8},{10,9... | collective-permute-start | bytes 786440 | tf_op jit(solution)/shard_map/ppermute | solution.py:27
  35.4 8.8 %collective-permute-start.3 = (bf16[1024,128]{1,0:T(8,128)(2,1)S(1)}, bf16[1024,128]{1,0:T(8,128)(2,1)S(1)}, u32[]{:S(2)}, u32[]{:S(2)}) collective-permute-start(bf16[1024,128]{1,0:T(8,128)(2,1)S(1)} %add_convert_fusion), channel_id=1, source_target_pairs={{0,32},{32,64},{64,96},{96,128},{128,160},{160,192},{192,224},{224... | collective-permute-start | bytes 786440 | tf_op jit(solution)/shard_map/ppermute | solution.py:27
  37.2 7.1 %collective-permute-start.4 = (bf16[1024,128]{1,0:T(8,128)(2,1)S(1)}, bf16[1024,128]{1,0:T(8,128)(2,1)S(1)}, u32[]{:S(2)}, u32[]{:S(2)}) collective-permute-start(bf16[1024,128]{1,0:T(8,128)(2,1)S(1)} %add_convert_fusion), channel_id=1, source_target_pairs={{0,224},{32,0},{64,32},{96,64},{128,96},{160,128},{192,160},{224,1... | collective-permute-start | bytes 786440 | tf_op jit(solution)/shard_map/ppermute | solution.py:27
  44.3 18.1 %collective-permute-start.9 = (f32[4,8,16,1024]{3,2,1,0:T(8,128)}, f32[4,8,16,1024]{3,2,1,0:T(8,128)S(1)}, u32[]{:S(2)}, u32[]{:S(2)}) collective-permute-start(f32[4,8,16,1024]{3,2,1,0:T(8,128)} %get-tuple-element.200), channel_id=1, source_target_pairs={{0,4},{4,0},{1,5},{5,1},{2,6},{6,2},{3,7},{7,3},{8,12},{12,8},{9,1... | collective-permute-start | bytes 6291464 | tf_op jit(solution)/shard_map/ppermute | solution.py:27
  46.8 10.0 %collective-permute-start.5 = (bf16[1024,128]{1,0:T(8,128)(2,1)S(1)}, bf16[1024,128]{1,0:T(8,128)(2,1)S(1)}, u32[]{:S(2)}, u32[]{:S(2)}) collective-permute-start(bf16[1024,128]{1,0:T(8,128)(2,1)S(1)} %collective-permute-done.3.refs_0_), channel_id=1, source_target_pairs={{0,32},{32,64},{64,96},{96,128},{128,160},{160,192},{192,224},{224... | collective-permute-start | bytes 786440 | tf_op jit(solution)/shard_map/ppermute | solution.py:27
  48.3 9.1 %collective-permute-start.6 = (bf16[1024,128]{1,0:T(8,128)(2,1)S(1)}, bf16[1024,128]{1,0:T(8,128)(2,1)S(1)}, u32[]{:S(2)}, u32[]{:S(2)}) collective-permute-start(bf16[1024,128]{1,0:T(8,128)(2,1)S(1)} %collective-permute-done.4.refs_1_), channel_id=1, source_target_pairs={{0,224},{32,0},{64,32},{96,64},{128,96},{160,128},{192,160},{224,1... | collective-permute-start | bytes 786440 | tf_op jit(solution)/shard_map/ppermute | solution.py:27
  57.4 9.1 %collective-permute-start.7 = (bf16[1024,128]{1,0:T(8,128)(2,1)S(1)}, bf16[1024,128]{1,0:T(8,128)(2,1)S(1)}, u32[]{:S(2)}, u32[]{:S(2)}) collective-permute-start(bf16[1024,128]{1,0:T(8,128)(2,1)S(1)} %collective-permute-done.5.refs_0_), channel_id=1, source_target_pairs={{0,32},{32,64},{64,96},{96,128},{128,160},{160,192},{192,224},{224... | collective-permute-start | bytes 786440 | tf_op jit(solution)/shard_map/ppermute | solution.py:27
  60.4 7.7 %collective-permute-start.8 = (bf16[1024,128]{1,0:T(8,128)(2,1)S(1)}, bf16[1024,128]{1,0:T(8,128)(2,1)S(1)}, u32[]{:S(2)}, u32[]{:S(2)}) collective-permute-start(bf16[1024,128]{1,0:T(8,128)(2,1)S(1)} %collective-permute-done.6.refs_1_), channel_id=1, source_target_pairs={{0,224},{32,0},{64,32},{96,64},{128,96},{160,128},{192,160},{224,1... | collective-permute-start | bytes 786440 | tf_op jit(solution)/shard_map/ppermute | solution.py:27
  68.0 7.2 %collective-permute-start.10 = (bf16[512,128]{1,0:T(8,128)(2,1)S(1)}, bf16[512,128]{1,0:T(8,128)(2,1)S(1)}, u32[]{:S(2)}, u32[]{:S(2)}) collective-permute-start(bf16[512,128]{1,0:T(8,128)(2,1)S(1)} %slice.33), channel_id=1, source_target_pairs={{0,32},{32,64},{64,96},{96,128},{128,160},{160,192},{192,224},{224... | collective-permute-start | bytes 393224 | tf_op jit(solution)/shard_map/ppermute | solution.py:27
  69.7 5.5 %collective-permute-start.11 = (bf16[512,128]{1,0:T(8,128)(2,1)S(1)}, bf16[512,128]{1,0:T(8,128)(2,1)S(1)}, u32[]{:S(2)}, u32[]{:S(2)}) collective-permute-start(bf16[512,128]{1,0:T(8,128)(2,1)S(1)} %slice.34), channel_id=1, source_target_pairs={{0,224},{32,0},{64,32},{96,64},{128,96},{160,128},{192,160},{224,1... | collective-permute-start | bytes 393224 | tf_op jit(solution)/shard_map/ppermute | solution.py:27
  73.4 2.7 %copy-start.15 = (bf16[2,4,128,128]{3,2,1,0:T(8,128)(2,1)}, bf16[2,4,128,128]{3,2,1,0:T(8,128)(2,1)S(1)}, u32[]{:S(2)}) copy-start(bf16[2,4,128,128]{3,2,1,0:T(8,128)(2,1)S(1)} %get-tuple-element.248.refs_9_) | copy-start | bytes 786436
  73.4 2.7 %copy-start.17 = (bf16[2,4,128,128]{3,2,1,0:T(8,128)(2,1)}, bf16[2,4,128,128]{3,2,1,0:T(8,128)(2,1)S(1)}, u32[]{:S(2)}) copy-start(bf16[2,4,128,128]{3,2,1,0:T(8,128)(2,1)S(1)} %get-tuple-element.249.refs_10_) | copy-start | bytes 786436
  75.2 3.5 %copy-start.19 = (bf16[2,4,128,128]{3,2,1,0:T(8,128)(2,1)}, bf16[2,4,128,128]{3,2,1,0:T(8,128)(2,1)S(1)}, u32[]{:S(2)}) copy-start(bf16[2,4,128,128]{3,2,1,0:T(8,128)(2,1)S(1)} %get-tuple-element.245.refs_6_) | copy-start | bytes 786436
  75.2 3.5 %copy-start.21 = (bf16[2,4,128,128]{3,2,1,0:T(8,128)(2,1)}, bf16[2,4,128,128]{3,2,1,0:T(8,128)(2,1)S(1)}, u32[]{:S(2)}) copy-start(bf16[2,4,128,128]{3,2,1,0:T(8,128)(2,1)S(1)} %get-tuple-element.246.refs_7_) | copy-start | bytes 786436
  75.2 3.5 %copy-start.33 = (f32[2,8,128]{2,1,0:T(8,128)}, f32[2,8,128]{2,1,0:T(8,128)S(1)}, u32[]{:S(2)}) copy-start(f32[2,8,128]{2,1,0:T(8,128)S(1)} %get-tuple-element.247.refs_8_) | copy-start | bytes 24580
  76.1 2.6 %copy-start.29 = (bf16[1,4,128,128]{3,2,1,0:T(8,128)(2,1)}, bf16[1,4,128,128]{3,2,1,0:T(8,128)(2,1)S(1)}, u32[]{:S(2)}) copy-start(bf16[1,4,128,128]{3,2,1,0:T(8,128)(2,1)S(1)} %get-tuple-element.251.refs_12_) | copy-start | bytes 393220
  76.1 2.6 %copy-start.31 = (bf16[1,4,128,128]{3,2,1,0:T(8,128)(2,1)}, bf16[1,4,128,128]{3,2,1,0:T(8,128)(2,1)S(1)}, u32[]{:S(2)}) copy-start(bf16[1,4,128,128]{3,2,1,0:T(8,128)(2,1)S(1)} %get-tuple-element.252.refs_13_) | copy-start | bytes 393220
  78.7 21.3 %collective-permute-start.16 = (bf16[4,256,512]{2,1,0:T(8,128)(2,1)S(1)}, bf16[4,256,512]{2,1,0:T(8,128)(2,1)S(1)}, u32[]{:S(2)}, u32[]{:S(2)}) collective-permute-start(bf16[4,256,512]{2,1,0:T(8,128)(2,1)S(1)} %send1.1), channel_id=1, source_target_pairs={{0,4},{4,0},{1,5},{5,1},{2,6},{6,2},{3,7},{7,3},{8,12},{12,8},{9,1... | collective-permute-start | bytes 3145736 | tf_op jit(solution)/shard_map/ppermute | solution.py:27
  78.8 8.2 %copy-start.39 = (s32[1,1,256]{2,1,0:T(1,128)S(1)}, s32[1,1,256]{2,1,0:T(1,128)}, u32[]{:S(2)}) copy-start(s32[1,1,256]{2,1,0:T(1,128)} %param.24) | copy-start | bytes 3076
  81.4 27.5 %collective-permute-start.12 = (bf16[4,256,512]{2,1,0:T(8,128)(2,1)S(1)}, bf16[4,256,512]{2,1,0:T(8,128)(2,1)S(1)}, u32[]{:S(2)}, u32[]{:S(2)}) collective-permute-start(bf16[4,256,512]{2,1,0:T(8,128)(2,1)S(1)} %send0.1), channel_id=1, source_target_pairs={{0,4},{4,0},{1,5},{5,1},{2,6},{6,2},{3,7},{7,3},{8,12},{12,8},{9,1... | collective-permute-start | bytes 3145736 | tf_op jit(solution)/shard_map/ppermute | solution.py:27
  81.9 14.2 %collective-permute-start.19 = (bf16[8,16,1024]{2,1,0:T(8,128)(2,1)S(1)}, bf16[8,16,1024]{2,1,0:T(8,128)(2,1)S(1)}, u32[]{:S(2)}, u32[]{:S(2)}) collective-permute-start(bf16[8,16,1024]{2,1,0:T(8,128)(2,1)S(1)} %get-tuple-element.292), channel_id=1, source_target_pairs={{0,24},{8,0},{16,8},{24,16},{1,25},{9,1},{17,9},{25,17},{2,26},{10... | collective-permute-start | bytes 786440 | tf_op jit(solution)/shard_map/ppermute | solution.py:27
  84.7 11.5 %collective-permute-start.18 = (bf16[8,16,1024]{2,1,0:T(8,128)(2,1)S(1)}, bf16[8,16,1024]{2,1,0:T(8,128)(2,1)S(1)}, u32[]{:S(2)}, u32[]{:S(2)}) collective-permute-start(bf16[8,16,1024]{2,1,0:T(8,128)(2,1)S(1)} %get-tuple-element.291), channel_id=1, source_target_pairs={{0,16},{8,24},{16,0},{24,8},{1,17},{9,25},{17,1},{25,9},{2,18},{10... | collective-permute-start | bytes 786440 | tf_op jit(solution)/shard_map/ppermute | solution.py:27
  85.5 14.3 %collective-permute-start.17 = (bf16[8,16,1024]{2,1,0:T(8,128)(2,1)S(1)}, bf16[8,16,1024]{2,1,0:T(8,128)(2,1)S(1)}, u32[]{:S(2)}, u32[]{:S(2)}) collective-permute-start(bf16[8,16,1024]{2,1,0:T(8,128)(2,1)S(1)} %get-tuple-element.290), channel_id=1, source_target_pairs={{0,8},{8,16},{16,24},{24,0},{1,9},{9,17},{17,25},{25,1},{2,10},{10... | collective-permute-start | bytes 786440 | tf_op jit(solution)/shard_map/ppermute | solution.py:27
  100.0 3.5 %copy-start.35 = (f32[8,16,1024]{2,1,0:T(8,128)}, f32[8,16,1024]{2,1,0:T(8,128)S(1)}, u32[]{:S(2)}) copy-start(f32[8,16,1024]{2,1,0:T(8,128)S(1)} %convert_add_fusion) | copy-start | bytes 1572868
  100.0 8.9 %copy-start.28 = (bf16[1,4,128,128]{3,2,1,0:T(8,128)(2,1)S(1)}, bf16[1,4,128,128]{3,2,1,0:T(8,128)(2,1)}, u32[]{:S(2)}) copy-start(bf16[1,4,128,128]{3,2,1,0:T(8,128)(2,1)} %copy-done.27) | copy-start | bytes 393220
  100.0 8.9 %copy-start.34 = (f32[2,8,128]{2,1,0:T(8,128)S(1)}, f32[2,8,128]{2,1,0:T(8,128)}, u32[]{:S(2)}) copy-start(f32[2,8,128]{2,1,0:T(8,128)} %copy-done.33) | copy-start | bytes 24580
  104.2 33.2 %all-to-all-start.1 = ((bf16[8,16,1024]{2,1,0:T(8,128)(2,1)}), bf16[8,16,1024]{2,1,0:T(8,128)(2,1)}, u32[]{:S(2)}, u32[]{:S(2)}) async-start(bf16[8,16,1024]{2,1,0:T(8,128)(2,1)} %convert_element_type.67), calls=%async_computation.1 | async-start | bytes 524288 | tf_op jit(solution)/shard_map/all_to_all | solution.py:439
  116.4 5.3 %copy-start.38 = (s32[1,1,2048]{2,1,0:T(1,128)S(1)}, s32[1,1,2048]{2,1,0:T(1,128)}, u32[]{:S(2)}) copy-start(s32[1,1,2048]{2,1,0:T(1,128)} %param.20) | copy-start | bytes 24580
  116.4 33.5 %copy-start.5 = (f32[1,1,2048,128]{3,2,1,0:T(8,128)S(1)}, f32[1,1,2048,128]{3,2,1,0:T(8,128)}, u32[]{:S(2)}) copy-start(f32[1,1,2048,128]{3,2,1,0:T(8,128)} %param.21) | copy-start | bytes 3145732
  116.4 33.5 %copy-start.7 = (f32[1,1,2048]{2,1,0:T(1,128)S(1)}, f32[1,1,2048]{2,1,0:T(1,128)}, u32[]{:S(2)}) copy-start(f32[1,1,2048]{2,1,0:T(1,128)} %param.22) | copy-start | bytes 24580
  116.4 33.5 %copy-start.8 = (s32[1,1,256]{2,1,0:T(1,128)S(1)}, s32[1,1,256]{2,1,0:T(1,128)}, u32[]{:S(2)}) copy-start(s32[1,1,256]{2,1,0:T(1,128)} %param.23) | copy-start | bytes 3076
  121.2 16.3 %collective-permute-start.13 = (bf16[256,512]{1,0:T(8,128)(2,1)}, bf16[256,512]{1,0:T(8,128)(2,1)S(1)}, u32[]{:S(2)}, u32[]{:S(2)}) collective-permute-start(bf16[256,512]{1,0:T(8,128)(2,1)} %get-tuple-element.255), channel_id=1, source_target_pairs={{0,8},{8,16},{16,24},{24,0},{1,9},{9,17},{17,25},{25,1},{2,10},{10... | collective-permute-start | bytes 786440 | tf_op jit(solution)/shard_map/ppermute | solution.py:27
  122.8 17.2 %collective-permute-start.14 = (bf16[256,512]{1,0:T(8,128)(2,1)}, bf16[256,512]{1,0:T(8,128)(2,1)S(1)}, u32[]{:S(2)}, u32[]{:S(2)}) collective-permute-start(bf16[256,512]{1,0:T(8,128)(2,1)} %copy-done.6), channel_id=1, source_target_pairs={{0,16},{8,24},{16,0},{24,8},{1,17},{9,25},{17,1},{25,9},{2,18},{10... | collective-permute-start | bytes 786440 | tf_op jit(solution)/shard_map/ppermute | solution.py:27
  125.0 15.1 %collective-permute-start.15 = (bf16[256,512]{1,0:T(8,128)(2,1)S(1)}, bf16[256,512]{1,0:T(8,128)(2,1)S(1)}, u32[]{:S(2)}, u32[]{:S(2)}) collective-permute-start(bf16[256,512]{1,0:T(8,128)(2,1)S(1)} %get-tuple-element.257), channel_id=1, source_target_pairs={{0,24},{8,0},{16,8},{24,16},{1,25},{9,1},{17,9},{25,17},{2,26},{10... | collective-permute-start | bytes 786440 | tf_op jit(solution)/shard_map/ppermute | solution.py:27
  126.4 21.1 %collective-permute-start.20 = (bf16[256,512]{1,0:T(8,128)(2,1)S(1)}, bf16[256,512]{1,0:T(8,128)(2,1)S(1)}, u32[]{:S(2)}, u32[]{:S(2)}) collective-permute-start(bf16[256,512]{1,0:T(8,128)(2,1)S(1)} %get-tuple-element.294), channel_id=1, source_target_pairs={{0,8},{8,16},{16,24},{24,0},{1,9},{9,17},{17,25},{25,1},{2,10},{10... | collective-permute-start | bytes 786440 | tf_op jit(solution)/shard_map/ppermute | solution.py:27
  127.0 20.4 %collective-permute-start.21 = (bf16[256,512]{1,0:T(8,128)(2,1)S(1)}, bf16[256,512]{1,0:T(8,128)(2,1)}, u32[]{:S(2)}, u32[]{:S(2)}) collective-permute-start(bf16[256,512]{1,0:T(8,128)(2,1)S(1)} %get-tuple-element.295), channel_id=1, source_target_pairs={{0,16},{8,24},{16,0},{24,8},{1,17},{9,25},{17,1},{25,9},{2,18},{10... | collective-permute-start | bytes 786440 | tf_op jit(solution)/shard_map/ppermute | solution.py:27
  137.5 12.4 %collective-permute-start.22 = (bf16[256,512]{1,0:T(8,128)(2,1)S(1)}, bf16[256,512]{1,0:T(8,128)(2,1)}, u32[]{:S(2)}, u32[]{:S(2)}) collective-permute-start(bf16[256,512]{1,0:T(8,128)(2,1)S(1)} %get-tuple-element.296), channel_id=1, source_target_pairs={{0,24},{8,0},{16,8},{24,16},{1,25},{9,1},{17,9},{25,17},{2,26},{10... | collective-permute-start | bytes 786440 | tf_op jit(solution)/shard_map/ppermute | solution.py:27
  159.5 5.1 %collective-permute-start.23 = (f32[136,128]{1,0:T(8,128)S(1)}, f32[136,128]{1,0:T(8,128)S(1)}, u32[]{:S(2)}, u32[]{:S(2)}) collective-permute-start(f32[136,128]{1,0:T(8,128)S(1)} %get-tuple-element.310), channel_id=1, source_target_pairs={{0,1},{1,2},{2,3},{3,0},{4,5},{5,6},{6,7},{7,4},{8,9},{9,10},{10,1... | collective-permute-start | bytes 208904 | tf_op jit(solution)/shard_map/ppermute | solution.py:27
  160.3 5.9 %collective-permute-start.24 = (f32[136,128]{1,0:T(8,128)S(1)}, f32[136,128]{1,0:T(8,128)S(1)}, u32[]{:S(2)}, u32[]{:S(2)}) collective-permute-start(f32[136,128]{1,0:T(8,128)S(1)} %get-tuple-element.311), channel_id=1, source_target_pairs={{0,2},{1,3},{2,0},{3,1},{4,6},{5,7},{6,4},{7,5},{8,10},{9,11},{10,... | collective-permute-start | bytes 208904 | tf_op jit(solution)/shard_map/ppermute | solution.py:27
  161.9 5.0 %collective-permute-start.25 = (f32[136,128]{1,0:T(8,128)S(1)}, f32[136,128]{1,0:T(8,128)S(1)}, u32[]{:S(2)}, u32[]{:S(2)}) collective-permute-start(f32[136,128]{1,0:T(8,128)S(1)} %get-tuple-element.312), channel_id=1, source_target_pairs={{0,3},{1,0},{2,1},{3,2},{4,7},{5,4},{6,5},{7,6},{8,11},{9,8},{10,9... | collective-permute-start | bytes 208904 | tf_op jit(solution)/shard_map/ppermute | solution.py:27
  (20 other events, 18.9 us)
where the time goes:
time: 170 us; the launch traced here: 168 us
  waiting for transfers between devices  54.8 us (32%)
  starting transfers between devices  47.8 us (28%)
  Pallas kernels  40.1 us (24%)
  local copies, waits for them, and re-layouts  18.7 us (11%)
  other arithmetic  4.86 us (3%)
  between operations  1.7 us (1%)
    ppermute x26, waiting for transfers between devices, shifted(): return lax.ppermute(x, axis, [(i, (i + step) % size) for i in range(size)])  54.8 us
    ppermute x26, starting transfers between devices, shifted(): return lax.ppermute(x, axis, [(i, (i + step) % size) for i in range(size)])  34.8 us
    unnamed x81, local copies, waits for them, and re-layouts  18.1 us
    all_to_all x1, starting transfers between devices, on_device(): codes = lax.all_to_all(codes, Z, split_axis=0, concat_axis=0, tiled=True)  8.46 us
    pallas_call x1, Pallas kernels, on_device(): call(update_kernel, [SMEM] * 3 + [VMEM] * 11, [shape((2048, 128), F32), s...  7.45 us
    pallas_call x5, Pallas kernels, pick(): call(functools.partial(pick_kernel, count), [VMEM] * 4, outs, [pltpu.VMEM...  7.13 us
    pallas_call x2, Pallas kernels, on_device(): call(keep_kernel, [VMEM] * 16, [shape((256, 512), F32)] + [shape((256, 51...  5.95 us
    pallas_call x1, Pallas kernels, on_device(): call(top_kernel, [SMEM, VMEM, VMEM, VMEM], [shape((bags, 1024), BF16), sh...  5.62 us
  transfers between devices with their start and end apart: 28, of which 16 were waited for; matrix products, arithmetic and copies ran while one was open for 4% of the time, Pallas kernels for 12%

commit v1 on v0

--- a/solution.py
+++ b/solution.py
@@ -34,7 +34,7 @@
         out_specs=[VMEM] * len(outs),
         out_shape=outs,
         scratch_shapes=scratch,
-        compiler_params=pltpu.CompilerParams(vmem_limit_bytes=48 << 20),
+        compiler_params=pltpu.CompilerParams(vmem_limit_bytes=20 << 20),
         cost_estimate=pl.CostEstimate(flops=flops, bytes_accessed=moved, transcendentals=0),
         name=name,
     )
@@ -228,11 +228,37 @@
     lax.fori_loop(0, 2, piece, 0)
 
 
-def update_kernel(pos, slots_s, goal_s, slot_map, weight, accum, *refs):
-    parts, refs = refs[:8], refs[8:]
-    new_weight, new_accum = refs[:2]
-    held, refs = refs[2:6], refs[6:]
-    rhs, acc_wide, hold, hold_acc = refs
+def finish_kernel(pos, total, blocks, out):
+    z = pos[0]
+    acc = total[z]
+    for k in range(1, 8):
+        acc = acc + blocks[lax.rem(z + k, 8)].astype(F32)
+    out[...] = acc
+
+
+def leave_kernel(slots_s, goal_s, accum_s, weight, slot_out, weight_out, accum_out):
+    slot_out[...] = jnp.full_like(slot_out, -1.0)
+    weight_out[...] = jnp.zeros_like(weight_out)
+    accum_out[...] = jnp.zeros_like(accum_out)
+
+    def leave(i, carry):
+        for j in range(4):
+            slot, goal = slots_s[4 * i + j], goal_s[4 * i + j]
+            at = pl.ds(goal, 1)
+            slot_out[at, :] = jnp.full((1, 128), slot, I32).astype(F32)
+            weight_out[at, :] = weight[pl.ds(slot, 1), :]
+            accum_out[at, :] = jnp.full((1, 128), accum_s[slot], F32)
+        return carry
+
+    lax.fori_loop(0, slots_s.shape[0] // 4, leave, 0)
+
+
+def square():
+    return lax.broadcasted_iota(I32, (128, 128), 0) == lax.broadcasted_iota(I32, (128, 128), 1)
+
+
+def evict_kernel(slot_map, slot_in, weight, accum, *refs):
+    parts, rhs, held, pick = refs[:8], refs[8], refs[9:13], refs[13]
     for t in range(2):
         own = parts[4 * t][...]
         for k in range(1, 4):
@@ -243,17 +269,41 @@
             at = (4 * t + l) * 256
             rhs[at : at + 256, :128] = high[:, l * 128 : (l + 1) * 128]
             rhs[at : at + 256, 128:] = low[:, l * 128 : (l + 1) * 128]
-    hold[...] = jnp.zeros_like(hold)
-    hold_acc[...] = jnp.zeros_like(hold_acc)
-    eye = lax.broadcasted_iota(I32, (128, 128), 0) == lax.broadcasted_iota(I32, (128, 128), 1)
+    eye = square()
+
+    def block(k, carry):
+        at = pl.ds(pl.multiple_of(k * 128, 128), 128)
+        slots = slot_in[at, :]
+        for i in range(16):
+            lane = slice(i * 128, (i + 1) * 128)
+            pick[:, lane] = jnp.where(slots == slot_map[:, lane], 1.0, 0.0).astype(BF16)
+        both = jnp.dot(pick[...], rhs[...], preferred_element_type=F32)
+        g = both[:, :128] + both[:, 128:]
+        acc = accum[at, :] + jnp.sum(g * g, axis=1, keepdims=True) * (1.0 / 128.0)
+        row = weight[at, :] - LEARN_RATE * g / (jnp.sqrt(acc) + EPSILON)
+        line = jnp.sum(jnp.where(eye, acc, 0.0), axis=0, keepdims=True)
+        for i in range(4):
+
+            @pl.when(k == i)
+            def _():
+                held[i][:128, :] = row
+                held[i][128:, :] = jnp.broadcast_to(line, (HELD - 128, 128))
+
+        return carry
+
+    lax.fori_loop(0, 4, block, 0)
+
+
+def update_kernel(slot_map, rhs, weight, accum, new_weight, new_accum):
+    eye = square()
     step = 256
     ids = lax.broadcasted_iota(I32, (step, 2048), 0).astype(F32).astype(BF16)
     slot_row = slot_map[...]
 
     def chunk(i, carry):
         at = pl.multiple_of(i * step, step)
-        near = slot_row - at
-        near = jnp.where((near >= 0) & (near < step), near, 2 * step).astype(F32).astype(BF16)
+        near = slot_row - at.astype(F32)
+        near = jnp.where((near >= 0.0) & (near < step), near, 2.0 * step).astype(BF16)
         pick = jnp.where(
             jnp.broadcast_to(near, (step, 2048)) == ids, jnp.ones((), BF16), jnp.zeros((), BF16)
         )
@@ -264,27 +314,12 @@
             b = i * (step // 128) + j
             kept = jnp.sum(jnp.where(eye, accum[pl.ds(b, 1), :], 0.0), axis=1, keepdims=True)
             acc = kept + jnp.sum(g * g, axis=1, keepdims=True) * (1.0 / 128.0)
-            wide = jnp.broadcast_to(acc, (128, 128))
             here = pl.ds(pl.multiple_of(at + j * 128, 128), 128)
-            acc_wide[here, :] = wide
-            new_accum[pl.ds(b, 1), :] = jnp.sum(jnp.where(eye, wide, 0.0), axis=0, keepdims=True)
+            new_accum[pl.ds(b, 1), :] = jnp.sum(jnp.where(eye, acc, 0.0), axis=0, keepdims=True)
             new_weight[here, :] = weight[here, :] - LEARN_RATE * g / (jnp.sqrt(acc) + EPSILON)
         return carry
 
     lax.fori_loop(0, 2048 // step, chunk, 0)
-
-    def leave(i, carry):
-        for j in range(8):
-            slot, goal = slots_s[8 * i + j], goal_s[8 * i + j]
-            hold[pl.ds(goal, 1), :] = new_weight[pl.ds(slot, 1), :]
-            hold_acc[pl.ds(goal, 1), :] = acc_wide[pl.ds(slot, 1), :]
-        return carry
-
-    lax.fori_loop(0, slots_s.shape[0] // 8, leave, 0)
-    for k in range(4):
-        held[k][:128, :] = hold[k * 128 : (k + 1) * 128, :]
-        line = jnp.sum(jnp.where(eye, hold_acc[k * 128 : (k + 1) * 128, :], 0.0), axis=0, keepdims=True)
-        held[k][128:, :] = jnp.broadcast_to(line, (HELD - 128, 128))
 
 
 def arrive_kernel(pos, b0, b1, b2, b3, rows, accum):
@@ -336,9 +371,6 @@
     )(pos, pooled, w_up, grad_out)
     got = [shifted(parts[k], H, k) for k in (1, 2, 3)]
 
-    (delta,), (owners, rows, lookup_weight, lens) = together(
-        (delta,), (owners, rows, lookup_weight, lens)
-    )
     value = rows * 2048 + (lookup_weight.astype(F32) * 512.0).astype(I32)
     (codes,) = call(
         code_kernel, [SMEM, VMEM, VMEM, VMEM], [shape((8, 16, bags), I32)], [], 1 << 22, 1 << 20, "codes"
@@ -400,25 +432,31 @@
     mid = (up, down)
     (up, down), near, *picked = together((up, down), near, *picked)
     up, down = shifted(up, Z, 1), shifted(down, Z, -1)
-    picked.append(pick(1, near))
     grad_x = grad + there
     total, blocks = grad_x[0], [grad_x[k].astype(BF16) for k in (1, 2, 3)]
+    near, (total,), blocks = together(near, (total,), blocks)
+    got_x = [shifted(blocks[k - 1], X, k) for k in (1, 2, 3)]
+    picked.append(pick(1, near))
     far = (up, down)
-    (up, down), mid, (total,), blocks, picked[1] = together((up, down), mid, (total,), blocks, picked[1])
+    (up, down), mid, picked[1] = together((up, down), mid, picked[1])
     last = (shifted(up[:bags], Z, 1), shifted(down[bags:], Z, -1))
-    got_x = [shifted(blocks[k - 1], X, k) for k in (1, 2, 3)]
     picked.append(pick(2, mid))
+    far, picked[2] = together(far, picked[2])
     picked.append(pick(3, far))
+    last, got_x, picked[3] = together(last, got_x, picked[3])
     picked.append(pick(4, last))
 
     work = [pltpu.VMEM((256, 8 * MOST), BF16), pltpu.VMEM((8 * MOST, 512), BF16)]
     half = lambda t, side: [a for p in picked for a in p[3 * (2 * t + side) : 3 * (2 * t + side) + 3]]
     others = []
     for t in range(2):
+        if others:
+            others, picked[4] = together(others, picked[4])
         (out,) = call(
             send_kernel, [VMEM] * 15, [shape((4, 256, 512), BF16)], work, 4 << 30, 5 << 20, f"send{t}"
         )(*half(t, 1))
-        others.append(shifted(out, C, 1))
+        others.append(out)
+    others = [shifted(out, C, 1) for out in others]
     arrived = []
     for t in range(2):
         outs = call(
@@ -430,16 +468,26 @@
             5 << 20,
             f"keep{t}",
         )(others[t], *half(t, 0))
+        if t == 0:
+            outs, (others[1],) = together(outs, (others[1],))
         arrived += [outs[0]] + [shifted(outs[k], X, k) for k in (1, 2, 3)]
 
     for block in got_x:
         total = total + block.astype(F32)
-    keep_now, (total,) = together((arrived[4],), (total,))
-    arrived[4] = keep_now[0]
+    first, total, slot_map, evict_slots, evict_dest = lax.optimization_barrier(
+        (arrived[5], total, slot_map, evict_slots, evict_dest)
+    )
+    arrived[5] = first
     blocks = lax.all_to_all(total.astype(BF16), Z, split_axis=0, concat_axis=0, tiled=True)
-    blocks = jnp.where(jnp.arange(8, dtype=I32)[:, None, None] == z, 0.0, blocks.astype(F32))
-    grad_up = lax.dynamic_index_in_dim(total, z, 0, keepdims=False) + blocks.sum(axis=0)
-    arrived, (grad_up,) = together(arrived, (grad_up,))
+    (grad_up,) = call(
+        finish_kernel,
+        [SMEM, VMEM, VMEM],
+        [shape((16, 1024), F32)],
+        [],
+        1 << 10,
+        1 << 18,
+        "finish",
+    )(pos, total, blocks)
 
     list_len = evict_slots.shape[-1]
     departure = evict_dest[0, 0]
@@ -450,30 +498,38 @@
     counted = jnp.dot(before, picks, preferred_element_type=F32)
     placed = jnp.sum(counted * picks.astype(F32), axis=-1).astype(I32)
     goal = jnp.where(live, lax.rem(departure + 4 - h, 4) * 128 + placed, 512)
-    slot_rows = jnp.swapaxes(slot_map.reshape(2, 256, 4), 1, 2).reshape(1, 2048)
-    new_weight, new_accum, *held = call(
+    slot_rows = jnp.swapaxes(slot_map.reshape(2, 256, 4), 1, 2).reshape(1, 2048).astype(F32)
+    slot_rows, goal = lax.optimization_barrier((slot_rows, goal))
+    leaving = call(
+        leave_kernel,
+        [SMEM] * 3 + [VMEM],
+        [shape((520, 128), F32)] * 3,
+        [],
+        1 << 10,
+        1 << 20,
+        "leave",
+    )(evict_slots.reshape(-1), goal, cache_accum.reshape(-1), cache_weight[0, 0])
+    arrived, leaving = together(arrived, leaving)
+    rhs, *held = call(
+        evict_kernel,
+        [VMEM] * 12,
+        [shape((2048, 256), BF16)] + [shape((HELD, 128), F32)] * 4,
+        [pltpu.VMEM((128, 2048), BF16)],
+        1 << 29,
+        4 << 20,
+        "evict",
+    )(slot_rows, *leaving, *arrived)
+    moved = [shifted(held[k], H, k) for k in (1, 2, 3)]
+    new_weight, new_accum = call(
         update_kernel,
-        [SMEM] * 3 + [VMEM] * 11,
-        [shape((2048, 128), F32), shape((16, 128), F32)] + [shape((HELD, 128), F32)] * 4,
-        [
-            pltpu.VMEM((2048, 256), BF16),
-            pltpu.VMEM((2048, 128), F32),
-            pltpu.VMEM((520, 128), F32),
-            pltpu.VMEM((520, 128), F32),
-        ],
+        [VMEM] * 4,
+        [shape((2048, 128), F32), shape((16, 128), F32)],
+        [],
         2 << 30,
         4 << 20,
         "update",
-    )(
-        pos,
-        evict_slots.reshape(-1),
-        goal,
-        slot_rows,
-        cache_weight[0, 0],
-        cache_accum.reshape(16, 128),
-        *arrived,
-    )
-    held = [held[0]] + [shifted(held[k], H, k) for k in (1, 2, 3)]
+    )(slot_rows, rhs, cache_weight[0, 0], cache_accum.reshape(16, 128))
+    held = [held[0]] + moved
     held_rows, held_accum = call(
         arrive_kernel,
         [SMEM] + [VMEM] * 4,

time: 170 us -> 138 us (0.81)
  waiting for transfers between devices: 54.8 us -> 27 us
  local copies, waits for them, and re-layouts: 18.7 us -> 8.23 us
  starting transfers between devices: 47.8 us -> 55.2 us
  Pallas kernels: 40.1 us -> 42.6 us
  other arithmetic: 4.86 us -> 2.64 us
    ppermute x26, waiting for transfers between devices: 54.8 us -> 27 us  [shifted(): return lax.ppermute(x, axis, [(i, (i + step) % size) for i in range(size)])]
    unnamed x81 -> x26, local copies, waits for them, and re-layouts: 18.1 us -> 7.69 us
    all_to_all x1, starting transfers between devices: 4.61 us -> 9.39 us  [on_device(): lax.all_to_all(total.astype(BF16), Z, split_axis=0, concat_axis=0, tiled=...]
    pallas_call x1 -> x4, Pallas kernels: 7.45 us -> 11.5 us  [the longest x1 5.32 us: on_device(): call(update_kernel, [VMEM] * 4, [shape((2048, 128), F32), shape((16, 128)...]
    ppermute x26, starting transfers between devices: 34.8 us -> 37.4 us  [shifted(): return lax.ppermute(x, axis, [(i, (i + step) % size) for i in range(size)])]
  transfers between devices with their start and end apart: 28 -> 28, of which waited for: 16 -> 11; matrix products, arithmetic and copies ran while one was open for 4% -> 2% of each run, Pallas kernels for 12% -> 24%
where the time goes in v1:
time: 138 us
  starting transfers between devices  55.2 us (40%)
  Pallas kernels  42.6 us (31%)
  waiting for transfers between devices  27 us (20%)
  local copies, waits for them, and re-layouts  8.23 us (6%)
  other arithmetic  2.64 us (2%)
  between operations  1.58 us (1%)
    ppermute x26, starting transfers between devices, shifted(): return lax.ppermute(x, axis, [(i, (i + step) % size) for i in range(size)])  37.4 us
    ppermute x26, waiting for transfers between devices, shifted(): return lax.ppermute(x, axis, [(i, (i + step) % size) for i in range(size)])  27 us
    all_to_all x1, starting transfers between devices, on_device(): lax.all_to_all(total.astype(BF16), Z, split_axis=0, concat_axis=0, tiled=...  9.39 us
    all_to_all x1, starting transfers between devices, on_device(): codes = lax.all_to_all(codes, Z, split_axis=0, concat_axis=0, tiled=True)  8.47 us
    unnamed x26, local copies, waits for them, and re-layouts  7.69 us
    pallas_call x5, Pallas kernels, pick(): call(functools.partial(pick_kernel, count), [VMEM] * 4, outs, [pltpu.VMEM...  7.15 us
    pallas_call x2, Pallas kernels, on_device(): call(keep_kernel, [VMEM] * 16, [shape((256, 512), F32)] + [shape((256, 51...  6.76 us
    pallas_call x1, Pallas kernels, on_device(): call(update_kernel, [VMEM] * 4, [shape((2048, 128), F32), shape((16, 128)...  5.32 us
  transfers between devices with their start and end apart: 28, of which 11 were waited for; matrix products, arithmetic and copies ran while one was open for 2% of the time, Pallas kernels for 24%

profile of v1, /device:TPU:8, one launch (start us, length us, event | category | flops | bytes accessed | tf_op | source)
XLA Modules:
  0.0 137.5 jit_solution(5943913444550190855)
XLA Ops:
  3.0 1.5 %codes.1 = s32[8,16,512]{2,1,0:T(8,128)} custom-call(s32[4]{0:T(128)S(1)} %pad_add_fusion.pos, s32[2,8,512]{2,1,0:T(8,128)S(1)} %bitcast.30, s32[2,8,512]{2,1,0:T(8,128)S(1)} %add_bitcast_fusion.value, s32[2,512]{1,0:T(2,128)S(1)} %copy-done.3), custom_call_target="tpu_custom_call" | custom-call | flops 4194304 | bytes 1048576 | tf_op jit(solution)/shard_map/codes/pallas_call | solution.py:375
  4.5 8.5 %all-to-all-start = ((s32[8,16,512]{2,1,0:T(8,128)}), s32[8,16,512]{2,1,0:T(8,128)S(1)}, u32[]{:S(2)}, u32[]{:S(2)}) async-start(s32[8,16,512]{2,1,0:T(8,128)} %codes.1), calls=%async_computation | async-start | bytes 524288 | tf_op jit(solution)/shard_map/all_to_all | solution.py:378
  12.9 1.6 %copy-done.5 = bf16[1024,1024]{1,0:T(8,128)(2,1)S(1)} copy-done((bf16[1024,1024]{1,0:T(8,128)(2,1)S(1)}, bf16[1024,1024]{1,0:T(8,128)(2,1)}, u32[]{:S(2)}) %copy-start.5) | copy-done | bytes 2097176
  14.5 1.2 copy-done.6
  15.8 1.2 copy-done.7
  17.0 4.5 %top.1 = (bf16[512,1024]{1,0:T(8,128)(2,1)S(1)}, f32[1024,128]{1,0:T(8,128)S(1)}, bf16[1024,128]{1,0:T(8,128)(2,1)S(1)}, bf16[1024,128]{1,0:T(8,128)(2,1)S(1)}, bf16[1024,128]{1,0:T(8,128)(2,1)S(1)}) custom-call(s32[4]{0:T(128)S(1)} %pad_add_fusion.pos, bf16[512,1024]{1,0:T(8,128)(2,1)S(1)} %copy-done.7, bf16[1024,1024]{1,0:T(8,128)(2,1)S(1)} %copy-done.5, ...), custom_call_target="tpu_custom_call" | custom-call | flops 2147483648 | bytes 6291456 | tf_op jit(solution)/shard_map/top/pallas_call | solution.py:363
  21.5 1.0 copy-done.9
  22.5 1.6 %collective-permute-start = (bf16[1024,128]{1,0:T(8,128)(2,1)S(1)}, bf16[1024,128]{1,0:T(8,128)(2,1)S(1)}, u32[]{:S(2)}, u32[]{:S(2)}) collective-permute-start(bf16[1024,128]{1,0:T(8,128)(2,1)S(1)} %get-tuple-element.215), channel_id=1, source_target_pairs={{0,1},{1,2},{2,3},{3,0},{4,5},{5,6},{6,7},{7,4},{8,9},{9,10},{10,1... | collective-permute-start | bytes 786440 | tf_op jit(solution)/shard_map/ppermute | solution.py:27
  25.0 2.4 %collective-permute-start.2 = (bf16[1024,128]{1,0:T(8,128)(2,1)S(1)}, bf16[1024,128]{1,0:T(8,128)(2,1)S(1)}, u32[]{:S(2)}, u32[]{:S(2)}) collective-permute-start(bf16[1024,128]{1,0:T(8,128)(2,1)S(1)} %get-tuple-element.217), channel_id=1, source_target_pairs={{0,3},{1,0},{2,1},{3,2},{4,7},{5,4},{6,5},{7,6},{8,11},{9,8},{10,9... | collective-permute-start | bytes 786440 | tf_op jit(solution)/shard_map/ppermute | solution.py:27
  27.4 4.3 %collective-permute-done = bf16[1024,128]{1,0:T(8,128)(2,1)S(1)} collective-permute-done((bf16[1024,128]{1,0:T(8,128)(2,1)S(1)}, bf16[1024,128]{1,0:T(8,128)(2,1)S(1)}, u32[]{:S(2)}, u32[]{:S(2)}) %collective-permute-start) | collective-permute-done | bytes 262176 | tf_op jit(solution)/shard_map/ppermute | solution.py:27
  31.7 3.1 %collective-permute-done.1 = bf16[1024,128]{1,0:T(8,128)(2,1)S(1)} collective-permute-done((bf16[1024,128]{1,0:T(8,128)(2,1)S(1)}, bf16[1024,128]{1,0:T(8,128)(2,1)S(1)}, u32[]{:S(2)}, u32[]{:S(2)}) %collective-permute-start.1) | collective-permute-done | bytes 262176 | tf_op jit(solution)/shard_map/ppermute | solution.py:27
  34.8 3.1 %collective-permute-done.2 = bf16[1024,128]{1,0:T(8,128)(2,1)S(1)} collective-permute-done((bf16[1024,128]{1,0:T(8,128)(2,1)S(1)}, bf16[1024,128]{1,0:T(8,128)(2,1)S(1)}, u32[]{:S(2)}, u32[]{:S(2)}) %collective-permute-start.2) | collective-permute-done | bytes 262176 | tf_op jit(solution)/shard_map/ppermute | solution.py:27
  38.0 1.8 %collective-permute-start.3 = (bf16[1024,128]{1,0:T(8,128)(2,1)S(1)}, bf16[1024,128]{1,0:T(8,128)(2,1)S(1)}, u32[]{:S(2)}, u32[]{:S(2)}) collective-permute-start(bf16[1024,128]{1,0:T(8,128)(2,1)S(1)} %add_convert_fusion), channel_id=1, source_target_pairs={{0,32},{32,64},{64,96},{96,128},{128,160},{160,192},{192,224},{224... | collective-permute-start | bytes 786440 | tf_op jit(solution)/shard_map/ppermute | solution.py:27
  39.8 1.5 %collective-permute-start.4 = (bf16[1024,128]{1,0:T(8,128)(2,1)S(1)}, bf16[1024,128]{1,0:T(8,128)(2,1)S(1)}, u32[]{:S(2)}, u32[]{:S(2)}) collective-permute-start(bf16[1024,128]{1,0:T(8,128)(2,1)S(1)} %add_convert_fusion), channel_id=1, source_target_pairs={{0,224},{32,0},{64,32},{96,64},{128,96},{160,128},{192,160},{224,1... | collective-permute-start | bytes 786440 | tf_op jit(solution)/shard_map/ppermute | solution.py:27
  41.3 1.2 copy-done.10
  42.6 2.3 %grad.1 = (f32[4,8,16,1024]{3,2,1,0:T(8,128)S(1)}, f32[4,8,16,1024]{3,2,1,0:T(8,128)S(1)}) custom-call(s32[4]{0:T(128)S(1)} %pad_add_fusion.pos, bf16[512,1024]{1,0:T(8,128)(2,1)S(1)} %copy-done.8, bf16[512,1024]{1,0:T(8,128)(2,1)S(1)} %copy-done.10), custom_call_target="tpu_custom_call" | custom-call | flops 1073741824 | bytes 6291456 | tf_op jit(solution)/shard_map/grad/pallas_call | solution.py:418
  44.9 1.8 %collective-permute-done.3.refs_0_ = bf16[1024,128]{1,0:T(8,128)(2,1)S(1)} collective-permute-done((bf16[1024,128]{1,0:T(8,128)(2,1)S(1)}, bf16[1024,128]{1,0:T(8,128)(2,1)S(1)}, u32[]{:S(2)}, u32[]{:S(2)}) %collective-permute-start.3) | collective-permute-done | bytes 262176 | tf_op jit(solution)/shard_map/ppermute | solution.py:27
  46.9 2.5 %prep.1 = (f32[2,8,512]{2,1,0:T(8,128)S(1)}, f32[4,8,512]{2,1,0:T(8,128)S(1)}, f32[4,8,512]{2,1,0:T(8,128)S(1)}, f32[4,8,512]{2,1,0:T(8,128)S(1)}, f32[2,8,512]{...) custom-call(s32[4]{0:T(128)S(1)} %pad_add_fusion.pos, ...), custom_call_target="tpu_custom_call" | custom-call | flops 67108864 | bytes 3145728 | tf_op jit(solution)/shard_map/prep/pallas_call | solution.py:385
  49.4 1.5 %collective-permute-start.5 = (bf16[1024,128]{1,0:T(8,128)(2,1)S(1)}, bf16[1024,128]{1,0:T(8,128)(2,1)S(1)}, u32[]{:S(2)}, u32[]{:S(2)}) collective-permute-start(bf16[1024,128]{1,0:T(8,128)(2,1)S(1)} %collective-permute-done.3.refs_0_), channel_id=1, source_target_pairs={{0,32},{32,64},{64,96},{96,128},{128,160},{160,192},{192,224},{224... | collective-permute-start | bytes 786440 | tf_op jit(solution)/shard_map/ppermute | solution.py:27
  51.0 1.8 %collective-permute-start.6 = (bf16[1024,128]{1,0:T(8,128)(2,1)S(1)}, bf16[1024,128]{1,0:T(8,128)(2,1)S(1)}, u32[]{:S(2)}, u32[]{:S(2)}) collective-permute-start(bf16[1024,128]{1,0:T(8,128)(2,1)S(1)} %collective-permute-done.4.refs_1_), channel_id=1, source_target_pairs={{0,224},{32,0},{64,32},{96,64},{128,96},{160,128},{192,160},{224,1... | collective-permute-start | bytes 786440 | tf_op jit(solution)/shard_map/ppermute | solution.py:27
  53.7 5.8 %collective-permute-done.5.refs_0_ = bf16[1024,128]{1,0:T(8,128)(2,1)S(1)} collective-permute-done((bf16[1024,128]{1,0:T(8,128)(2,1)S(1)}, bf16[1024,128]{1,0:T(8,128)(2,1)S(1)}, u32[]{:S(2)}, u32[]{:S(2)}) %collective-permute-start.5) | collective-permute-done | bytes 262176 | tf_op jit(solution)/shard_map/ppermute | solution.py:27
  60.1 3.0 %collective-permute-start.7 = (bf16[1024,128]{1,0:T(8,128)(2,1)S(1)}, bf16[1024,128]{1,0:T(8,128)(2,1)S(1)}, u32[]{:S(2)}, u32[]{:S(2)}) collective-permute-start(bf16[1024,128]{1,0:T(8,128)(2,1)S(1)} %collective-permute-done.5.refs_0_), channel_id=1, source_target_pairs={{0,32},{32,64},{64,96},{96,128},{128,160},{160,192},{192,224},{224... | collective-permute-start | bytes 786440 | tf_op jit(solution)/shard_map/ppermute | solution.py:27
  64.2 1.6 %collective-permute-start.12 = (bf16[8,16,1024]{2,1,0:T(8,128)(2,1)S(1)}, bf16[8,16,1024]{2,1,0:T(8,128)(2,1)S(1)}, u32[]{:S(2)}, u32[]{:S(2)}) collective-permute-start(bf16[8,16,1024]{2,1,0:T(8,128)(2,1)S(1)} %get-tuple-element.292), channel_id=1, source_target_pairs={{0,8},{8,16},{16,24},{24,0},{1,9},{9,17},{17,25},{25,1},{2,10},{10... | collective-permute-start | bytes 786440 | tf_op jit(solution)/shard_map/ppermute | solution.py:27
  65.7 2.7 %collective-permute-start.13 = (bf16[8,16,1024]{2,1,0:T(8,128)(2,1)S(1)}, bf16[8,16,1024]{2,1,0:T(8,128)(2,1)S(1)}, u32[]{:S(2)}, u32[]{:S(2)}) collective-permute-start(bf16[8,16,1024]{2,1,0:T(8,128)(2,1)S(1)} %get-tuple-element.293), channel_id=1, source_target_pairs={{0,16},{8,24},{16,0},{24,8},{1,17},{9,25},{17,1},{25,9},{2,18},{10... | collective-permute-start | bytes 786440 | tf_op jit(solution)/shard_map/ppermute | solution.py:27
  68.5 1.4 %collective-permute-start.14 = (bf16[8,16,1024]{2,1,0:T(8,128)(2,1)S(1)}, bf16[8,16,1024]{2,1,0:T(8,128)(2,1)S(1)}, u32[]{:S(2)}, u32[]{:S(2)}) collective-permute-start(bf16[8,16,1024]{2,1,0:T(8,128)(2,1)S(1)} %get-tuple-element.294), channel_id=1, source_target_pairs={{0,24},{8,0},{16,8},{24,16},{1,25},{9,1},{17,9},{25,17},{2,26},{10... | collective-permute-start | bytes 786440 | tf_op jit(solution)/shard_map/ppermute | solution.py:27
  69.9 1.8 %pick1.1 = (bf16[2,4,128,128]{3,2,1,0:T(8,128)(2,1)S(1)}, bf16[2,4,128,128]{3,2,1,0:T(8,128)(2,1)S(1)}, f32[2,8,128]{2,1,0:T(8,128)S(1)}, bf16[2,4,128,128]{3,2,...) custom-call(f32[4,8,512]{2,1,0:T(8,128)S(1)} %get-tuple-element.248., ...), custom_call_target="tpu_custom_call" | custom-call | flops 1073741824 | bytes 4194304 | tf_op jit(solution)/shard_map/pick1/pallas_call | solution.py:402
  71.7 1.8 %collective-permute-start.10 = (bf16[512,128]{1,0:T(8,128)(2,1)S(1)}, bf16[512,128]{1,0:T(8,128)(2,1)S(1)}, u32[]{:S(2)}, u32[]{:S(2)}) collective-permute-start(bf16[512,128]{1,0:T(8,128)(2,1)S(1)} %slice.33), channel_id=1, source_target_pairs={{0,32},{32,64},{64,96},{96,128},{128,160},{160,192},{192,224},{224... | collective-permute-start | bytes 393224 | tf_op jit(solution)/shard_map/ppermute | solution.py:27
  73.5 1.6 %collective-permute-start.11 = (bf16[512,128]{1,0:T(8,128)(2,1)S(1)}, bf16[512,128]{1,0:T(8,128)(2,1)S(1)}, u32[]{:S(2)}, u32[]{:S(2)}) collective-permute-start(bf16[512,128]{1,0:T(8,128)(2,1)S(1)} %slice.34), channel_id=1, source_target_pairs={{0,224},{32,0},{64,32},{96,64},{128,96},{160,128},{192,160},{224,1... | collective-permute-start | bytes 393224 | tf_op jit(solution)/shard_map/ppermute | solution.py:27
  75.1 1.8 %pick2.1 = (bf16[2,4,128,128]{3,2,1,0:T(8,128)(2,1)S(1)}, bf16[2,4,128,128]{3,2,1,0:T(8,128)(2,1)S(1)}, f32[2,8,128]{2,1,0:T(8,128)S(1)}, bf16[2,4,128,128]{3,2,...) custom-call(f32[4,8,512]{2,1,0:T(8,128)S(1)} %get-tuple-element.271., ...), custom_call_target="tpu_custom_call" | custom-call | flops 1073741824 | bytes 4194304 | tf_op jit(solution)/shard_map/pick2/pallas_call | solution.py:402
  76.9 1.8 %pick3.1 = (bf16[2,4,128,128]{3,2,1,0:T(8,128)(2,1)S(1)}, bf16[2,4,128,128]{3,2,1,0:T(8,128)(2,1)S(1)}, f32[2,8,128]{2,1,0:T(8,128)S(1)}, bf16[2,4,128,128]{3,2,...) custom-call(f32[4,8,512]{2,1,0:T(8,128)S(1)} %get-tuple-element.295., ...), custom_call_target="tpu_custom_call" | custom-call | flops 1073741824 | bytes 4194304 | tf_op jit(solution)/shard_map/pick3/pallas_call | solution.py:402
  80.3 2.5 %send0.1 = bf16[4,256,512]{2,1,0:T(8,128)(2,1)S(1)} custom-call(bf16[1,4,128,128]{3,2,1,0:T(8,128)(2,1)S(1)} %get-tuple-element.243.refs_0_, bf16[1,4,128,128]{3,2,1,0:T(8,128)(2,1)S(1)} %get-tuple-element.244.refs_1_, f32[1,8,128]{2,1,0:T(8,128)S(1)} %get-tuple-element.245.refs_2_, bf16[2,4,128,128]{3,2,1,0:T(8,128)(2,1)S(1)} %get-tuple-element.268.refs_3_, ...), custom_call_target="tpu_custom_call" | custom-call | flops 4294967296 | bytes 5242880 | tf_op jit(solution)/shard_map/send0/pallas_call | solution.py:455
  83.0 2.5 %send1.1 = bf16[4,256,512]{2,1,0:T(8,128)(2,1)S(1)} custom-call(bf16[1,4,128,128]{3,2,1,0:T(8,128)(2,1)S(1)} %get-tuple-element.350.refs_0_, bf16[1,4,128,128]{3,2,1,0:T(8,128)(2,1)S(1)} %get-tuple-element.351.refs_1_, f32[1,8,128]{2,1,0:T(8,128)S(1)} %get-tuple-element.352.refs_2_, bf16[2,4,128,128]{3,2,1,0:T(8,128)(2,1)S(1)} %get-tuple-element.353.refs_3_, ...), custom_call_target="tpu_custom_call" | custom-call | flops 4294967296 | bytes 5242880 | tf_op jit(solution)/shard_map/send1/pallas_call | solution.py:455
  86.8 3.4 %keep0.1 = (f32[256,512]{1,0:T(8,128)S(1)}, bf16[256,512]{1,0:T(8,128)(2,1)}, bf16[256,512]{1,0:T(8,128)(2,1)}, bf16[256,512]{1,0:T(8,128)(2,1)}) custom-call(bf16[4,256,512]{2,1,0:T(8,128)(2,1)S(1)} %collective-permute-done.15.other, bf16[1,4,128,128]{3,2,1,0:T(8,128)(2,1)S(1)} %get-tuple-element.331.refs_0_, ...), custom_call_target="tpu_custom_call" | custom-call | flops 4294967296 | bytes 5242880 | tf_op jit(solution)/shard_map/keep0/pallas_call | solution.py:462
  90.2 3.3 %keep1.1 = (f32[256,512]{1,0:T(8,128)S(1)}, bf16[256,512]{1,0:T(8,128)(2,1)S(1)}, bf16[256,512]{1,0:T(8,128)(2,1)}, bf16[256,512]{1,0:T(8,128)(2,1)}) custom-call(bf16[4,256,512]{2,1,0:T(8,128)(2,1)S(1)} %collective-permute-done.16.other, bf16[1,4,128,128]{3,2,1,0:T(8,128)(2,1)S(1)} %get-tuple-element.366.refs_0_, ...), custom_call_target="tpu_custom_call" | custom-call | flops 4294967296 | bytes 5242880 | tf_op jit(solution)/shard_map/keep1/pallas_call | solution.py:462
  93.5 1.5 %collective-permute-start.17 = (bf16[256,512]{1,0:T(8,128)(2,1)S(1)}, bf16[256,512]{1,0:T(8,128)(2,1)S(1)}, u32[]{:S(2)}, u32[]{:S(2)}) collective-permute-start(bf16[256,512]{1,0:T(8,128)(2,1)S(1)} %get-tuple-element.381), channel_id=1, source_target_pairs={{0,8},{8,16},{16,24},{24,0},{1,9},{9,17},{17,25},{25,1},{2,10},{10... | collective-permute-start | bytes 786440 | tf_op jit(solution)/shard_map/ppermute | solution.py:27
  95.2 2.5 %collective-permute-start.21 = (bf16[256,512]{1,0:T(8,128)(2,1)}, bf16[256,512]{1,0:T(8,128)(2,1)S(1)}, u32[]{:S(2)}, u32[]{:S(2)}) collective-permute-start(bf16[256,512]{1,0:T(8,128)(2,1)} %get-tuple-element.396), channel_id=1, source_target_pairs={{0,16},{8,24},{16,0},{24,8},{1,17},{9,25},{17,1},{25,9},{2,18},{10... | collective-permute-start | bytes 786440 | tf_op jit(solution)/shard_map/ppermute | solution.py:27
  97.7 1.5 %collective-permute-start.22 = (bf16[256,512]{1,0:T(8,128)(2,1)}, bf16[256,512]{1,0:T(8,128)(2,1)}, u32[]{:S(2)}, u32[]{:S(2)}) collective-permute-start(bf16[256,512]{1,0:T(8,128)(2,1)} %get-tuple-element.397), channel_id=1, source_target_pairs={{0,24},{8,0},{16,8},{24,16},{1,25},{9,1},{17,9},{25,17},{2,26},{10... | collective-permute-start | bytes 786440 | tf_op jit(solution)/shard_map/ppermute | solution.py:27
  99.7 1.1 collective-permute-start.19
  100.8 3.8 %collective-permute-done.17.refs_5_ = bf16[256,512]{1,0:T(8,128)(2,1)S(1)} collective-permute-done((bf16[256,512]{1,0:T(8,128)(2,1)S(1)}, bf16[256,512]{1,0:T(8,128)(2,1)S(1)}, u32[]{:S(2)}, u32[]{:S(2)}) %collective-permute-start.17) | collective-permute-done | bytes 262176 | tf_op jit(solution)/shard_map/ppermute | solution.py:27
  106.3 9.4 %all-to-all-start.1 = ((bf16[8,16,1024]{2,1,0:T(8,128)(2,1)}), bf16[8,16,1024]{2,1,0:T(8,128)(2,1)S(1)}, u32[]{:S(2)}, u32[]{:S(2)}) async-start(bf16[8,16,1024]{2,1,0:T(8,128)(2,1)} %convert_element_type.84), calls=%async_computation.1 | async-start | bytes 524288 | tf_op jit(solution)/shard_map/all_to_all | solution.py:481
  116.0 1.6 %leave.1 = (f32[520,128]{1,0:T(8,128)S(1)}, f32[520,128]{1,0:T(8,128)S(1)}, f32[520,128]{1,0:T(8,128)S(1)}) custom-call(s32[256]{0:T(256)S(1)} %bitcast.33, s32[256]{0:T(256)S(1)} %fusion.9.goal_s, f32[2048]{0:T(1024)S(1)} %bitcast.31, f32[2048,128]{1,0:T(8,128)S(1)} %bitcast.28), custom_call_target="tpu_custom_call" | custom-call | flops 1024 | bytes 1048576 | tf_op jit(solution)/shard_map/leave/pallas_call | solution.py:503
  117.6 3.0 %collective-permute-done.19.refs_2_ = bf16[256,512]{1,0:T(8,128)(2,1)} collective-permute-done((bf16[256,512]{1,0:T(8,128)(2,1)}, bf16[256,512]{1,0:T(8,128)(2,1)}, u32[]{:S(2)}, u32[]{:S(2)}) %collective-permute-start.19) | collective-permute-done | bytes 262176 | tf_op jit(solution)/shard_map/ppermute | solution.py:27
  121.1 3.4 %evict.1 = (bf16[2048,256]{1,0:T(8,128)(2,1)S(1)}, f32[136,128]{1,0:T(8,128)S(1)}, f32[136,128]{1,0:T(8,128)S(1)}, f32[136,128]{1,0:T(8,128)S(1)}, f32[136,128]{1,0:T(8,128)S(1)}) custom-call(f32[1,2048]{1,0:T(1,128)S(1)} %convert_element_type.88.slot_map, f32[520,128]{1,0:T(8,128)S(1)} %get-tuple-element.403.slot_in, ...), custom_call_target="tpu_custom_call" | custom-call | flops 536870912 | bytes 4194304 | tf_op jit(solution)/shard_map/evict/pallas_call | solution.py:513
  125.3 1.9 %collective-permute-start.24 = (f32[136,128]{1,0:T(8,128)S(1)}, f32[136,128]{1,0:T(8,128)S(1)}, u32[]{:S(2)}, u32[]{:S(2)}) collective-permute-start(f32[136,128]{1,0:T(8,128)S(1)} %get-tuple-element.419), channel_id=1, source_target_pairs={{0,2},{1,3},{2,0},{3,1},{4,6},{5,7},{6,4},{7,5},{8,10},{9,11},{10,... | collective-permute-start | bytes 208904 | tf_op jit(solution)/shard_map/ppermute | solution.py:27
  127.2 2.5 %collective-permute-start.25 = (f32[136,128]{1,0:T(8,128)S(1)}, f32[136,128]{1,0:T(8,128)S(1)}, u32[]{:S(2)}, u32[]{:S(2)}) collective-permute-start(f32[136,128]{1,0:T(8,128)S(1)} %get-tuple-element.420), channel_id=1, source_target_pairs={{0,3},{1,0},{2,1},{3,2},{4,7},{5,4},{6,5},{7,6},{8,11},{9,8},{10,9... | collective-permute-start | bytes 208904 | tf_op jit(solution)/shard_map/ppermute | solution.py:27
  129.7 5.3 %update.1 = (f32[2048,128]{1,0:T(8,128)}, f32[16,128]{1,0:T(8,128)}) custom-call(f32[1,2048]{1,0:T(1,128)S(1)} %convert_element_type.88.slot_map, bf16[2048,256]{1,0:T(8,128)(2,1)S(1)} %get-tuple-element.414.rhs, f32[2048,128]{1,0:T(8,128)S(1)} %bitcast.29, f32[16,128]{1,0:T(8,128)S(1)} %bitcast.32), custom_call_target="tpu_custom_call" | custom-call | flops 2147483648 | bytes 4194304 | tf_op jit(solution)/shard_map/update/pallas_call | solution.py:523
  135.0 1.3 arrive.1
  136.3 1.2 finish.1
  (70 shorter events, 12.5 us)
Async XLA Ops:
  1.5 0.8 copy-start.1
  2.3 0.7 copy-start.3
  4.5 33.4 %all-to-all-start = ((s32[8,16,512]{2,1,0:T(8,128)}), s32[8,16,512]{2,1,0:T(8,128)S(1)}, u32[]{:S(2)}, u32[]{:S(2)}) async-start(s32[8,16,512]{2,1,0:T(8,128)} %codes.1), calls=%async_computation | async-start | bytes 524288 | tf_op jit(solution)/shard_map/all_to_all | solution.py:378
  12.9 1.6 %copy-start.5 = (bf16[1024,1024]{1,0:T(8,128)(2,1)S(1)}, bf16[1024,1024]{1,0:T(8,128)(2,1)}, u32[]{:S(2)}) copy-start(bf16[1024,1024]{1,0:T(8,128)(2,1)} %w_up.1) | copy-start | bytes 6291460
  14.5 1.2 copy-start.6
  15.8 1.2 copy-start.7
  17.0 24.3 %copy-start.8 = (bf16[512,1024]{1,0:T(8,128)(2,1)S(1)}, bf16[512,1024]{1,0:T(8,128)(2,1)}, u32[]{:S(2)}) copy-start(bf16[512,1024]{1,0:T(8,128)(2,1)} %pooled.3) | copy-start | bytes 3145732
  21.5 1.0 copy-start.9
  22.5 9.2 %collective-permute-start = (bf16[1024,128]{1,0:T(8,128)(2,1)S(1)}, bf16[1024,128]{1,0:T(8,128)(2,1)S(1)}, u32[]{:S(2)}, u32[]{:S(2)}) collective-permute-start(bf16[1024,128]{1,0:T(8,128)(2,1)S(1)} %get-tuple-element.215), channel_id=1, source_target_pairs={{0,1},{1,2},{2,3},{3,0},{4,5},{5,6},{6,7},{7,4},{8,9},{9,10},{10,1... | collective-permute-start | bytes 786440 | tf_op jit(solution)/shard_map/ppermute | solution.py:27
  24.1 10.7 %collective-permute-start.1 = (bf16[1024,128]{1,0:T(8,128)(2,1)S(1)}, bf16[1024,128]{1,0:T(8,128)(2,1)S(1)}, u32[]{:S(2)}, u32[]{:S(2)}) collective-permute-start(bf16[1024,128]{1,0:T(8,128)(2,1)S(1)} %get-tuple-element.216), channel_id=1, source_target_pairs={{0,2},{1,3},{2,0},{3,1},{4,6},{5,7},{6,4},{7,5},{8,10},{9,11},{10,... | collective-permute-start | bytes 786440 | tf_op jit(solution)/shard_map/ppermute | solution.py:27
  25.0 12.9 %collective-permute-start.2 = (bf16[1024,128]{1,0:T(8,128)(2,1)S(1)}, bf16[1024,128]{1,0:T(8,128)(2,1)S(1)}, u32[]{:S(2)}, u32[]{:S(2)}) collective-permute-start(bf16[1024,128]{1,0:T(8,128)(2,1)S(1)} %get-tuple-element.217), channel_id=1, source_target_pairs={{0,3},{1,0},{2,1},{3,2},{4,7},{5,4},{6,5},{7,6},{8,11},{9,8},{10,9... | collective-permute-start | bytes 786440 | tf_op jit(solution)/shard_map/ppermute | solution.py:27
  38.0 8.7 %collective-permute-start.3 = (bf16[1024,128]{1,0:T(8,128)(2,1)S(1)}, bf16[1024,128]{1,0:T(8,128)(2,1)S(1)}, u32[]{:S(2)}, u32[]{:S(2)}) collective-permute-start(bf16[1024,128]{1,0:T(8,128)(2,1)S(1)} %add_convert_fusion), channel_id=1, source_target_pairs={{0,32},{32,64},{64,96},{96,128},{128,160},{160,192},{192,224},{224... | collective-permute-start | bytes 786440 | tf_op jit(solution)/shard_map/ppermute | solution.py:27
  39.8 7.1 %collective-permute-start.4 = (bf16[1024,128]{1,0:T(8,128)(2,1)S(1)}, bf16[1024,128]{1,0:T(8,128)(2,1)S(1)}, u32[]{:S(2)}, u32[]{:S(2)}) collective-permute-start(bf16[1024,128]{1,0:T(8,128)(2,1)S(1)} %add_convert_fusion), channel_id=1, source_target_pairs={{0,224},{32,0},{64,32},{96,64},{128,96},{160,128},{192,160},{224,1... | collective-permute-start | bytes 786440 | tf_op jit(solution)/shard_map/ppermute | solution.py:27
  41.3 1.2 copy-start.10
  46.9 16.4 %collective-permute-start.9 = (f32[4,8,16,1024]{3,2,1,0:T(8,128)S(1)}, f32[4,8,16,1024]{3,2,1,0:T(8,128)S(1)}, u32[]{:S(2)}, u32[]{:S(2)}) collective-permute-start(f32[4,8,16,1024]{3,2,1,0:T(8,128)S(1)} %get-tuple-element.253), channel_id=1, source_target_pairs={{0,4},{4,0},{1,5},{5,1},{2,6},{6,2},{3,7},{7,3},{8,12},{12,8},{9,1... | collective-permute-start | bytes 6291464 | tf_op jit(solution)/shard_map/ppermute | solution.py:27
  49.4 10.0 %collective-permute-start.5 = (bf16[1024,128]{1,0:T(8,128)(2,1)S(1)}, bf16[1024,128]{1,0:T(8,128)(2,1)S(1)}, u32[]{:S(2)}, u32[]{:S(2)}) collective-permute-start(bf16[1024,128]{1,0:T(8,128)(2,1)S(1)} %collective-permute-done.3.refs_0_), channel_id=1, source_target_pairs={{0,32},{32,64},{64,96},{96,128},{128,160},{160,192},{192,224},{224... | collective-permute-start | bytes 786440 | tf_op jit(solution)/shard_map/ppermute | solution.py:27
  51.0 9.1 %collective-permute-start.6 = (bf16[1024,128]{1,0:T(8,128)(2,1)S(1)}, bf16[1024,128]{1,0:T(8,128)(2,1)S(1)}, u32[]{:S(2)}, u32[]{:S(2)}) collective-permute-start(bf16[1024,128]{1,0:T(8,128)(2,1)S(1)} %collective-permute-done.4.refs_1_), channel_id=1, source_target_pairs={{0,224},{32,0},{64,32},{96,64},{128,96},{160,128},{192,160},{224,1... | collective-permute-start | bytes 786440 | tf_op jit(solution)/shard_map/ppermute | solution.py:27
  60.1 11.6 %collective-permute-start.7 = (bf16[1024,128]{1,0:T(8,128)(2,1)S(1)}, bf16[1024,128]{1,0:T(8,128)(2,1)S(1)}, u32[]{:S(2)}, u32[]{:S(2)}) collective-permute-start(bf16[1024,128]{1,0:T(8,128)(2,1)S(1)} %collective-permute-done.5.refs_0_), channel_id=1, source_target_pairs={{0,32},{32,64},{64,96},{96,128},{128,160},{160,192},{192,224},{224... | collective-permute-start | bytes 786440 | tf_op jit(solution)/shard_map/ppermute | solution.py:27
  63.0 8.7 %collective-permute-start.8 = (bf16[1024,128]{1,0:T(8,128)(2,1)S(1)}, bf16[1024,128]{1,0:T(8,128)(2,1)S(1)}, u32[]{:S(2)}, u32[]{:S(2)}) collective-permute-start(bf16[1024,128]{1,0:T(8,128)(2,1)S(1)} %collective-permute-done.6.refs_1_), channel_id=1, source_target_pairs={{0,224},{32,0},{64,32},{96,64},{128,96},{160,128},{192,160},{224,1... | collective-permute-start | bytes 786440 | tf_op jit(solution)/shard_map/ppermute | solution.py:27
  64.2 14.5 %collective-permute-start.12 = (bf16[8,16,1024]{2,1,0:T(8,128)(2,1)S(1)}, bf16[8,16,1024]{2,1,0:T(8,128)(2,1)S(1)}, u32[]{:S(2)}, u32[]{:S(2)}) collective-permute-start(bf16[8,16,1024]{2,1,0:T(8,128)(2,1)S(1)} %get-tuple-element.292), channel_id=1, source_target_pairs={{0,8},{8,16},{16,24},{24,0},{1,9},{9,17},{17,25},{25,1},{2,10},{10... | collective-permute-start | bytes 786440 | tf_op jit(solution)/shard_map/ppermute | solution.py:27
  65.7 13.7 %collective-permute-start.13 = (bf16[8,16,1024]{2,1,0:T(8,128)(2,1)S(1)}, bf16[8,16,1024]{2,1,0:T(8,128)(2,1)S(1)}, u32[]{:S(2)}, u32[]{:S(2)}) collective-permute-start(bf16[8,16,1024]{2,1,0:T(8,128)(2,1)S(1)} %get-tuple-element.293), channel_id=1, source_target_pairs={{0,16},{8,24},{16,0},{24,8},{1,17},{9,25},{17,1},{25,9},{2,18},{10... | collective-permute-start | bytes 786440 | tf_op jit(solution)/shard_map/ppermute | solution.py:27
  68.5 11.0 %collective-permute-start.14 = (bf16[8,16,1024]{2,1,0:T(8,128)(2,1)S(1)}, bf16[8,16,1024]{2,1,0:T(8,128)(2,1)S(1)}, u32[]{:S(2)}, u32[]{:S(2)}) collective-permute-start(bf16[8,16,1024]{2,1,0:T(8,128)(2,1)S(1)} %get-tuple-element.294), channel_id=1, source_target_pairs={{0,24},{8,0},{16,8},{24,16},{1,25},{9,1},{17,9},{25,17},{2,26},{10... | collective-permute-start | bytes 786440 | tf_op jit(solution)/shard_map/ppermute | solution.py:27
  71.7 7.0 %collective-permute-start.10 = (bf16[512,128]{1,0:T(8,128)(2,1)S(1)}, bf16[512,128]{1,0:T(8,128)(2,1)S(1)}, u32[]{:S(2)}, u32[]{:S(2)}) collective-permute-start(bf16[512,128]{1,0:T(8,128)(2,1)S(1)} %slice.33), channel_id=1, source_target_pairs={{0,32},{32,64},{64,96},{96,128},{128,160},{160,192},{192,224},{224... | collective-permute-start | bytes 393224 | tf_op jit(solution)/shard_map/ppermute | solution.py:27
  73.5 5.2 %collective-permute-start.11 = (bf16[512,128]{1,0:T(8,128)(2,1)S(1)}, bf16[512,128]{1,0:T(8,128)(2,1)S(1)}, u32[]{:S(2)}, u32[]{:S(2)}) collective-permute-start(bf16[512,128]{1,0:T(8,128)(2,1)S(1)} %slice.34), channel_id=1, source_target_pairs={{0,224},{32,0},{64,32},{96,64},{128,96},{160,128},{192,160},{224,1... | collective-permute-start | bytes 393224 | tf_op jit(solution)/shard_map/ppermute | solution.py:27
  82.9 3.9 %collective-permute-start.15 = (bf16[4,256,512]{2,1,0:T(8,128)(2,1)S(1)}, bf16[4,256,512]{2,1,0:T(8,128)(2,1)S(1)}, u32[]{:S(2)}, u32[]{:S(2)}) collective-permute-start(bf16[4,256,512]{2,1,0:T(8,128)(2,1)S(1)} %send0.1), channel_id=1, source_target_pairs={{0,4},{4,0},{1,5},{5,1},{2,6},{6,2},{3,7},{7,3},{8,12},{12,8},{9,1... | collective-permute-start | bytes 3145736 | tf_op jit(solution)/shard_map/ppermute | solution.py:27
  85.5 4.7 %collective-permute-start.16 = (bf16[4,256,512]{2,1,0:T(8,128)(2,1)S(1)}, bf16[4,256,512]{2,1,0:T(8,128)(2,1)S(1)}, u32[]{:S(2)}, u32[]{:S(2)}) collective-permute-start(bf16[4,256,512]{2,1,0:T(8,128)(2,1)S(1)} %send1.1), channel_id=1, source_target_pairs={{0,4},{4,0},{1,5},{5,1},{2,6},{6,2},{3,7},{7,3},{8,12},{12,8},{9,1... | collective-permute-start | bytes 3145736 | tf_op jit(solution)/shard_map/ppermute | solution.py:27
  90.2 14.9 %copy-start.11 = (s32[1,1,2048]{2,1,0:T(1,128)S(1)}, s32[1,1,2048]{2,1,0:T(1,128)}, u32[]{:S(2)}) copy-start(s32[1,1,2048]{2,1,0:T(1,128)} %param.20) | copy-start | bytes 24580
  93.5 22.2 %copy-start.12 = (s32[1,1,256]{2,1,0:T(1,128)S(1)}, s32[1,1,256]{2,1,0:T(1,128)}, u32[]{:S(2)}) copy-start(s32[1,1,256]{2,1,0:T(1,128)} %param.24) | copy-start | bytes 3076
  93.5 22.4 %copy-start = (f32[1,1,2048,128]{3,2,1,0:T(8,128)S(1)}, f32[1,1,2048,128]{3,2,1,0:T(8,128)}, u32[]{:S(2)}) copy-start(f32[1,1,2048,128]{3,2,1,0:T(8,128)} %param.21) | copy-start | bytes 3145732
  93.5 22.4 %copy-start.2 = (f32[1,1,2048]{2,1,0:T(1,128)S(1)}, f32[1,1,2048]{2,1,0:T(1,128)}, u32[]{:S(2)}) copy-start(f32[1,1,2048]{2,1,0:T(1,128)} %param.22) | copy-start | bytes 24580
  93.5 22.4 %copy-start.4 = (s32[1,1,256]{2,1,0:T(1,128)S(1)}, s32[1,1,256]{2,1,0:T(1,128)}, u32[]{:S(2)}) copy-start(s32[1,1,256]{2,1,0:T(1,128)} %param.23) | copy-start | bytes 3076
  93.5 11.1 %collective-permute-start.17 = (bf16[256,512]{1,0:T(8,128)(2,1)S(1)}, bf16[256,512]{1,0:T(8,128)(2,1)S(1)}, u32[]{:S(2)}, u32[]{:S(2)}) collective-permute-start(bf16[256,512]{1,0:T(8,128)(2,1)S(1)} %get-tuple-element.381), channel_id=1, source_target_pairs={{0,8},{8,16},{16,24},{24,0},{1,9},{9,17},{17,25},{25,1},{2,10},{10... | collective-permute-start | bytes 786440 | tf_op jit(solution)/shard_map/ppermute | solution.py:27
  95.2 22.4 %collective-permute-start.21 = (bf16[256,512]{1,0:T(8,128)(2,1)}, bf16[256,512]{1,0:T(8,128)(2,1)S(1)}, u32[]{:S(2)}, u32[]{:S(2)}) collective-permute-start(bf16[256,512]{1,0:T(8,128)(2,1)} %get-tuple-element.396), channel_id=1, source_target_pairs={{0,16},{8,24},{16,0},{24,8},{1,17},{9,25},{17,1},{25,9},{2,18},{10... | collective-permute-start | bytes 786440 | tf_op jit(solution)/shard_map/ppermute | solution.py:27
  97.7 19.9 %collective-permute-start.22 = (bf16[256,512]{1,0:T(8,128)(2,1)}, bf16[256,512]{1,0:T(8,128)(2,1)}, u32[]{:S(2)}, u32[]{:S(2)}) collective-permute-start(bf16[256,512]{1,0:T(8,128)(2,1)} %get-tuple-element.397), channel_id=1, source_target_pairs={{0,24},{8,0},{16,8},{24,16},{1,25},{9,1},{17,9},{25,17},{2,26},{10... | collective-permute-start | bytes 786440 | tf_op jit(solution)/shard_map/ppermute | solution.py:27
  99.1 18.4 %collective-permute-start.18 = (bf16[256,512]{1,0:T(8,128)(2,1)}, bf16[256,512]{1,0:T(8,128)(2,1)}, u32[]{:S(2)}, u32[]{:S(2)}) collective-permute-start(bf16[256,512]{1,0:T(8,128)(2,1)} %get-tuple-element.391), channel_id=1, source_target_pairs={{0,8},{8,16},{16,24},{24,0},{1,9},{9,17},{17,25},{25,1},{2,10},{10... | collective-permute-start | bytes 786440 | tf_op jit(solution)/shard_map/ppermute | solution.py:27
  99.7 20.9 %collective-permute-start.19 = (bf16[256,512]{1,0:T(8,128)(2,1)}, bf16[256,512]{1,0:T(8,128)(2,1)}, u32[]{:S(2)}, u32[]{:S(2)}) collective-permute-start(bf16[256,512]{1,0:T(8,128)(2,1)} %get-tuple-element.392), channel_id=1, source_target_pairs={{0,16},{8,24},{16,0},{24,8},{1,17},{9,25},{17,1},{25,9},{2,18},{10... | collective-permute-start | bytes 786440 | tf_op jit(solution)/shard_map/ppermute | solution.py:27
  104.7 16.5 %collective-permute-start.20 = (bf16[256,512]{1,0:T(8,128)(2,1)}, bf16[256,512]{1,0:T(8,128)(2,1)}, u32[]{:S(2)}, u32[]{:S(2)}) collective-permute-start(bf16[256,512]{1,0:T(8,128)(2,1)} %get-tuple-element.393), channel_id=1, source_target_pairs={{0,24},{8,0},{16,8},{24,16},{1,25},{9,1},{17,9},{25,17},{2,26},{10... | collective-permute-start | bytes 786440 | tf_op jit(solution)/shard_map/ppermute | solution.py:27
  106.3 30.0 %all-to-all-start.1 = ((bf16[8,16,1024]{2,1,0:T(8,128)(2,1)}), bf16[8,16,1024]{2,1,0:T(8,128)(2,1)S(1)}, u32[]{:S(2)}, u32[]{:S(2)}) async-start(bf16[8,16,1024]{2,1,0:T(8,128)(2,1)} %convert_element_type.84), calls=%async_computation.1 | async-start | bytes 524288 | tf_op jit(solution)/shard_map/all_to_all | solution.py:481
  124.5 10.5 %collective-permute-start.23 = (f32[136,128]{1,0:T(8,128)S(1)}, f32[136,128]{1,0:T(8,128)S(1)}, u32[]{:S(2)}, u32[]{:S(2)}) collective-permute-start(f32[136,128]{1,0:T(8,128)S(1)} %get-tuple-element.418), channel_id=1, source_target_pairs={{0,1},{1,2},{2,3},{3,0},{4,5},{5,6},{6,7},{7,4},{8,9},{9,10},{10,1... | collective-permute-start | bytes 208904 | tf_op jit(solution)/shard_map/ppermute | solution.py:27
  125.3 9.7 %collective-permute-start.24 = (f32[136,128]{1,0:T(8,128)S(1)}, f32[136,128]{1,0:T(8,128)S(1)}, u32[]{:S(2)}, u32[]{:S(2)}) collective-permute-start(f32[136,128]{1,0:T(8,128)S(1)} %get-tuple-element.419), channel_id=1, source_target_pairs={{0,2},{1,3},{2,0},{3,1},{4,6},{5,7},{6,4},{7,5},{8,10},{9,11},{10,... | collective-permute-start | bytes 208904 | tf_op jit(solution)/shard_map/ppermute | solution.py:27
  127.2 7.9 %collective-permute-start.25 = (f32[136,128]{1,0:T(8,128)S(1)}, f32[136,128]{1,0:T(8,128)S(1)}, u32[]{:S(2)}, u32[]{:S(2)}) collective-permute-start(f32[136,128]{1,0:T(8,128)S(1)} %get-tuple-element.420), channel_id=1, source_target_pairs={{0,3},{1,0},{2,1},{3,2},{4,7},{5,4},{6,5},{7,6},{8,11},{9,8},{10,9... | collective-permute-start | bytes 208904 | tf_op jit(solution)/shard_map/ppermute | solution.py:27

commit v2 on v1

--- a/solution.py
+++ b/solution.py
@@ -70,76 +70,84 @@
             ref[t * bags : (t + 1) * bags, :] = feature[k, :, t * 128 : (t + 1) * 128].astype(ref.dtype)
 
 
-def code_kernel(pos, owner, value, lens, out):
-    x, c = pos[1], pos[2]
+def field_kernel(owner, row, weight, lens, out, earlier_out):
     tables, bag, bags = owner.shape
+    for t in range(tables):
+        slot = lax.broadcasted_iota(I32, (bag, bags), 0)
+        used = jnp.where(slot < lens[t : t + 1, :], owner[t], 64)
+        fields = [used, lax.shift_right_logical(row[t], 2), row[t] & 3]
+        fields = [f.astype(F32) for f in fields] + [weight[t].astype(F32)]
+        fields = jnp.concatenate(fields, axis=0).astype(BF16)
+        for q in range(4):
+            out[t, q * 32 : (q + 1) * 32, :] = fields[:, q * 128 : (q + 1) * 128]
+    shape = earlier_out.shape
+    earlier = lax.broadcasted_iota(I32, shape, 0) < lax.broadcasted_iota(I32, shape, 1)
+    earlier_out[...] = jnp.where(earlier, 1.0, 0.0).astype(BF16)
+
+
+def own_kernel(own, one, two, three, fields, out):
+    bags, lines = own.shape[0] // 2, fields.shape[1]
+    for t in range(2):
+        at = slice(t * bags, (t + 1) * bags)
+        total = own[at, :] + one[at, :].astype(F32) + two[at, :].astype(F32) + three[at, :].astype(F32)
+        first = t * (bags + lines)
+        out[first : first + bags, :] = total.astype(BF16)
+        out[first + bags : first + bags + lines, :] = fields[t]
+
+
+STEPS = (1, 2, 2, 2, 1)
+
+
+def pick_kernel(count, pos, earlier, *refs):
+    blocks = 2 if count == 2 or len(refs) == 19 else 1
+    msgs, refs = refs[:blocks], refs[blocks:]
+    outs, (bag_all, dense, ranks, picks, rhs) = refs[:12], refs[12:]
+    bags = bag_all.shape[2]
+    units = 2 * count
+    lines = 128
+    z, x, c = pos[0], pos[1], pos[2]
     j = lax.broadcasted_iota(I32, (8, bags), 0)
-    there = 2 * ((x + j) & 3) + ((c + (j >> 2)) & 1)
-    for t in range(tables):
-        used = [jnp.where(l < lens[t : t + 1, :], owner[t, l : l + 1, :], -1) for l in range(bag)]
-        vals = [value[t, l : l + 1, :] for l in range(bag)]
-        for k in range(out.shape[0]):
-            ids = there + k * 8
-            total = jnp.zeros((8, bags), I32)
-            for l in range(bag):
-                total = total + jnp.where(used[l] == ids, vals[l], 0)
-            out[k, 8 * t : 8 * t + 8, :] = total
-
-
-STEPS = (1, 2, 2, 2, 1)
-
-
-def prep_kernel(order, pos, codes, *refs):
-    ranks, sides, code_all, rank_all = refs[:5], refs[5:10], refs[10], refs[11]
-    bags = code_all.shape[1]
-    for s in range(8):
-        code_all[16 * s : 16 * s + 16, :] = codes[lax.rem(pos[0] + 8 - order[s], 8)]
-    earlier = (
-        lax.broadcasted_iota(I32, (bags, bags), 0) < lax.broadcasted_iota(I32, (bags, bags), 1)
-    )
-    earlier = jnp.where(earlier, 1.0, 0.0).astype(BF16)
-    present = code_all[...] > 0
-    rank = jnp.dot(jnp.where(present, 1.0, 0.0).astype(BF16), earlier, preferred_element_type=F32)
-    rank_all[...] = jnp.where(present, rank, 255.0)
-    first = 0
-    for step, count in enumerate(STEPS):
-
-        def unit(i, carry):
-            at = pl.ds(pl.multiple_of((first + i) * 8, 8), 8)
-            code = code_all[at, :]
-            ranks[step][i] = rank_all[at, :]
-            row = lax.shift_right_logical(code, 11)
-            fields = [
-                lax.shift_right_logical(row, 2).astype(F32),
-                (code & 2047).astype(F32) * (1.0 / 512.0),
-                (row & 3).astype(F32),
-                jnp.zeros((128 - 24, bags), F32),
-            ]
-            sides[step][i] = jnp.concatenate(fields, axis=0).T.astype(BF16)
-            return carry
-
-        lax.fori_loop(0, 2 * count, unit, 0)
-        first += 2 * count
-
-
-def pick_kernel(count, ranks, sides, *refs):
-    blocks, refs = refs[:2], refs[2:]
-    outs, bag_all, picks, rhs = refs[:12], refs[12], refs[13], refs[14]
-    bags = bag_all.shape[2]
-    if count == 1:
+    ids = (z * 8 + 2 * ((x + j) & 3) + ((c + (j >> 2)) & 1)).astype(F32)
+    for s in range(count):
         for t in range(2):
-            bag_all[0, t] = blocks[t][...]
-    else:
-        for s in range(2):
-            for t in range(2):
-                bag_all[s, t] = blocks[s][t * bags : (t + 1) * bags, :]
+            if count == 2:
+                ref, first = msgs[s], t * (bags + lines)
+            elif blocks == 2:
+                ref, first = msgs[t], 0
+            else:
+                ref, first = msgs[0], t * (bags + lines)
+            bag_all[s, t] = ref[first : first + bags, :]
+            first += bags
+            fields = jnp.concatenate(
+                [ref[first + q * 32 : first + (q + 1) * 32, :].astype(F32) for q in range(4)], axis=1
+            )
+            high = jnp.zeros((8, bags), F32)
+            low, weight = high, high
+            for l in range(8):
+                mine = fields[l : l + 1] == ids
+                high = high + jnp.where(mine, fields[8 + l : 9 + l], 0.0)
+                low = low + jnp.where(mine, fields[16 + l : 17 + l], 0.0)
+                weight = weight + jnp.where(mine, fields[24 + l : 25 + l], 0.0)
+            u = 2 * s + t
+            dense[u, 0:8] = high
+            dense[u, 8:16] = weight
+            dense[u, 16:24] = low
+    present = jnp.concatenate([dense[u, 8:16] for u in range(units)], axis=0) > 0.0
+    rank = jnp.dot(
+        jnp.where(present, 1.0, 0.0).astype(BF16), earlier[...], preferred_element_type=F32
+    )
+    rank = jnp.where(present, rank, 255.0)
+    for u in range(units):
+        ranks[u] = rank[8 * u : 8 * u + 8]
     place = lax.broadcasted_iota(I32, (MOST, bags), 0).astype(F32).astype(BF16)
 
     def source(s, carry):
         for t in range(2):
+            u = 2 * s + t
             rhs[t, :, :128] = bag_all[s, t]
-            rhs[t, :, 128:] = sides[2 * s + t]
-            rank = ranks[2 * s + t].astype(BF16)
+            moved = jnp.concatenate([dense[u], jnp.zeros((128 - 24, bags), F32)], axis=0)
+            rhs[t, :, 128:] = moved.T.astype(BF16)
+            rank = ranks[u].astype(BF16)
             for o in range(8):
                 line = jnp.broadcast_to(rank[o : o + 1, :], (MOST, bags))
                 picks[t, o * MOST : (o + 1) * MOST, :] = jnp.where(
@@ -196,17 +204,18 @@
     lax.fori_loop(0, 4, one, 0)
 
 
-def keep_kernel(other, *refs):
-    steps = [refs[3 * i : 3 * i + 3] for i in range(5)]
-    outs, onto, both, total = refs[15:19], refs[19], refs[20], refs[21]
-
-    def one(k, carry):
-        total[k] = spread_one(k, steps, onto, both) + other[k].astype(F32)
-        return carry
-
-    lax.fori_loop(0, 4, one, 0)
-    for k in range(4):
-        outs[k][...] = total[k].astype(outs[k].dtype)
+def keep_kernel(other0, other1, *refs):
+    outs, onto, both, total = refs[30:34], refs[34], refs[35], refs[36]
+    for t, other in enumerate((other0, other1)):
+        steps = [refs[15 * t + 3 * i : 15 * t + 3 * i + 3] for i in range(5)]
+
+        def one(k, carry):
+            total[k] = spread_one(k, steps, onto, both) + other[k].astype(F32)
+            return carry
+
+        lax.fori_loop(0, 4, one, 0)
+        for k in range(4):
+            outs[k][t * 256 : (t + 1) * 256, :] = total[k].astype(outs[k].dtype)
 
 
 def grad_kernel(pos, pooled, delta, keep, send, half):
@@ -258,11 +267,12 @@
 
 
 def evict_kernel(slot_map, slot_in, weight, accum, *refs):
-    parts, rhs, held, pick = refs[:8], refs[8], refs[9:13], refs[13]
+    parts, rhs, held, pick, sums = refs[:4], refs[4], refs[5:9], refs[9], refs[10]
     for t in range(2):
-        own = parts[4 * t][...]
+        at = slice(t * 256, (t + 1) * 256)
+        own = parts[0][at, :]
         for k in range(1, 4):
-            own = own + parts[4 * t + k][...].astype(F32)
+            own = own + parts[k][at, :].astype(F32)
         high = own.astype(BF16)
         low = (own - high.astype(F32)).astype(BF16)
         for l in range(4):
@@ -270,47 +280,37 @@
             rhs[at : at + 256, :128] = high[:, l * 128 : (l + 1) * 128]
             rhs[at : at + 256, 128:] = low[:, l * 128 : (l + 1) * 128]
     eye = square()
-
-    def block(k, carry):
-        at = pl.ds(pl.multiple_of(k * 128, 128), 128)
-        slots = slot_in[at, :]
-        for i in range(16):
-            lane = slice(i * 128, (i + 1) * 128)
-            pick[:, lane] = jnp.where(slots == slot_map[:, lane], 1.0, 0.0).astype(BF16)
-        both = jnp.dot(pick[...], rhs[...], preferred_element_type=F32)
-        g = both[:, :128] + both[:, 128:]
+    for i in range(16):
+        lane = slice(i * 128, (i + 1) * 128)
+        pick[:, lane] = jnp.where(slot_in[:512, :] == slot_map[:, lane], 1.0, 0.0).astype(BF16)
+    sums[...] = jnp.dot(pick[...], rhs[...], preferred_element_type=F32)
+    for i in range(4):
+        at = slice(i * 128, (i + 1) * 128)
+        g = sums[at, :128] + sums[at, 128:]
         acc = accum[at, :] + jnp.sum(g * g, axis=1, keepdims=True) * (1.0 / 128.0)
-        row = weight[at, :] - LEARN_RATE * g / (jnp.sqrt(acc) + EPSILON)
+        held[i][:128, :] = weight[at, :] - LEARN_RATE * g / (jnp.sqrt(acc) + EPSILON)
         line = jnp.sum(jnp.where(eye, acc, 0.0), axis=0, keepdims=True)
-        for i in range(4):
-
-            @pl.when(k == i)
-            def _():
-                held[i][:128, :] = row
-                held[i][128:, :] = jnp.broadcast_to(line, (HELD - 128, 128))
-
-        return carry
-
-    lax.fori_loop(0, 4, block, 0)
-
-
-def update_kernel(slot_map, rhs, weight, accum, new_weight, new_accum):
+        held[i][128:, :] = jnp.broadcast_to(line, (HELD - 128, 128))
+
+
+def update_kernel(slot_map, rhs, weight, accum, new_weight, new_accum, pick, sums):
     eye = square()
-    step = 256
-    ids = lax.broadcasted_iota(I32, (step, 2048), 0).astype(F32).astype(BF16)
+    step, part = 512, 256
+    ids = lax.broadcasted_iota(I32, (part, 2048), 0).astype(F32).astype(BF16)
     slot_row = slot_map[...]
 
     def chunk(i, carry):
         at = pl.multiple_of(i * step, step)
-        near = slot_row - at.astype(F32)
-        near = jnp.where((near >= 0.0) & (near < step), near, 2.0 * step).astype(BF16)
-        pick = jnp.where(
-            jnp.broadcast_to(near, (step, 2048)) == ids, jnp.ones((), BF16), jnp.zeros((), BF16)
-        )
-        both = jnp.dot(pick, rhs[...], preferred_element_type=F32)
-        grad = both[:, :128] + both[:, 128:]
+        for j in range(step // part):
+            near = slot_row - (at + j * part).astype(F32)
+            near = jnp.where((near >= 0.0) & (near < part), near, 2.0 * part).astype(BF16)
+            pick[j * part : (j + 1) * part, :] = jnp.where(
+                jnp.broadcast_to(near, (part, 2048)) == ids, jnp.ones((), BF16), jnp.zeros((), BF16)
+            )
+        sums[...] = jnp.dot(pick[...], rhs[...], preferred_element_type=F32)
         for j in range(step // 128):
-            g = grad[j * 128 : (j + 1) * 128]
+            part_at = slice(j * 128, (j + 1) * 128)
+            g = sums[part_at, :128] + sums[part_at, 128:]
             b = i * (step // 128) + j
             kept = jnp.sum(jnp.where(eye, accum[pl.ds(b, 1), :], 0.0), axis=1, keepdims=True)
             acc = kept + jnp.sum(g * g, axis=1, keepdims=True) * (1.0 / 128.0)
@@ -371,26 +371,21 @@
     )(pos, pooled, w_up, grad_out)
     got = [shifted(parts[k], H, k) for k in (1, 2, 3)]
 
-    value = rows * 2048 + (lookup_weight.astype(F32) * 512.0).astype(I32)
-    (codes,) = call(
-        code_kernel, [SMEM, VMEM, VMEM, VMEM], [shape((8, 16, bags), I32)], [], 1 << 22, 1 << 20, "codes"
-    )(pos, jnp.swapaxes(owners, 1, 2), jnp.swapaxes(value, 1, 2), lens)
-    codes = lax.all_to_all(codes, Z, split_axis=0, concat_axis=0, tiled=True)
-
-    got, (codes,) = together(got, (codes,))
-    own = parts[0] + got[0].astype(F32) + got[1].astype(F32) + got[2].astype(F32)
-    own = own.astype(BF16)
-    order = (0, 1, 7, 2, 6, 3, 5, 4)
-    units = [2 * n for n in STEPS]
-    prep = call(
-        functools.partial(prep_kernel, order),
-        [SMEM, VMEM],
-        [shape((n, 8, bags), F32) for n in units] + [shape((n, bags, 128), BF16) for n in units],
-        [pltpu.VMEM((128, bags), I32), pltpu.VMEM((128, bags), F32)],
-        1 << 26,
-        3 << 20,
-        "prep",
-    )(pos, codes)
+    (delta,), (owners, rows, lookup_weight, lens) = together(
+        (delta,), (owners, rows, lookup_weight, lens)
+    )
+    fields, earlier = call(
+        field_kernel,
+        [VMEM] * 4,
+        [shape((2, 128, 128), BF16), shape((bags, bags), BF16)],
+        [],
+        1 << 20,
+        1 << 20,
+        "fields",
+    )(*[jnp.swapaxes(a, 1, 2) for a in (owners, rows, lookup_weight)], lens)
+    (own,) = call(
+        own_kernel, [VMEM] * 5, [shape((2 * (bags + 128), 128), BF16)], [], 1 << 20, 2 << 20, "own"
+    )(parts[0], *got, fields)
 
     def pick(step, blocks):
         count = STEPS[step]
@@ -401,17 +396,19 @@
         ] * 4
         return call(
             functools.partial(pick_kernel, count),
-            [VMEM] * 4,
+            [SMEM, VMEM] + [VMEM] * len(blocks),
             outs,
             [
                 pltpu.VMEM((count, 2, bags, 128), BF16),
+                pltpu.VMEM((2 * count, 24, bags), F32),
+                pltpu.VMEM((2 * count, 8, bags), F32),
                 pltpu.VMEM((2, 8 * MOST, bags), BF16),
                 pltpu.VMEM((2, bags, 256), BF16),
             ],
             1 << 30,
             4 << 20,
             f"pick{step}",
-        )(prep[step], prep[5 + step], *blocks)
+        )(pos, earlier, *blocks)
 
     up, down = shifted(own, Z, 1), shifted(own, Z, -1)
     (delta,), (own,) = together((delta,), (own,))
@@ -428,7 +425,7 @@
     (up, down), (grad, there) = together((up, down), (grad, there))
     there = shifted(there, C, 1)
     up, down = shifted(up, Z, 1), shifted(down, Z, -1)
-    picked = [pick(0, (own[:bags], own[bags:]))]
+    picked = [pick(0, (own,))]
     mid = (up, down)
     (up, down), near, *picked = together((up, down), near, *picked)
     up, down = shifted(up, Z, 1), shifted(down, Z, -1)
@@ -439,7 +436,8 @@
     picked.append(pick(1, near))
     far = (up, down)
     (up, down), mid, picked[1] = together((up, down), mid, picked[1])
-    last = (shifted(up[:bags], Z, 1), shifted(down[bags:], Z, -1))
+    part = bags + 128
+    last = (shifted(up[:part], Z, 1), shifted(down[part:], Z, -1))
     picked.append(pick(2, mid))
     far, picked[2] = together(far, picked[2])
     picked.append(pick(3, far))
@@ -457,27 +455,23 @@
         )(*half(t, 1))
         others.append(out)
     others = [shifted(out, C, 1) for out in others]
-    arrived = []
-    for t in range(2):
-        outs = call(
-            keep_kernel,
-            [VMEM] * 16,
-            [shape((256, 512), F32)] + [shape((256, 512), BF16)] * 3,
-            work + [pltpu.VMEM((4, 256, 512), F32)],
-            4 << 30,
-            5 << 20,
-            f"keep{t}",
-        )(others[t], *half(t, 0))
-        if t == 0:
-            outs, (others[1],) = together(outs, (others[1],))
-        arrived += [outs[0]] + [shifted(outs[k], X, k) for k in (1, 2, 3)]
+    outs = call(
+        keep_kernel,
+        [VMEM] * 32,
+        [shape((512, 512), F32)] + [shape((512, 512), BF16)] * 3,
+        work + [pltpu.VMEM((4, 256, 512), F32)],
+        8 << 30,
+        10 << 20,
+        "keep",
+    )(*others, *half(0, 0), *half(1, 0))
+    arrived = [outs[0]] + [shifted(outs[k], X, k) for k in (1, 2, 3)]
 
     for block in got_x:
         total = total + block.astype(F32)
     first, total, slot_map, evict_slots, evict_dest = lax.optimization_barrier(
-        (arrived[5], total, slot_map, evict_slots, evict_dest)
-    )
-    arrived[5] = first
+        (arrived[0], total, slot_map, evict_slots, evict_dest)
+    )
+    arrived[0] = first
     blocks = lax.all_to_all(total.astype(BF16), Z, split_axis=0, concat_axis=0, tiled=True)
     (grad_up,) = call(
         finish_kernel,
@@ -512,9 +506,9 @@
     arrived, leaving = together(arrived, leaving)
     rhs, *held = call(
         evict_kernel,
-        [VMEM] * 12,
+        [VMEM] * 8,
         [shape((2048, 256), BF16)] + [shape((HELD, 128), F32)] * 4,
-        [pltpu.VMEM((128, 2048), BF16)],
+        [pltpu.VMEM((512, 2048), BF16), pltpu.VMEM((512, 256), F32)],
         1 << 29,
         4 << 20,
         "evict",
@@ -524,7 +518,7 @@
         update_kernel,
         [VMEM] * 4,
         [shape((2048, 128), F32), shape((16, 128), F32)],
-        [],
+        [pltpu.VMEM((512, 2048), BF16), pltpu.VMEM((512, 256), F32)],
         2 << 30,
         4 << 20,
         "update",

time: 138 us -> 133 us (0.964)
  starting transfers between devices: 55.2 us -> 41.4 us
  waiting for transfers between devices: 27 us -> 35.1 us
  local copies, waits for them, and re-layouts: 8.23 us -> 11.2 us
    all_to_all x1 -> x0, starting transfers between devices: 8.47 us -> none  [on_device(): codes = lax.all_to_all(codes, Z, split_axis=0, concat_axis=0, tiled=True)]
    all_to_all x1, waiting for transfers between devices: 0.01 us -> 5.29 us  [on_device(): lax.all_to_all(total.astype(BF16), Z, split_axis=0, concat_axis=0, tiled=...]
    all_to_all x1, starting transfers between devices: 9.39 us -> 4.61 us  [on_device(): lax.all_to_all(total.astype(BF16), Z, split_axis=0, concat_axis=0, tiled=...]
    ppermute x26 -> x23, waiting for transfers between devices: 27 us -> 29.8 us  [shifted(): return lax.ppermute(x, axis, [(i, (i + step) % size) for i in range(size)])]
    convert_element_type x3, local copies, waits for them, and re-layouts: 0.39 us -> 2.05 us  [on_device(): jnp.swapaxes(slot_map.reshape(2, 256, 4), 1, 2).reshape(1, 2048).astype(F32)]
    unnamed x26 -> x38, local copies, waits for them, and re-layouts: 7.69 us -> 9.05 us
    ppermute x26 -> x23, starting transfers between devices: 37.4 us -> 36.8 us  [shifted(): return lax.ppermute(x, axis, [(i, (i + step) % size) for i in range(size)])]
    pallas_call x10 -> x9, Pallas kernels: 21.3 us -> 21.1 us  [the longest x5 11.9 us: pick(): call(functools.partial(pick_kernel, count), [SMEM, VMEM] + [VMEM] * len(b...]
  transfers between devices with their start and end apart: 28 -> 24, of which waited for: 11 -> 10; matrix products, arithmetic and copies ran while one was open for 2% -> 3% of each run, Pallas kernels for 24% -> 15%
where the time goes in v2:
time: 133 us
  Pallas kernels  41.4 us (31%)
  starting transfers between devices  41.4 us (31%)
  waiting for transfers between devices  35.1 us (26%)
  local copies, waits for them, and re-layouts  11.2 us (8%)
  other arithmetic  1.72 us (1%)
  between operations  1.59 us (1%)
    ppermute x23, starting transfers between devices, shifted(): return lax.ppermute(x, axis, [(i, (i + step) % size) for i in range(size)])  36.8 us
    ppermute x23, waiting for transfers between devices, shifted(): return lax.ppermute(x, axis, [(i, (i + step) % size) for i in range(size)])  29.8 us
    pallas_call x5, Pallas kernels, pick(): call(functools.partial(pick_kernel, count), [SMEM, VMEM] + [VMEM] * len(b...  11.9 us
    unnamed x38, local copies, waits for them, and re-layouts  9.05 us
    pallas_call x1, Pallas kernels, on_device(): call(keep_kernel, [VMEM] * 32, [shape((512, 512), F32)] + [shape((512, 51...  6.36 us
    all_to_all x1, waiting for transfers between devices, on_device(): lax.all_to_all(total.astype(BF16), Z, split_axis=0, concat_axis=0, tiled=...  5.29 us
    pallas_call x2, Pallas kernels, on_device(): call(send_kernel, [VMEM] * 15, [shape((4, 256, 512), BF16)], work, 4 << 3...  5.06 us
    all_to_all x1, starting transfers between devices, on_device(): lax.all_to_all(total.astype(BF16), Z, split_axis=0, concat_axis=0, tiled=...  4.61 us
  transfers between devices with their start and end apart: 24, of which 10 were waited for; matrix products, arithmetic and copies ran while one was open for 3% of the time, Pallas kernels for 15%

profile of v2, /device:TPU:8, one launch (start us, length us, event | category | flops | bytes accessed | tf_op | source)
XLA Modules:
  0.0 132.7 jit_solution(14872330093194347985)
XLA Ops:
  0.7 1.6 %copy-done.13 = bf16[1024,1024]{1,0:T(8,128)(2,1)S(1)} copy-done((bf16[1024,1024]{1,0:T(8,128)(2,1)S(1)}, bf16[1024,1024]{1,0:T(8,128)(2,1)}, u32[]{:S(2)}) %copy-start.13) | copy-done | bytes 2097176
  2.3 1.2 copy-done.14
  3.5 1.2 copy-done.15
  4.8 4.5 %top.1 = (bf16[512,1024]{1,0:T(8,128)(2,1)S(1)}, f32[1024,128]{1,0:T(8,128)S(1)}, bf16[1024,128]{1,0:T(8,128)(2,1)S(1)}, bf16[1024,128]{1,0:T(8,128)(2,1)S(1)}, bf16[1024,128]{1,0:T(8,128)(2,1)S(1)}) custom-call(s32[4]{0:T(128)S(1)} %pad_add_fusion.pos, bf16[512,1024]{1,0:T(8,128)(2,1)S(1)} %copy-done.15, bf16[1024,1024]{1,0:T(8,128)(2,1)S(1)} %copy-done.13, ...), custom_call_target="tpu_custom_call" | custom-call | flops 2147483648 | bytes 6291456 | tf_op jit(solution)/shard_map/top/pallas_call | solution.py:363
  9.3 1.6 %collective-permute-start = (bf16[1024,128]{1,0:T(8,128)(2,1)S(1)}, bf16[1024,128]{1,0:T(8,128)(2,1)S(1)}, u32[]{:S(2)}, u32[]{:S(2)}) collective-permute-start(bf16[1024,128]{1,0:T(8,128)(2,1)S(1)} %get-tuple-element.195), channel_id=1, source_target_pairs={{0,1},{1,2},{2,3},{3,0},{4,5},{5,6},{6,7},{7,4},{8,9},{9,10},{10,1... | collective-permute-start | bytes 786440 | tf_op jit(solution)/shard_map/ppermute | solution.py:27
  11.0 2.7 %collective-permute-start.1 = (bf16[1024,128]{1,0:T(8,128)(2,1)S(1)}, bf16[1024,128]{1,0:T(8,128)(2,1)S(1)}, u32[]{:S(2)}, u32[]{:S(2)}) collective-permute-start(bf16[1024,128]{1,0:T(8,128)(2,1)S(1)} %get-tuple-element.196), channel_id=1, source_target_pairs={{0,2},{1,3},{2,0},{3,1},{4,6},{5,7},{6,4},{7,5},{8,10},{9,11},{10,... | collective-permute-start | bytes 786440 | tf_op jit(solution)/shard_map/ppermute | solution.py:27
  14.4 4.4 %collective-permute-done.one = bf16[1024,128]{1,0:T(8,128)(2,1)S(1)} collective-permute-done((bf16[1024,128]{1,0:T(8,128)(2,1)S(1)}, bf16[1024,128]{1,0:T(8,128)(2,1)S(1)}, u32[]{:S(2)}, u32[]{:S(2)}) %collective-permute-start) | collective-permute-done | bytes 262176 | tf_op jit(solution)/shard_map/ppermute | solution.py:27
  18.8 2.9 %collective-permute-done.1.two = bf16[1024,128]{1,0:T(8,128)(2,1)S(1)} collective-permute-done((bf16[1024,128]{1,0:T(8,128)(2,1)S(1)}, bf16[1024,128]{1,0:T(8,128)(2,1)S(1)}, u32[]{:S(2)}, u32[]{:S(2)}) %collective-permute-start.1) | collective-permute-done | bytes 262176 | tf_op jit(solution)/shard_map/ppermute | solution.py:27
  21.7 3.5 %collective-permute-done.2.three = bf16[1024,128]{1,0:T(8,128)(2,1)S(1)} collective-permute-done((bf16[1024,128]{1,0:T(8,128)(2,1)S(1)}, bf16[1024,128]{1,0:T(8,128)(2,1)S(1)}, u32[]{:S(2)}, u32[]{:S(2)}) %collective-permute-start.2) | collective-permute-done | bytes 262176 | tf_op jit(solution)/shard_map/ppermute | solution.py:27
  25.3 2.0 %collective-permute-start.3 = (bf16[1280,128]{1,0:T(8,128)(2,1)S(1)}, bf16[1280,128]{1,0:T(8,128)(2,1)S(1)}, u32[]{:S(2)}, u32[]{:S(2)}) collective-permute-start(bf16[1280,128]{1,0:T(8,128)(2,1)S(1)} %own.1.refs_0_), channel_id=1, source_target_pairs={{0,32},{32,64},{64,96},{96,128},{128,160},{160,192},{192,224},{224... | collective-permute-start | bytes 983048 | tf_op jit(solution)/shard_map/ppermute | solution.py:27
  27.3 4.0 %collective-permute-start.4 = (bf16[1280,128]{1,0:T(8,128)(2,1)S(1)}, bf16[1280,128]{1,0:T(8,128)(2,1)S(1)}, u32[]{:S(2)}, u32[]{:S(2)}) collective-permute-start(bf16[1280,128]{1,0:T(8,128)(2,1)S(1)} %own.1.refs_0_), channel_id=1, source_target_pairs={{0,224},{32,0},{64,32},{96,64},{128,96},{160,128},{192,160},{224,1... | collective-permute-start | bytes 983048 | tf_op jit(solution)/shard_map/ppermute | solution.py:27
  31.3 2.3 %grad.1 = (f32[4,8,16,1024]{3,2,1,0:T(8,128)S(1)}, f32[4,8,16,1024]{3,2,1,0:T(8,128)S(1)}) custom-call(s32[4]{0:T(128)S(1)} %pad_add_fusion.pos, bf16[512,1024]{1,0:T(8,128)(2,1)S(1)} %copy-done.16, bf16[512,1024]{1,0:T(8,128)(2,1)S(1)} %get-tuple-element.205.delta), custom_call_target="tpu_custom_call" | custom-call | flops 1073741824 | bytes 6291456 | tf_op jit(solution)/shard_map/grad/pallas_call | solution.py:415
  33.7 4.7 %collective-permute-done.3.refs_0_ = bf16[1280,128]{1,0:T(8,128)(2,1)S(1)} collective-permute-done((bf16[1280,128]{1,0:T(8,128)(2,1)S(1)}, bf16[1280,128]{1,0:T(8,128)(2,1)S(1)}, u32[]{:S(2)}, u32[]{:S(2)}) %collective-permute-start.3) | collective-permute-done | bytes 327712 | tf_op jit(solution)/shard_map/ppermute | solution.py:27
  38.4 3.2 %collective-permute-start.6 = (bf16[1280,128]{1,0:T(8,128)(2,1)S(1)}, bf16[1280,128]{1,0:T(8,128)(2,1)S(1)}, u32[]{:S(2)}, u32[]{:S(2)}) collective-permute-start(bf16[1280,128]{1,0:T(8,128)(2,1)S(1)} %collective-permute-done.4.refs_1_), channel_id=1, source_target_pairs={{0,224},{32,0},{64,32},{96,64},{128,96},{160,128},{192,160},{224,1... | collective-permute-start | bytes 983048 | tf_op jit(solution)/shard_map/ppermute | solution.py:27
  41.6 1.7 %pick0.1 = (bf16[1,4,128,128]{3,2,1,0:T(8,128)(2,1)S(1)}, bf16[1,4,128,128]{3,2,1,0:T(8,128)(2,1)S(1)}, f32[1,8,128]{2,1,0:T(8,128)S(1)}, bf16[1,4,128,128]{3,2,...) custom-call(s32[4]{0:T(128)S(1)} %pad_add_fusion.pos, ...), custom_call_target="tpu_custom_call" | custom-call | flops 1073741824 | bytes 4194304 | tf_op jit(solution)/shard_map/pick0/pallas_call | solution.py:397
  43.3 6.5 %collective-permute-done.5.refs_0_ = bf16[1280,128]{1,0:T(8,128)(2,1)S(1)} collective-permute-done((bf16[1280,128]{1,0:T(8,128)(2,1)S(1)}, bf16[1280,128]{1,0:T(8,128)(2,1)S(1)}, u32[]{:S(2)}, u32[]{:S(2)}) %collective-permute-start.5) | collective-permute-done | bytes 327712 | tf_op jit(solution)/shard_map/ppermute | solution.py:27
  49.8 2.4 %collective-permute-start.7 = (bf16[1280,128]{1,0:T(8,128)(2,1)S(1)}, bf16[1280,128]{1,0:T(8,128)(2,1)S(1)}, u32[]{:S(2)}, u32[]{:S(2)}) collective-permute-start(bf16[1280,128]{1,0:T(8,128)(2,1)S(1)} %collective-permute-done.5.refs_0_), channel_id=1, source_target_pairs={{0,32},{32,64},{64,96},{96,128},{128,160},{160,192},{192,224},{224... | collective-permute-start | bytes 983048 | tf_op jit(solution)/shard_map/ppermute | solution.py:27
  53.9 1.6 %collective-permute-start.12 = (bf16[8,16,1024]{2,1,0:T(8,128)(2,1)S(1)}, bf16[8,16,1024]{2,1,0:T(8,128)(2,1)S(1)}, u32[]{:S(2)}, u32[]{:S(2)}) collective-permute-start(bf16[8,16,1024]{2,1,0:T(8,128)(2,1)S(1)} %get-tuple-element.269), channel_id=1, source_target_pairs={{0,8},{8,16},{16,24},{24,0},{1,9},{9,17},{17,25},{25,1},{2,10},{10... | collective-permute-start | bytes 786440 | tf_op jit(solution)/shard_map/ppermute | solution.py:27
  55.4 2.7 %collective-permute-start.13 = (bf16[8,16,1024]{2,1,0:T(8,128)(2,1)S(1)}, bf16[8,16,1024]{2,1,0:T(8,128)(2,1)S(1)}, u32[]{:S(2)}, u32[]{:S(2)}) collective-permute-start(bf16[8,16,1024]{2,1,0:T(8,128)(2,1)S(1)} %get-tuple-element.270), channel_id=1, source_target_pairs={{0,16},{8,24},{16,0},{24,8},{1,17},{9,25},{17,1},{25,9},{2,18},{10... | collective-permute-start | bytes 786440 | tf_op jit(solution)/shard_map/ppermute | solution.py:27
  58.2 1.4 %collective-permute-start.14 = (bf16[8,16,1024]{2,1,0:T(8,128)(2,1)S(1)}, bf16[8,16,1024]{2,1,0:T(8,128)(2,1)S(1)}, u32[]{:S(2)}, u32[]{:S(2)}) collective-permute-start(bf16[8,16,1024]{2,1,0:T(8,128)(2,1)S(1)} %get-tuple-element.271), channel_id=1, source_target_pairs={{0,24},{8,0},{16,8},{24,16},{1,25},{9,1},{17,9},{25,17},{2,26},{10... | collective-permute-start | bytes 786440 | tf_op jit(solution)/shard_map/ppermute | solution.py:27
  59.6 2.9 %pick1.1 = (bf16[2,4,128,128]{3,2,1,0:T(8,128)(2,1)S(1)}, bf16[2,4,128,128]{3,2,1,0:T(8,128)(2,1)S(1)}, f32[2,8,128]{2,1,0:T(8,128)S(1)}, bf16[2,4,128,128]{3,2,...) custom-call(s32[4]{0:T(128)S(1)} %pad_add_fusion.pos, ...), custom_call_target="tpu_custom_call" | custom-call | flops 1073741824 | bytes 4194304 | tf_op jit(solution)/shard_map/pick1/pallas_call | solution.py:397
  62.5 1.3 collective-permute-start.10
  63.8 2.1 %collective-permute-start.11 = (bf16[640,128]{1,0:T(8,128)(2,1)S(1)}, bf16[640,128]{1,0:T(8,128)(2,1)S(1)}, u32[]{:S(2)}, u32[]{:S(2)}) collective-permute-start(bf16[640,128]{1,0:T(8,128)(2,1)S(1)} %slice.26), channel_id=1, source_target_pairs={{0,224},{32,0},{64,32},{96,64},{128,96},{160,128},{192,160},{224,1... | collective-permute-start | bytes 491528 | tf_op jit(solution)/shard_map/ppermute | solution.py:27
  65.9 2.9 %pick2.1 = (bf16[2,4,128,128]{3,2,1,0:T(8,128)(2,1)S(1)}, bf16[2,4,128,128]{3,2,1,0:T(8,128)(2,1)S(1)}, f32[2,8,128]{2,1,0:T(8,128)S(1)}, bf16[2,4,128,128]{3,2,...) custom-call(s32[4]{0:T(128)S(1)} %pad_add_fusion.pos, ...), custom_call_target="tpu_custom_call" | custom-call | flops 1073741824 | bytes 4194304 | tf_op jit(solution)/shard_map/pick2/pallas_call | solution.py:397
  68.8 2.9 %pick3.1 = (bf16[2,4,128,128]{3,2,1,0:T(8,128)(2,1)S(1)}, bf16[2,4,128,128]{3,2,1,0:T(8,128)(2,1)S(1)}, f32[2,8,128]{2,1,0:T(8,128)S(1)}, bf16[2,4,128,128]{3,2,...) custom-call(s32[4]{0:T(128)S(1)} %pad_add_fusion.pos, ...), custom_call_target="tpu_custom_call" | custom-call | flops 1073741824 | bytes 4194304 | tf_op jit(solution)/shard_map/pick3/pallas_call | solution.py:397
  71.7 1.7 %pick4.1 = (bf16[1,4,128,128]{3,2,1,0:T(8,128)(2,1)S(1)}, bf16[1,4,128,128]{3,2,1,0:T(8,128)(2,1)S(1)}, f32[1,8,128]{2,1,0:T(8,128)S(1)}, bf16[1,4,128,128]{3,2,...) custom-call(s32[4]{0:T(128)S(1)} %pad_add_fusion.pos, ...), custom_call_target="tpu_custom_call" | custom-call | flops 1073741824 | bytes 4194304 | tf_op jit(solution)/shard_map/pick4/pallas_call | solution.py:397
  73.3 2.5 %send0.1 = bf16[4,256,512]{2,1,0:T(8,128)(2,1)S(1)} custom-call(bf16[1,4,128,128]{3,2,1,0:T(8,128)(2,1)S(1)} %get-tuple-element.224.refs_0_, bf16[1,4,128,128]{3,2,1,0:T(8,128)(2,1)S(1)} %get-tuple-element.225.refs_1_, f32[1,8,128]{2,1,0:T(8,128)S(1)} %get-tuple-element.226.refs_2_, bf16[2,4,128,128]{3,2,1,0:T(8,128)(2,1)S(1)} %get-tuple-element.247.refs_3_, ...), custom_call_target="tpu_custom_call" | custom-call | flops 4294967296 | bytes 5242880 | tf_op jit(solution)/shard_map/send0/pallas_call | solution.py:453
  75.9 2.5 %send1.1 = bf16[4,256,512]{2,1,0:T(8,128)(2,1)S(1)} custom-call(bf16[1,4,128,128]{3,2,1,0:T(8,128)(2,1)S(1)} %get-tuple-element.304.refs_0_, bf16[1,4,128,128]{3,2,1,0:T(8,128)(2,1)S(1)} %get-tuple-element.305.refs_1_, f32[1,8,128]{2,1,0:T(8,128)S(1)} %get-tuple-element.306.refs_2_, bf16[2,4,128,128]{3,2,1,0:T(8,128)(2,1)S(1)} %get-tuple-element.307.refs_3_, ...), custom_call_target="tpu_custom_call" | custom-call | flops 4294967296 | bytes 5242880 | tf_op jit(solution)/shard_map/send1/pallas_call | solution.py:453
  79.9 1.3 collective-permute-done.16.other1
  81.2 1.5 %collective-permute-done.15.other0 = bf16[4,256,512]{2,1,0:T(8,128)(2,1)S(1)} collective-permute-done((bf16[4,256,512]{2,1,0:T(8,128)(2,1)S(1)}, bf16[4,256,512]{2,1,0:T(8,128)(2,1)S(1)}, u32[]{:S(2)}, u32[]{:S(2)}) %collective-permute-start.15) | collective-permute-done | bytes 1048608 | tf_op jit(solution)/shard_map/ppermute | solution.py:27
  82.7 6.4 %keep.1 = (f32[512,512]{1,0:T(8,128)S(1)}, bf16[512,512]{1,0:T(8,128)(2,1)}, bf16[512,512]{1,0:T(8,128)(2,1)}, bf16[512,512]{1,0:T(8,128)(2,1)}) custom-call(bf16[4,256,512]{2,1,0:T(8,128)(2,1)S(1)} %collective-permute-done.15.other0, bf16[4,256,512]{2,1,0:T(8,128)(2,1)S(1)} %collective-permute-done.16.other1, ...), custom_call_target="tpu_custom_call" | custom-call | flops 8589934592 | bytes 10485760 | tf_op jit(solution)/shard_map/keep/pallas_call | solution.py:458
  89.6 2.4 %collective-permute-start.18 = (bf16[512,512]{1,0:T(8,128)(2,1)}, bf16[512,512]{1,0:T(8,128)(2,1)}, u32[]{:S(2)}, u32[]{:S(2)}) collective-permute-start(bf16[512,512]{1,0:T(8,128)(2,1)} %get-tuple-element.360), channel_id=1, source_target_pairs={{0,16},{8,24},{16,0},{24,8},{1,17},{9,25},{17,1},{25,9},{2,18},{10... | collective-permute-start | bytes 1572872 | tf_op jit(solution)/shard_map/ppermute | solution.py:27
  92.0 1.4 %collective-permute-start.19 = (bf16[512,512]{1,0:T(8,128)(2,1)}, bf16[512,512]{1,0:T(8,128)(2,1)}, u32[]{:S(2)}, u32[]{:S(2)}) collective-permute-start(bf16[512,512]{1,0:T(8,128)(2,1)} %get-tuple-element.361), channel_id=1, source_target_pairs={{0,24},{8,0},{16,8},{24,16},{1,25},{9,1},{17,9},{25,17},{2,26},{10... | collective-permute-start | bytes 1572872 | tf_op jit(solution)/shard_map/ppermute | solution.py:27
  94.2 4.6 %all-to-all-start = ((bf16[8,16,1024]{2,1,0:T(8,128)(2,1)}), bf16[8,16,1024]{2,1,0:T(8,128)(2,1)S(1)}, u32[]{:S(2)}, u32[]{:S(2)}) async-start(bf16[8,16,1024]{2,1,0:T(8,128)(2,1)} %convert_element_type.60), calls=%async_computation | async-start | bytes 524288 | tf_op jit(solution)/shard_map/all_to_all | solution.py:475
  98.8 1.0 convert_element_type.62
  99.8 1.1 copy.19
  101.2 1.6 %leave.1 = (f32[520,128]{1,0:T(8,128)S(1)}, f32[520,128]{1,0:T(8,128)S(1)}, f32[520,128]{1,0:T(8,128)S(1)}) custom-call(s32[256]{0:T(256)S(1)} %bitcast.35, s32[256]{0:T(256)S(1)} %fusion.9.goal_s, f32[2048]{0:T(1024)S(1)} %bitcast.33, f32[2048,128]{1,0:T(8,128)S(1)} %bitcast.28), custom_call_target="tpu_custom_call" | custom-call | flops 1024 | bytes 1048576 | tf_op jit(solution)/shard_map/leave/pallas_call | solution.py:497
  104.9 5.3 %all-to-all-done.blocks = bf16[8,16,1024]{2,1,0:T(8,128)(2,1)S(1)} async-done(((bf16[8,16,1024]{2,1,0:T(8,128)(2,1)}), bf16[8,16,1024]{2,1,0:T(8,128)(2,1)S(1)}, u32[]{:S(2)}, u32[]{:S(2)}) %all-to-all-start) | async-done | bytes 262176 | tf_op jit(solution)/shard_map/all_to_all | solution.py:475
  110.2 1.2 finish.1
  111.4 4.3 %collective-permute-done.17.refs_1_ = bf16[512,512]{1,0:T(8,128)(2,1)S(1)} collective-permute-done((bf16[512,512]{1,0:T(8,128)(2,1)}, bf16[512,512]{1,0:T(8,128)(2,1)S(1)}, u32[]{:S(2)}, u32[]{:S(2)}) %collective-permute-start.17) | collective-permute-done | bytes 524320 | tf_op jit(solution)/shard_map/ppermute | solution.py:27
  116.4 0.9 copy-done.2
  117.3 0.9 copy-done.4
  118.3 0.9 copy-done.6
  119.2 2.6 %evict.1 = (bf16[2048,256]{1,0:T(8,128)(2,1)S(1)}, f32[136,128]{1,0:T(8,128)S(1)}, f32[136,128]{1,0:T(8,128)S(1)}, f32[136,128]{1,0:T(8,128)S(1)}, f32[136,128]{1,0:T(8,128)S(1)}) custom-call(f32[1,2048]{1,0:T(1,128)S(1)} %convert_element_type.64.slot_map, f32[520,128]{1,0:T(8,128)S(1)} %copy-done.2, f32[520,128]{1,0:T(8,128)S(1)} %copy-done.4, ...), custom_call_target="tpu_custom_call" | custom-call | flops 536870912 | bytes 4194304 | tf_op jit(solution)/shard_map/evict/pallas_call | solution.py:507
  122.6 1.9 %collective-permute-start.21 = (f32[136,128]{1,0:T(8,128)S(1)}, f32[136,128]{1,0:T(8,128)S(1)}, u32[]{:S(2)}, u32[]{:S(2)}) collective-permute-start(f32[136,128]{1,0:T(8,128)S(1)} %get-tuple-element.379), channel_id=1, source_target_pairs={{0,2},{1,3},{2,0},{3,1},{4,6},{5,7},{6,4},{7,5},{8,10},{9,11},{10,... | collective-permute-start | bytes 208904 | tf_op jit(solution)/shard_map/ppermute | solution.py:27
  124.6 2.5 %collective-permute-start.22 = (f32[136,128]{1,0:T(8,128)S(1)}, f32[136,128]{1,0:T(8,128)S(1)}, u32[]{:S(2)}, u32[]{:S(2)}) collective-permute-start(f32[136,128]{1,0:T(8,128)S(1)} %get-tuple-element.380), channel_id=1, source_target_pairs={{0,3},{1,0},{2,1},{3,2},{4,7},{5,4},{6,5},{7,6},{8,11},{9,8},{10,9... | collective-permute-start | bytes 208904 | tf_op jit(solution)/shard_map/ppermute | solution.py:27
  127.1 4.3 %update.1 = (f32[2048,128]{1,0:T(8,128)}, f32[16,128]{1,0:T(8,128)}) custom-call(f32[1,2048]{1,0:T(1,128)S(1)} %convert_element_type.64.slot_map, bf16[2048,256]{1,0:T(8,128)(2,1)S(1)} %get-tuple-element.374.rhs, f32[2048,128]{1,0:T(8,128)S(1)} %bitcast.29, f32[16,128]{1,0:T(8,128)S(1)} %bitcast.34), custom_call_target="tpu_custom_call" | custom-call | flops 2147483648 | bytes 4194304 | tf_op jit(solution)/shard_map/update/pallas_call | solution.py:517
  131.4 1.3 arrive.1
  (70 shorter events, 8.7 us)
Async XLA Ops:
  0.7 1.6 %copy-start.13 = (bf16[1024,1024]{1,0:T(8,128)(2,1)S(1)}, bf16[1024,1024]{1,0:T(8,128)(2,1)}, u32[]{:S(2)}) copy-start(bf16[1024,1024]{1,0:T(8,128)(2,1)} %w_up.1) | copy-start | bytes 6291460
  2.3 1.2 copy-start.14
  3.5 1.2 copy-start.15
  4.8 9.6 %copy-start.7 = (s32[2,512,8]{1,2,0:T(8,128)S(1)}, s32[2,512,8]{1,2,0:T(8,128)}, u32[]{:S(2)}) copy-start(s32[2,512,8]{1,2,0:T(8,128)} %param.16) | copy-start | bytes 98308
  4.8 9.6 %copy-start.8 = (s32[2,512,8]{1,2,0:T(8,128)S(1)}, s32[2,512,8]{1,2,0:T(8,128)}, u32[]{:S(2)}) copy-start(s32[2,512,8]{1,2,0:T(8,128)} %param.17) | copy-start | bytes 98308
  4.8 9.6 %copy-start.9 = (bf16[2,512,8]{1,2,0:T(8,128)(2,1)S(1)}, bf16[2,512,8]{1,2,0:T(8,128)(2,1)}, u32[]{:S(2)}) copy-start(bf16[2,512,8]{1,2,0:T(8,128)(2,1)} %param.18) | copy-start | bytes 49156
  4.8 9.6 %copy-start.11 = (s32[2,512]{1,0:T(2,128)S(1)}, s32[2,512]{1,0:T(2,128)}, u32[]{:S(2)}) copy-start(s32[2,512]{1,0:T(2,128)} %lens) | copy-start | bytes 12292
  4.8 26.5 %copy-start.16 = (bf16[512,1024]{1,0:T(8,128)(2,1)S(1)}, bf16[512,1024]{1,0:T(8,128)(2,1)}, u32[]{:S(2)}) copy-start(bf16[512,1024]{1,0:T(8,128)(2,1)} %pooled.3) | copy-start | bytes 3145732
  9.3 9.4 %collective-permute-start = (bf16[1024,128]{1,0:T(8,128)(2,1)S(1)}, bf16[1024,128]{1,0:T(8,128)(2,1)S(1)}, u32[]{:S(2)}, u32[]{:S(2)}) collective-permute-start(bf16[1024,128]{1,0:T(8,128)(2,1)S(1)} %get-tuple-element.195), channel_id=1, source_target_pairs={{0,1},{1,2},{2,3},{3,0},{4,5},{5,6},{6,7},{7,4},{8,9},{9,10},{10,1... | collective-permute-start | bytes 786440 | tf_op jit(solution)/shard_map/ppermute | solution.py:27
  11.0 10.7 %collective-permute-start.1 = (bf16[1024,128]{1,0:T(8,128)(2,1)S(1)}, bf16[1024,128]{1,0:T(8,128)(2,1)S(1)}, u32[]{:S(2)}, u32[]{:S(2)}) collective-permute-start(bf16[1024,128]{1,0:T(8,128)(2,1)S(1)} %get-tuple-element.196), channel_id=1, source_target_pairs={{0,2},{1,3},{2,0},{3,1},{4,6},{5,7},{6,4},{7,5},{8,10},{9,11},{10,... | collective-permute-start | bytes 786440 | tf_op jit(solution)/shard_map/ppermute | solution.py:27
  13.6 11.5 %collective-permute-start.2 = (bf16[1024,128]{1,0:T(8,128)(2,1)S(1)}, bf16[1024,128]{1,0:T(8,128)(2,1)S(1)}, u32[]{:S(2)}, u32[]{:S(2)}) collective-permute-start(bf16[1024,128]{1,0:T(8,128)(2,1)S(1)} %get-tuple-element.197), channel_id=1, source_target_pairs={{0,3},{1,0},{2,1},{3,2},{4,7},{5,4},{6,5},{7,6},{8,11},{9,8},{10,9... | collective-permute-start | bytes 786440 | tf_op jit(solution)/shard_map/ppermute | solution.py:27
  25.3 13.1 %collective-permute-start.3 = (bf16[1280,128]{1,0:T(8,128)(2,1)S(1)}, bf16[1280,128]{1,0:T(8,128)(2,1)S(1)}, u32[]{:S(2)}, u32[]{:S(2)}) collective-permute-start(bf16[1280,128]{1,0:T(8,128)(2,1)S(1)} %own.1.refs_0_), channel_id=1, source_target_pairs={{0,32},{32,64},{64,96},{96,128},{128,160},{160,192},{192,224},{224... | collective-permute-start | bytes 983048 | tf_op jit(solution)/shard_map/ppermute | solution.py:27
  27.3 11.1 %collective-permute-start.4 = (bf16[1280,128]{1,0:T(8,128)(2,1)S(1)}, bf16[1280,128]{1,0:T(8,128)(2,1)S(1)}, u32[]{:S(2)}, u32[]{:S(2)}) collective-permute-start(bf16[1280,128]{1,0:T(8,128)(2,1)S(1)} %own.1.refs_0_), channel_id=1, source_target_pairs={{0,224},{32,0},{64,32},{96,64},{128,96},{160,128},{192,160},{224,1... | collective-permute-start | bytes 983048 | tf_op jit(solution)/shard_map/ppermute | solution.py:27
  38.4 14.7 %collective-permute-start.9 = (f32[4,8,16,1024]{3,2,1,0:T(8,128)S(1)}, f32[4,8,16,1024]{3,2,1,0:T(8,128)S(1)}, u32[]{:S(2)}, u32[]{:S(2)}) collective-permute-start(f32[4,8,16,1024]{3,2,1,0:T(8,128)S(1)} %get-tuple-element.232), channel_id=1, source_target_pairs={{0,4},{4,0},{1,5},{5,1},{2,6},{6,2},{3,7},{7,3},{8,12},{12,8},{9,1... | collective-permute-start | bytes 6291464 | tf_op jit(solution)/shard_map/ppermute | solution.py:27
  38.4 11.4 %collective-permute-start.5 = (bf16[1280,128]{1,0:T(8,128)(2,1)S(1)}, bf16[1280,128]{1,0:T(8,128)(2,1)S(1)}, u32[]{:S(2)}, u32[]{:S(2)}) collective-permute-start(bf16[1280,128]{1,0:T(8,128)(2,1)S(1)} %collective-permute-done.3.refs_0_), channel_id=1, source_target_pairs={{0,32},{32,64},{64,96},{96,128},{128,160},{160,192},{192,224},{224... | collective-permute-start | bytes 983048 | tf_op jit(solution)/shard_map/ppermute | solution.py:27
  38.4 11.4 %collective-permute-start.6 = (bf16[1280,128]{1,0:T(8,128)(2,1)S(1)}, bf16[1280,128]{1,0:T(8,128)(2,1)S(1)}, u32[]{:S(2)}, u32[]{:S(2)}) collective-permute-start(bf16[1280,128]{1,0:T(8,128)(2,1)S(1)} %collective-permute-done.4.refs_1_), channel_id=1, source_target_pairs={{0,224},{32,0},{64,32},{96,64},{128,96},{160,128},{192,160},{224,1... | collective-permute-start | bytes 983048 | tf_op jit(solution)/shard_map/ppermute | solution.py:27
  49.8 12.7 %collective-permute-start.7 = (bf16[1280,128]{1,0:T(8,128)(2,1)S(1)}, bf16[1280,128]{1,0:T(8,128)(2,1)S(1)}, u32[]{:S(2)}, u32[]{:S(2)}) collective-permute-start(bf16[1280,128]{1,0:T(8,128)(2,1)S(1)} %collective-permute-done.5.refs_0_), channel_id=1, source_target_pairs={{0,32},{32,64},{64,96},{96,128},{128,160},{160,192},{192,224},{224... | collective-permute-start | bytes 983048 | tf_op jit(solution)/shard_map/ppermute | solution.py:27
  52.2 10.3 %collective-permute-start.8 = (bf16[1280,128]{1,0:T(8,128)(2,1)S(1)}, bf16[1280,128]{1,0:T(8,128)(2,1)S(1)}, u32[]{:S(2)}, u32[]{:S(2)}) collective-permute-start(bf16[1280,128]{1,0:T(8,128)(2,1)S(1)} %collective-permute-done.6.refs_1_), channel_id=1, source_target_pairs={{0,224},{32,0},{64,32},{96,64},{128,96},{160,128},{192,160},{224,1... | collective-permute-start | bytes 983048 | tf_op jit(solution)/shard_map/ppermute | solution.py:27
  53.9 17.8 %collective-permute-start.12 = (bf16[8,16,1024]{2,1,0:T(8,128)(2,1)S(1)}, bf16[8,16,1024]{2,1,0:T(8,128)(2,1)S(1)}, u32[]{:S(2)}, u32[]{:S(2)}) collective-permute-start(bf16[8,16,1024]{2,1,0:T(8,128)(2,1)S(1)} %get-tuple-element.269), channel_id=1, source_target_pairs={{0,8},{8,16},{16,24},{24,0},{1,9},{9,17},{17,25},{25,1},{2,10},{10... | collective-permute-start | bytes 786440 | tf_op jit(solution)/shard_map/ppermute | solution.py:27
  55.4 16.2 %collective-permute-start.13 = (bf16[8,16,1024]{2,1,0:T(8,128)(2,1)S(1)}, bf16[8,16,1024]{2,1,0:T(8,128)(2,1)S(1)}, u32[]{:S(2)}, u32[]{:S(2)}) collective-permute-start(bf16[8,16,1024]{2,1,0:T(8,128)(2,1)S(1)} %get-tuple-element.270), channel_id=1, source_target_pairs={{0,16},{8,24},{16,0},{24,8},{1,17},{9,25},{17,1},{25,9},{2,18},{10... | collective-permute-start | bytes 786440 | tf_op jit(solution)/shard_map/ppermute | solution.py:27
  58.2 13.5 %collective-permute-start.14 = (bf16[8,16,1024]{2,1,0:T(8,128)(2,1)S(1)}, bf16[8,16,1024]{2,1,0:T(8,128)(2,1)S(1)}, u32[]{:S(2)}, u32[]{:S(2)}) collective-permute-start(bf16[8,16,1024]{2,1,0:T(8,128)(2,1)S(1)} %get-tuple-element.271), channel_id=1, source_target_pairs={{0,24},{8,0},{16,8},{24,16},{1,25},{9,1},{17,9},{25,17},{2,26},{10... | collective-permute-start | bytes 786440 | tf_op jit(solution)/shard_map/ppermute | solution.py:27
  62.5 9.1 %collective-permute-start.10 = (bf16[640,128]{1,0:T(8,128)(2,1)S(1)}, bf16[640,128]{1,0:T(8,128)(2,1)S(1)}, u32[]{:S(2)}, u32[]{:S(2)}) collective-permute-start(bf16[640,128]{1,0:T(8,128)(2,1)S(1)} %slice.25), channel_id=1, source_target_pairs={{0,32},{32,64},{64,96},{96,128},{128,160},{160,192},{192,224},{224... | collective-permute-start | bytes 491528 | tf_op jit(solution)/shard_map/ppermute | solution.py:27
  63.8 7.9 %collective-permute-start.11 = (bf16[640,128]{1,0:T(8,128)(2,1)S(1)}, bf16[640,128]{1,0:T(8,128)(2,1)S(1)}, u32[]{:S(2)}, u32[]{:S(2)}) collective-permute-start(bf16[640,128]{1,0:T(8,128)(2,1)S(1)} %slice.26), channel_id=1, source_target_pairs={{0,224},{32,0},{64,32},{96,64},{128,96},{160,128},{192,160},{224,1... | collective-permute-start | bytes 491528 | tf_op jit(solution)/shard_map/ppermute | solution.py:27
  78.4 2.7 %collective-permute-start.16 = (bf16[4,256,512]{2,1,0:T(8,128)(2,1)S(1)}, bf16[4,256,512]{2,1,0:T(8,128)(2,1)S(1)}, u32[]{:S(2)}, u32[]{:S(2)}) collective-permute-start(bf16[4,256,512]{2,1,0:T(8,128)(2,1)S(1)} %send1.1), channel_id=1, source_target_pairs={{0,4},{4,0},{1,5},{5,1},{2,6},{6,2},{3,7},{7,3},{8,12},{12,8},{9,1... | collective-permute-start | bytes 3145736 | tf_op jit(solution)/shard_map/ppermute | solution.py:27
  78.5 4.1 %collective-permute-start.15 = (bf16[4,256,512]{2,1,0:T(8,128)(2,1)S(1)}, bf16[4,256,512]{2,1,0:T(8,128)(2,1)S(1)}, u32[]{:S(2)}, u32[]{:S(2)}) collective-permute-start(bf16[4,256,512]{2,1,0:T(8,128)(2,1)S(1)} %send0.1), channel_id=1, source_target_pairs={{0,4},{4,0},{1,5},{5,1},{2,6},{6,2},{3,7},{7,3},{8,12},{12,8},{9,1... | collective-permute-start | bytes 3145736 | tf_op jit(solution)/shard_map/ppermute | solution.py:27
  79.8 19.0 %copy-start.17 = (s32[1,1,2048]{2,1,0:T(1,128)S(1)}, s32[1,1,2048]{2,1,0:T(1,128)}, u32[]{:S(2)}) copy-start(s32[1,1,2048]{2,1,0:T(1,128)} %param.20) | copy-start | bytes 24580
  79.8 21.1 %copy-start.18 = (s32[1,1,256]{2,1,0:T(1,128)S(1)}, s32[1,1,256]{2,1,0:T(1,128)}, u32[]{:S(2)}) copy-start(s32[1,1,256]{2,1,0:T(1,128)} %param.24) | copy-start | bytes 3076
  79.8 21.3 %copy-start.10 = (f32[1,1,2048]{2,1,0:T(1,128)S(1)}, f32[1,1,2048]{2,1,0:T(1,128)}, u32[]{:S(2)}) copy-start(f32[1,1,2048]{2,1,0:T(1,128)} %param.22) | copy-start | bytes 24580
  79.9 21.3 %copy-start.12 = (s32[1,1,256]{2,1,0:T(1,128)S(1)}, s32[1,1,256]{2,1,0:T(1,128)}, u32[]{:S(2)}) copy-start(s32[1,1,256]{2,1,0:T(1,128)} %param.23) | copy-start | bytes 3076
  89.0 12.1 %copy-start = (f32[1,1,2048,128]{3,2,1,0:T(8,128)S(1)}, f32[1,1,2048,128]{3,2,1,0:T(8,128)}, u32[]{:S(2)}) copy-start(f32[1,1,2048,128]{3,2,1,0:T(8,128)} %param.21) | copy-start | bytes 3145732
  89.0 26.6 %collective-permute-start.17 = (bf16[512,512]{1,0:T(8,128)(2,1)}, bf16[512,512]{1,0:T(8,128)(2,1)S(1)}, u32[]{:S(2)}, u32[]{:S(2)}) collective-permute-start(bf16[512,512]{1,0:T(8,128)(2,1)} %get-tuple-element.359), channel_id=1, source_target_pairs={{0,8},{8,16},{16,24},{24,0},{1,9},{9,17},{17,25},{25,1},{2,10},{10... | collective-permute-start | bytes 1572872 | tf_op jit(solution)/shard_map/ppermute | solution.py:27
  89.6 26.0 %collective-permute-start.18 = (bf16[512,512]{1,0:T(8,128)(2,1)}, bf16[512,512]{1,0:T(8,128)(2,1)}, u32[]{:S(2)}, u32[]{:S(2)}) collective-permute-start(bf16[512,512]{1,0:T(8,128)(2,1)} %get-tuple-element.360), channel_id=1, source_target_pairs={{0,16},{8,24},{16,0},{24,8},{1,17},{9,25},{17,1},{25,9},{2,18},{10... | collective-permute-start | bytes 1572872 | tf_op jit(solution)/shard_map/ppermute | solution.py:27
  92.0 24.4 %collective-permute-start.19 = (bf16[512,512]{1,0:T(8,128)(2,1)}, bf16[512,512]{1,0:T(8,128)(2,1)}, u32[]{:S(2)}, u32[]{:S(2)}) collective-permute-start(bf16[512,512]{1,0:T(8,128)(2,1)} %get-tuple-element.361), channel_id=1, source_target_pairs={{0,24},{8,0},{16,8},{24,16},{1,25},{9,1},{17,9},{25,17},{2,26},{10... | collective-permute-start | bytes 1572872 | tf_op jit(solution)/shard_map/ppermute | solution.py:27
  94.2 16.0 %all-to-all-start = ((bf16[8,16,1024]{2,1,0:T(8,128)(2,1)}), bf16[8,16,1024]{2,1,0:T(8,128)(2,1)S(1)}, u32[]{:S(2)}, u32[]{:S(2)}) async-start(bf16[8,16,1024]{2,1,0:T(8,128)(2,1)} %convert_element_type.60), calls=%async_computation | async-start | bytes 524288 | tf_op jit(solution)/shard_map/all_to_all | solution.py:475
  102.7 0.7 copy-start.1
  103.5 0.7 copy-start.3
  104.2 0.7 copy-start.5
  116.4 1.0 copy-start.2
  117.3 1.0 copy-start.4
  118.3 1.0 copy-start.6
  121.9 9.6 %collective-permute-start.20 = (f32[136,128]{1,0:T(8,128)S(1)}, f32[136,128]{1,0:T(8,128)S(1)}, u32[]{:S(2)}, u32[]{:S(2)}) collective-permute-start(f32[136,128]{1,0:T(8,128)S(1)} %get-tuple-element.378), channel_id=1, source_target_pairs={{0,1},{1,2},{2,3},{3,0},{4,5},{5,6},{6,7},{7,4},{8,9},{9,10},{10,1... | collective-permute-start | bytes 208904 | tf_op jit(solution)/shard_map/ppermute | solution.py:27
  122.6 8.8 %collective-permute-start.21 = (f32[136,128]{1,0:T(8,128)S(1)}, f32[136,128]{1,0:T(8,128)S(1)}, u32[]{:S(2)}, u32[]{:S(2)}) collective-permute-start(f32[136,128]{1,0:T(8,128)S(1)} %get-tuple-element.379), channel_id=1, source_target_pairs={{0,2},{1,3},{2,0},{3,1},{4,6},{5,7},{6,4},{7,5},{8,10},{9,11},{10,... | collective-permute-start | bytes 208904 | tf_op jit(solution)/shard_map/ppermute | solution.py:27
  124.6 6.9 %collective-permute-start.22 = (f32[136,128]{1,0:T(8,128)S(1)}, f32[136,128]{1,0:T(8,128)S(1)}, u32[]{:S(2)}, u32[]{:S(2)}) collective-permute-start(f32[136,128]{1,0:T(8,128)S(1)} %get-tuple-element.380), channel_id=1, source_target_pairs={{0,3},{1,0},{2,1},{3,2},{4,7},{5,4},{6,5},{7,6},{8,11},{9,8},{10,9... | collective-permute-start | bytes 208904 | tf_op jit(solution)/shard_map/ppermute | solution.py:27

commit v3 on v2

--- a/solution.py
+++ b/solution.py
@@ -27,7 +27,7 @@
     return lax.ppermute(x, axis, [(i, (i + step) % size) for i in range(size)])
 
 
-def call(body, ins, outs, scratch, flops, moved, name):
+def call(body, ins, outs, scratch, micros, name):
     return pl.pallas_call(
         body,
         in_specs=ins,
@@ -35,7 +35,9 @@
         out_shape=outs,
         scratch_shapes=scratch,
         compiler_params=pltpu.CompilerParams(vmem_limit_bytes=20 << 20),
-        cost_estimate=pl.CostEstimate(flops=flops, bytes_accessed=moved, transcendentals=0),
+        cost_estimate=pl.CostEstimate(
+            flops=1 << 20, bytes_accessed=int(micros * 3.5e6), transcendentals=0
+        ),
         name=name,
     )
 
@@ -99,8 +101,7 @@
 
 
 def pick_kernel(count, pos, earlier, *refs):
-    blocks = 2 if count == 2 or len(refs) == 19 else 1
-    msgs, refs = refs[:blocks], refs[blocks:]
+    msg, refs = refs[0], refs[1:]
     outs, (bag_all, dense, ranks, picks, rhs) = refs[:12], refs[12:]
     bags = bag_all.shape[2]
     units = 2 * count
@@ -110,12 +111,7 @@
     ids = (z * 8 + 2 * ((x + j) & 3) + ((c + (j >> 2)) & 1)).astype(F32)
     for s in range(count):
         for t in range(2):
-            if count == 2:
-                ref, first = msgs[s], t * (bags + lines)
-            elif blocks == 2:
-                ref, first = msgs[t], 0
-            else:
-                ref, first = msgs[0], t * (bags + lines)
+            ref, first = (msg.at[s] if count == 2 else msg), t * (bags + lines)
             bag_all[s, t] = ref[first : first + bags, :]
             first += bags
             fields = jnp.concatenate(
@@ -205,7 +201,7 @@
 
 
 def keep_kernel(other0, other1, *refs):
-    outs, onto, both, total = refs[30:34], refs[34], refs[35], refs[36]
+    outs, mark, onto, both, total = refs[30:34], refs[34], refs[35], refs[36], refs[37]
     for t, other in enumerate((other0, other1)):
         steps = [refs[15 * t + 3 * i : 15 * t + 3 * i + 3] for i in range(5)]
 
@@ -216,6 +212,7 @@
         lax.fori_loop(0, 4, one, 0)
         for k in range(4):
             outs[k][t * 256 : (t + 1) * 256, :] = total[k].astype(outs[k].dtype)
+    mark[...] = total[0, :8, :128]
 
 
 def grad_kernel(pos, pooled, delta, keep, send, half):
@@ -365,8 +362,7 @@
         [SMEM, VMEM, VMEM, VMEM],
         [shape((bags, 1024), BF16), shape((2 * bags, 128), F32)] + [shape((2 * bags, 128), BF16)] * 3,
         [pltpu.VMEM((4, bags, 256), F32)],
-        2 << 30,
-        6 << 20,
+        4.5,
         "top",
     )(pos, pooled, w_up, grad_out)
     got = [shifted(parts[k], H, k) for k in (1, 2, 3)]
@@ -379,15 +375,14 @@
         [VMEM] * 4,
         [shape((2, 128, 128), BF16), shape((bags, bags), BF16)],
         [],
-        1 << 20,
-        1 << 20,
+        1.0,
         "fields",
     )(*[jnp.swapaxes(a, 1, 2) for a in (owners, rows, lookup_weight)], lens)
     (own,) = call(
-        own_kernel, [VMEM] * 5, [shape((2 * (bags + 128), 128), BF16)], [], 1 << 20, 2 << 20, "own"
+        own_kernel, [VMEM] * 5, [shape((2 * (bags + 128), 128), BF16)], [], 0.5, "own"
     )(parts[0], *got, fields)
 
-    def pick(step, blocks):
+    def pick(step, block):
         count = STEPS[step]
         outs = [
             shape((count, 4, MOST, 128), BF16),
@@ -396,7 +391,7 @@
         ] * 4
         return call(
             functools.partial(pick_kernel, count),
-            [SMEM, VMEM] + [VMEM] * len(blocks),
+            [SMEM, VMEM, VMEM],
             outs,
             [
                 pltpu.VMEM((count, 2, bags, 128), BF16),
@@ -405,43 +400,42 @@
                 pltpu.VMEM((2, 8 * MOST, bags), BF16),
                 pltpu.VMEM((2, bags, 256), BF16),
             ],
-            1 << 30,
-            4 << 20,
+            2.8,
             f"pick{step}",
-        )(pos, earlier, *blocks)
-
-    up, down = shifted(own, Z, 1), shifted(own, Z, -1)
+        )(pos, earlier, block)
+
+    ways = [(2 * i, 2 * ((i + 1) % 8)) for i in range(8)]
+    ways += [(2 * i + 1, 2 * ((i + 7) % 8) + 1) for i in range(8)]
+
+    def passed(message):
+        return lax.ppermute(message, (Z, C), ways)
+
+    near = passed(jnp.stack([own, shifted(own, C, 1)]))
     (delta,), (own,) = together((delta,), (own,))
     grad, there = call(
         grad_kernel,
         [SMEM, VMEM, VMEM],
         [shape((4, 8, 16, 1024), F32)] * 2,
         [pltpu.VMEM((512, 1024), F32)],
-        1 << 30,
-        6 << 20,
+        2.3,
         "grad",
     )(pos, pooled, delta)
-    near = (up, down)
-    (up, down), (grad, there) = together((up, down), (grad, there))
+    picked = [pick(0, own)]
+    (near,), (grad, there), picked[0] = together((near,), (grad, there), picked[0])
     there = shifted(there, C, 1)
-    up, down = shifted(up, Z, 1), shifted(down, Z, -1)
-    picked = [pick(0, (own,))]
-    mid = (up, down)
-    (up, down), near, *picked = together((up, down), near, *picked)
-    up, down = shifted(up, Z, 1), shifted(down, Z, -1)
+    mid = passed(near)
+    picked.append(pick(1, near))
+    (mid,), picked[1] = together((mid,), picked[1])
+    far = passed(mid)
+    (there,), (mid,) = together((there,), (mid,))
     grad_x = grad + there
     total, blocks = grad_x[0], [grad_x[k].astype(BF16) for k in (1, 2, 3)]
-    near, (total,), blocks = together(near, (total,), blocks)
     got_x = [shifted(blocks[k - 1], X, k) for k in (1, 2, 3)]
-    picked.append(pick(1, near))
-    far = (up, down)
-    (up, down), mid, picked[1] = together((up, down), mid, picked[1])
-    part = bags + 128
-    last = (shifted(up[:part], Z, 1), shifted(down[part:], Z, -1))
+    last = passed(far[0])
+    (mid,), (total,), (far,) = together((mid,), (total,), (far,))
     picked.append(pick(2, mid))
-    far, picked[2] = together(far, picked[2])
     picked.append(pick(3, far))
-    last, got_x, picked[3] = together(last, got_x, picked[3])
+    (last,), got_x, picked[3] = together((last,), got_x, picked[3])
     picked.append(pick(4, last))
 
     work = [pltpu.VMEM((256, 8 * MOST), BF16), pltpu.VMEM((8 * MOST, 512), BF16)]
@@ -451,35 +445,32 @@
         if others:
             others, picked[4] = together(others, picked[4])
         (out,) = call(
-            send_kernel, [VMEM] * 15, [shape((4, 256, 512), BF16)], work, 4 << 30, 5 << 20, f"send{t}"
+            send_kernel, [VMEM] * 15, [shape((4, 256, 512), BF16)], work, 2.5, f"send{t}"
         )(*half(t, 1))
         others.append(out)
     others = [shifted(out, C, 1) for out in others]
     outs = call(
         keep_kernel,
         [VMEM] * 32,
-        [shape((512, 512), F32)] + [shape((512, 512), BF16)] * 3,
+        [shape((512, 512), F32)] + [shape((512, 512), BF16)] * 3 + [shape((8, 128), F32)],
         work + [pltpu.VMEM((4, 256, 512), F32)],
-        8 << 30,
-        10 << 20,
+        6.3,
         "keep",
     )(*others, *half(0, 0), *half(1, 0))
     arrived = [outs[0]] + [shifted(outs[k], X, k) for k in (1, 2, 3)]
 
     for block in got_x:
         total = total + block.astype(F32)
-    first, total, slot_map, evict_slots, evict_dest = lax.optimization_barrier(
-        (arrived[0], total, slot_map, evict_slots, evict_dest)
-    )
-    arrived[0] = first
+    _, total, slot_map, evict_slots, evict_dest = lax.optimization_barrier(
+        (outs[4], total, slot_map, evict_slots, evict_dest)
+    )
     blocks = lax.all_to_all(total.astype(BF16), Z, split_axis=0, concat_axis=0, tiled=True)
     (grad_up,) = call(
         finish_kernel,
         [SMEM, VMEM, VMEM],
         [shape((16, 1024), F32)],
         [],
-        1 << 10,
-        1 << 18,
+        1.2,
         "finish",
     )(pos, total, blocks)
 
@@ -499,18 +490,15 @@
         [SMEM] * 3 + [VMEM],
         [shape((520, 128), F32)] * 3,
         [],
-        1 << 10,
-        1 << 20,
+        1.6,
         "leave",
     )(evict_slots.reshape(-1), goal, cache_accum.reshape(-1), cache_weight[0, 0])
-    arrived, leaving = together(arrived, leaving)
     rhs, *held = call(
         evict_kernel,
         [VMEM] * 8,
         [shape((2048, 256), BF16)] + [shape((HELD, 128), F32)] * 4,
         [pltpu.VMEM((512, 2048), BF16), pltpu.VMEM((512, 256), F32)],
-        1 << 29,
-        4 << 20,
+        2.7,
         "evict",
     )(slot_rows, *leaving, *arrived)
     moved = [shifted(held[k], H, k) for k in (1, 2, 3)]
@@ -519,8 +507,7 @@
         [VMEM] * 4,
         [shape((2048, 128), F32), shape((16, 128), F32)],
         [pltpu.VMEM((512, 2048), BF16), pltpu.VMEM((512, 256), F32)],
-        2 << 30,
-        4 << 20,
+        4.3,
         "update",
     )(slot_rows, rhs, cache_weight[0, 0], cache_accum.reshape(16, 128))
     held = [held[0]] + moved
@@ -529,8 +516,7 @@
         [SMEM] + [VMEM] * 4,
         [shape((4, 128, 128), F32), shape((4, 128), F32)],
         [],
-        1 << 10,
-        1 << 19,
+        1.2,
         "arrive",
     )(pos, *held)
     return (

time: 133 us -> 147 us (1.11)
  waiting for transfers between devices: 35.1 us -> 62.2 us
  starting transfers between devices: 41.4 us -> 27 us
    ppermute x0 -> x4, waiting for transfers between devices: none -> 29.2 us  [passed(): return lax.ppermute(message, (Z, C), ways)]
    ppermute x23 -> x16, starting transfers between devices: 36.8 us -> 20.8 us  [shifted(): return lax.ppermute(x, axis, [(i, (i + step) % size) for i in range(size)])]
    all_to_all x1, waiting for transfers between devices: 5.29 us -> 0.01 us  [on_device(): lax.all_to_all(total.astype(BF16), Z, split_axis=0, concat_axis=0, tiled=...]
    ppermute x23 -> x16, waiting for transfers between devices: 29.8 us -> 32.9 us  [shifted(): return lax.ppermute(x, axis, [(i, (i + step) % size) for i in range(size)])]
    ppermute x0 -> x4, starting transfers between devices: none -> 2.09 us  [passed(): return lax.ppermute(message, (Z, C), ways)]
  transfers between devices with their start and end apart: 24 -> 21, of which waited for: 10 -> 12; matrix products, arithmetic and copies ran while one was open for 3% -> 3% of each run, Pallas kernels for 15% -> 15%
where the time goes in v3:
time: 147 us; the launch traced here: 146 us
  waiting for transfers between devices  62.2 us (42%)
  Pallas kernels  40.8 us (28%)
  starting transfers between devices  27 us (18%)
  local copies, waits for them, and re-layouts  12.2 us (8%)
  other arithmetic  1.79 us (1%)
  between operations  1.54 us (1%)
    ppermute x16, waiting for transfers between devices, shifted(): return lax.ppermute(x, axis, [(i, (i + step) % size) for i in range(size)])  32.9 us
    ppermute x4, waiting for transfers between devices, passed(): return lax.ppermute(message, (Z, C), ways)  29.2 us
    ppermute x16, starting transfers between devices, shifted(): return lax.ppermute(x, axis, [(i, (i + step) % size) for i in range(size)])  20.8 us
    pallas_call x5, Pallas kernels, pick(): call(functools.partial(pick_kernel, count), [SMEM, VMEM, VMEM], outs, [pl...  11.9 us
    unnamed x38, local copies, waits for them, and re-layouts  9.98 us
    pallas_call x1, Pallas kernels, on_device(): call(keep_kernel, [VMEM] * 32, [shape((512, 512), F32)] + [shape((512, 51...  6.34 us
    pallas_call x2, Pallas kernels, on_device(): call(send_kernel, [VMEM] * 15, [shape((4, 256, 512), BF16)], work, 2.5, f...  5.07 us
    pallas_call x1, Pallas kernels, on_device(): call(top_kernel, [SMEM, VMEM, VMEM, VMEM], [shape((bags, 1024), BF16), sh...  4.52 us
  transfers between devices with their start and end apart: 21, of which 12 were waited for; matrix products, arithmetic and copies ran while one was open for 3% of the time, Pallas kernels for 15%

profile of v3, /device:TPU:8, one launch (start us, length us, event | category | flops | bytes accessed | tf_op | source)
XLA Modules:
  0.0 145.7 jit_solution(17853060807041459210)
XLA Ops:
  0.7 1.2 copy-done
  1.9 1.6 %copy-done.3 = bf16[1024,1024]{1,0:T(8,128)(2,1)S(1)} copy-done((bf16[1024,1024]{1,0:T(8,128)(2,1)S(1)}, bf16[1024,1024]{1,0:T(8,128)(2,1)}, u32[]{:S(2)}) %copy-start.3) | copy-done | bytes 2097176
  3.5 1.2 copy-done.4
  4.8 4.5 %top.1 = (bf16[512,1024]{1,0:T(8,128)(2,1)S(1)}, f32[1024,128]{1,0:T(8,128)S(1)}, bf16[1024,128]{1,0:T(8,128)(2,1)S(1)}, bf16[1024,128]{1,0:T(8,128)(2,1)S(1)}, bf16[1024,128]{1,0:T(8,128)(2,1)S(1)}) custom-call(s32[4]{0:T(128)S(1)} %pad_add_fusion.pos, bf16[512,1024]{1,0:T(8,128)(2,1)S(1)} %copy-done, bf16[1024,1024]{1,0:T(8,128)(2,1)S(1)} %copy-done.3, ...), custom_call_target="tpu_custom_call" | custom-call | flops 1048576 | bytes 15750000 | tf_op jit(solution)/shard_map/top/pallas_call | solution.py:360
  9.3 1.7 %collective-permute-start = (bf16[1024,128]{1,0:T(8,128)(2,1)S(1)}, bf16[1024,128]{1,0:T(8,128)(2,1)S(1)}, u32[]{:S(2)}, u32[]{:S(2)}) collective-permute-start(bf16[1024,128]{1,0:T(8,128)(2,1)S(1)} %get-tuple-element.163), channel_id=1, source_target_pairs={{0,1},{1,2},{2,3},{3,0},{4,5},{5,6},{6,7},{7,4},{8,9},{9,10},{10,1... | collective-permute-start | bytes 786440 | tf_op jit(solution)/shard_map/ppermute | solution.py:27
  11.0 2.7 %collective-permute-start.1 = (bf16[1024,128]{1,0:T(8,128)(2,1)S(1)}, bf16[1024,128]{1,0:T(8,128)(2,1)S(1)}, u32[]{:S(2)}, u32[]{:S(2)}) collective-permute-start(bf16[1024,128]{1,0:T(8,128)(2,1)S(1)} %get-tuple-element.164), channel_id=1, source_target_pairs={{0,2},{1,3},{2,0},{3,1},{4,6},{5,7},{6,4},{7,5},{8,10},{9,11},{10,... | collective-permute-start | bytes 786440 | tf_op jit(solution)/shard_map/ppermute | solution.py:27
  14.4 4.4 %collective-permute-done.one = bf16[1024,128]{1,0:T(8,128)(2,1)S(1)} collective-permute-done((bf16[1024,128]{1,0:T(8,128)(2,1)S(1)}, bf16[1024,128]{1,0:T(8,128)(2,1)S(1)}, u32[]{:S(2)}, u32[]{:S(2)}) %collective-permute-start) | collective-permute-done | bytes 262176 | tf_op jit(solution)/shard_map/ppermute | solution.py:27
  18.8 2.9 %collective-permute-done.1.two = bf16[1024,128]{1,0:T(8,128)(2,1)S(1)} collective-permute-done((bf16[1024,128]{1,0:T(8,128)(2,1)S(1)}, bf16[1024,128]{1,0:T(8,128)(2,1)S(1)}, u32[]{:S(2)}, u32[]{:S(2)}) %collective-permute-start.1) | collective-permute-done | bytes 262176 | tf_op jit(solution)/shard_map/ppermute | solution.py:27
  21.7 3.5 %collective-permute-done.2.three = bf16[1024,128]{1,0:T(8,128)(2,1)S(1)} collective-permute-done((bf16[1024,128]{1,0:T(8,128)(2,1)S(1)}, bf16[1024,128]{1,0:T(8,128)(2,1)S(1)}, u32[]{:S(2)}, u32[]{:S(2)}) %collective-permute-start.2) | collective-permute-done | bytes 262176 | tf_op jit(solution)/shard_map/ppermute | solution.py:27
  25.4 1.6 %collective-permute-done.3 = bf16[1280,128]{1,0:T(8,128)(2,1)S(1)} collective-permute-done((bf16[1280,128]{1,0:T(8,128)(2,1)S(1)}, bf16[1280,128]{1,0:T(8,128)(2,1)S(1)}, u32[]{:S(2)}, u32[]{:S(2)}) %collective-permute-start.3) | collective-permute-done | bytes 327712 | tf_op jit(solution)/shard_map/ppermute | solution.py:27
  27.1 2.0 %collective-permute-start.4 = (bf16[2,1280,128]{2,1,0:T(8,128)(2,1)S(1)}, bf16[2,1280,128]{2,1,0:T(8,128)(2,1)S(1)}, u32[]{:S(2)}, u32[]{:S(2)}) collective-permute-start(bf16[2,1280,128]{2,1,0:T(8,128)(2,1)S(1)} %pad_maximum_fusion), channel_id=1, source_target_pairs={{0,32},{32,64},{64,96},{96,128},{128,160},{160,192},{192,224},{224... | collective-permute-start | bytes 1966088 | tf_op jit(solution)/shard_map/ppermute | solution.py:411
  29.1 2.3 %grad.1 = (f32[4,8,16,1024]{3,2,1,0:T(8,128)S(1)}, f32[4,8,16,1024]{3,2,1,0:T(8,128)S(1)}) custom-call(s32[4]{0:T(128)S(1)} %pad_add_fusion.pos, bf16[512,1024]{1,0:T(8,128)(2,1)S(1)} %copy-done.1, bf16[512,1024]{1,0:T(8,128)(2,1)S(1)} %get-tuple-element.173.delta), custom_call_target="tpu_custom_call" | custom-call | flops 1048576 | bytes 8049999 | tf_op jit(solution)/shard_map/grad/pallas_call | solution.py:415
  31.4 1.7 %pick0.1 = (bf16[1,4,128,128]{3,2,1,0:T(8,128)(2,1)S(1)}, bf16[1,4,128,128]{3,2,1,0:T(8,128)(2,1)S(1)}, f32[1,8,128]{2,1,0:T(8,128)S(1)}, bf16[1,4,128,128]{3,2,...) custom-call(s32[4]{0:T(128)S(1)} %pad_add_fusion.pos, ...), custom_call_target="tpu_custom_call" | custom-call | flops 1048576 | bytes 9800000 | tf_op jit(solution)/shard_map/pick0/pallas_call | solution.py:392
  33.0 8.5 %collective-permute-done.4.refs_0_ = bf16[2,1280,128]{2,1,0:T(8,128)(2,1)S(1)} collective-permute-done((bf16[2,1280,128]{2,1,0:T(8,128)(2,1)S(1)}, bf16[2,1280,128]{2,1,0:T(8,128)(2,1)S(1)}, u32[]{:S(2)}, u32[]{:S(2)}) %collective-permute-start.4) | collective-permute-done | bytes 655392 | tf_op jit(solution)/shard_map/ppermute | solution.py:411
  41.6 2.9 %pick1.1 = (bf16[2,4,128,128]{3,2,1,0:T(8,128)(2,1)S(1)}, bf16[2,4,128,128]{3,2,1,0:T(8,128)(2,1)S(1)}, f32[2,8,128]{2,1,0:T(8,128)S(1)}, bf16[2,4,128,128]{3,2,...) custom-call(s32[4]{0:T(128)S(1)} %pad_add_fusion.pos, ...), custom_call_target="tpu_custom_call" | custom-call | flops 1048576 | bytes 9800000 | tf_op jit(solution)/shard_map/pick1/pallas_call | solution.py:392
  44.4 8.9 %collective-permute-done.6.refs_0_ = bf16[2,1280,128]{2,1,0:T(8,128)(2,1)S(1)} collective-permute-done((bf16[2,1280,128]{2,1,0:T(8,128)(2,1)S(1)}, bf16[2,1280,128]{2,1,0:T(8,128)(2,1)S(1)}, u32[]{:S(2)}, u32[]{:S(2)}) %collective-permute-start.6) | collective-permute-done | bytes 655392 | tf_op jit(solution)/shard_map/ppermute | solution.py:411
  53.4 11.8 %collective-permute-done.7.refs_0_ = bf16[2,1280,128]{2,1,0:T(8,128)(2,1)S(1)} collective-permute-done((bf16[2,1280,128]{2,1,0:T(8,128)(2,1)S(1)}, bf16[2,1280,128]{2,1,0:T(8,128)(2,1)S(1)}, u32[]{:S(2)}, u32[]{:S(2)}) %collective-permute-start.7) | collective-permute-done | bytes 655392 | tf_op jit(solution)/shard_map/ppermute | solution.py:411
  66.1 3.1 %collective-permute-start.10 = (bf16[8,16,1024]{2,1,0:T(8,128)(2,1)S(1)}, bf16[8,16,1024]{2,1,0:T(8,128)(2,1)S(1)}, u32[]{:S(2)}, u32[]{:S(2)}) collective-permute-start(bf16[8,16,1024]{2,1,0:T(8,128)(2,1)S(1)} %get-tuple-element.322), channel_id=1, source_target_pairs={{0,16},{8,24},{16,0},{24,8},{1,17},{9,25},{17,1},{25,9},{2,18},{10... | collective-permute-start | bytes 786440 | tf_op jit(solution)/shard_map/ppermute | solution.py:27
  69.2 1.1 collective-permute-start.11
  71.3 2.9 %pick3.1 = (bf16[2,4,128,128]{3,2,1,0:T(8,128)(2,1)S(1)}, bf16[2,4,128,128]{3,2,1,0:T(8,128)(2,1)S(1)}, f32[2,8,128]{2,1,0:T(8,128)S(1)}, bf16[2,4,128,128]{3,2,...) custom-call(s32[4]{0:T(128)S(1)} %pad_add_fusion.pos, ...), custom_call_target="tpu_custom_call" | custom-call | flops 1048576 | bytes 9800000 | tf_op jit(solution)/shard_map/pick3/pallas_call | solution.py:392
  74.1 2.9 %pick2.1 = (bf16[2,4,128,128]{3,2,1,0:T(8,128)(2,1)S(1)}, bf16[2,4,128,128]{3,2,1,0:T(8,128)(2,1)S(1)}, f32[2,8,128]{2,1,0:T(8,128)S(1)}, bf16[2,4,128,128]{3,2,...) custom-call(s32[4]{0:T(128)S(1)} %pad_add_fusion.pos, ...), custom_call_target="tpu_custom_call" | custom-call | flops 1048576 | bytes 9800000 | tf_op jit(solution)/shard_map/pick2/pallas_call | solution.py:392
  77.0 4.5 %collective-permute-done.11 = bf16[8,16,1024]{2,1,0:T(8,128)(2,1)S(1)} collective-permute-done((bf16[8,16,1024]{2,1,0:T(8,128)(2,1)S(1)}, bf16[8,16,1024]{2,1,0:T(8,128)(2,1)S(1)}, u32[]{:S(2)}, u32[]{:S(2)}) %collective-permute-start.11) | collective-permute-done | bytes 262176 | tf_op jit(solution)/shard_map/ppermute | solution.py:27
  81.6 1.7 %pick4.1 = (bf16[1,4,128,128]{3,2,1,0:T(8,128)(2,1)S(1)}, bf16[1,4,128,128]{3,2,1,0:T(8,128)(2,1)S(1)}, f32[1,8,128]{2,1,0:T(8,128)S(1)}, bf16[1,4,128,128]{3,2,...) custom-call(s32[4]{0:T(128)S(1)} %pad_add_fusion.pos, ...), custom_call_target="tpu_custom_call" | custom-call | flops 1048576 | bytes 9800000 | tf_op jit(solution)/shard_map/pick4/pallas_call | solution.py:392
  83.2 2.5 %send0.1 = bf16[4,256,512]{2,1,0:T(8,128)(2,1)S(1)} custom-call(bf16[1,4,128,128]{3,2,1,0:T(8,128)(2,1)S(1)} %get-tuple-element.234.refs_0_, bf16[1,4,128,128]{3,2,1,0:T(8,128)(2,1)S(1)} %get-tuple-element.235.refs_1_, f32[1,8,128]{2,1,0:T(8,128)S(1)} %get-tuple-element.236.refs_2_, bf16[2,4,128,128]{3,2,1,0:T(8,128)(2,1)S(1)} %get-tuple-element.237.refs_3_, ...), custom_call_target="tpu_custom_call" | custom-call | flops 1048576 | bytes 8750000 | tf_op jit(solution)/shard_map/send0/pallas_call | solution.py:447
  85.8 2.5 %send1.1 = bf16[4,256,512]{2,1,0:T(8,128)(2,1)S(1)} custom-call(bf16[1,4,128,128]{3,2,1,0:T(8,128)(2,1)S(1)} %get-tuple-element.261.refs_0_, bf16[1,4,128,128]{3,2,1,0:T(8,128)(2,1)S(1)} %get-tuple-element.262.refs_1_, f32[1,8,128]{2,1,0:T(8,128)S(1)} %get-tuple-element.263.refs_2_, bf16[2,4,128,128]{3,2,1,0:T(8,128)(2,1)S(1)} %get-tuple-element.264.refs_3_, ...), custom_call_target="tpu_custom_call" | custom-call | flops 1048576 | bytes 8750000 | tf_op jit(solution)/shard_map/send1/pallas_call | solution.py:447
  89.6 1.5 %collective-permute-done.13.other1 = bf16[4,256,512]{2,1,0:T(8,128)(2,1)S(1)} collective-permute-done((bf16[4,256,512]{2,1,0:T(8,128)(2,1)S(1)}, bf16[4,256,512]{2,1,0:T(8,128)(2,1)S(1)}, u32[]{:S(2)}, u32[]{:S(2)}) %collective-permute-start.13) | collective-permute-done | bytes 1048608 | tf_op jit(solution)/shard_map/ppermute | solution.py:27
  91.1 1.5 %collective-permute-done.12.other0 = bf16[4,256,512]{2,1,0:T(8,128)(2,1)S(1)} collective-permute-done((bf16[4,256,512]{2,1,0:T(8,128)(2,1)S(1)}, bf16[4,256,512]{2,1,0:T(8,128)(2,1)S(1)}, u32[]{:S(2)}, u32[]{:S(2)}) %collective-permute-start.12) | collective-permute-done | bytes 1048608 | tf_op jit(solution)/shard_map/ppermute | solution.py:27
  92.6 6.3 %keep.1 = (f32[512,512]{1,0:T(8,128)S(1)}, bf16[512,512]{1,0:T(8,128)(2,1)}, bf16[512,512]{1,0:T(8,128)(2,1)}, bf16[512,512]{1,0:T(8,128)(2,1)}, f32[8,128]{1,0:T(8,128)}) custom-call(bf16[4,256,512]{2,1,0:T(8,128)(2,1)S(1)} %collective-permute-done.12.other0, bf16[4,256,512]{2,1,0:T(8,128)(2,1)S(1)} %collective-permute-done.13.other1, ...), custom_call_target="tpu_custom_call" | custom-call | flops 1048576 | bytes 22050000 | tf_op jit(solution)/shard_map/keep/pallas_call | solution.py:452
  98.9 1.0 copy-done.5
  99.9 1.5 %collective-permute-start.14 = (bf16[512,512]{1,0:T(8,128)(2,1)}, bf16[512,512]{1,0:T(8,128)(2,1)S(1)}, u32[]{:S(2)}, u32[]{:S(2)}) collective-permute-start(bf16[512,512]{1,0:T(8,128)(2,1)} %get-tuple-element.307), channel_id=1, source_target_pairs={{0,8},{8,16},{16,24},{24,0},{1,9},{9,17},{17,25},{25,1},{2,10},{10... | collective-permute-start | bytes 1572872 | tf_op jit(solution)/shard_map/ppermute | solution.py:27
  101.4 2.7 %collective-permute-start.15 = (bf16[512,512]{1,0:T(8,128)(2,1)}, bf16[512,512]{1,0:T(8,128)(2,1)S(1)}, u32[]{:S(2)}, u32[]{:S(2)}) collective-permute-start(bf16[512,512]{1,0:T(8,128)(2,1)} %get-tuple-element.308), channel_id=1, source_target_pairs={{0,16},{8,24},{16,0},{24,8},{1,17},{9,25},{17,1},{25,9},{2,18},{10... | collective-permute-start | bytes 1572872 | tf_op jit(solution)/shard_map/ppermute | solution.py:27
  104.1 1.4 collective-permute-start.16
  106.4 4.1 %all-to-all-start = ((bf16[8,16,1024]{2,1,0:T(8,128)(2,1)}), bf16[8,16,1024]{2,1,0:T(8,128)(2,1)S(1)}, u32[]{:S(2)}, u32[]{:S(2)}) async-start(bf16[8,16,1024]{2,1,0:T(8,128)(2,1)} %convert_element_type.60), calls=%async_computation | async-start | bytes 524288 | tf_op jit(solution)/shard_map/all_to_all | solution.py:467
  110.5 1.0 convert_element_type.62
  111.5 1.1 copy.19
  112.9 1.6 %leave.1 = (f32[520,128]{1,0:T(8,128)S(1)}, f32[520,128]{1,0:T(8,128)S(1)}, f32[520,128]{1,0:T(8,128)S(1)}) custom-call(s32[256]{0:T(256)S(1)} %bitcast.40, s32[256]{0:T(256)S(1)} %fusion.9.goal_s, f32[2048]{0:T(1024)S(1)} %bitcast.35, f32[2048,128]{1,0:T(8,128)S(1)} %bitcast.32), custom_call_target="tpu_custom_call" | custom-call | flops 1048576 | bytes 5600000 | tf_op jit(solution)/shard_map/leave/pallas_call | solution.py:488
  114.5 0.9 collective-permute-done.14.refs_1_
  115.4 12.1 %collective-permute-done.15.refs_2_ = bf16[512,512]{1,0:T(8,128)(2,1)S(1)} collective-permute-done((bf16[512,512]{1,0:T(8,128)(2,1)}, bf16[512,512]{1,0:T(8,128)(2,1)S(1)}, u32[]{:S(2)}, u32[]{:S(2)}) %collective-permute-start.15) | collective-permute-done | bytes 524320 | tf_op jit(solution)/shard_map/ppermute | solution.py:27
  129.1 1.2 copy-done.6
  130.3 1.0 copy-done.8
  131.3 1.0 copy-done.10
  132.4 2.0 %evict.1 = (bf16[2048,256]{1,0:T(8,128)(2,1)S(1)}, f32[136,128]{1,0:T(8,128)S(1)}, f32[136,128]{1,0:T(8,128)}, f32[136,128]{1,0:T(8,128)}, f32[136,128]{1,0:T(8,128)}) custom-call(f32[1,2048]{1,0:T(1,128)S(1)} %convert_element_type.64.slot_map, f32[520,128]{1,0:T(8,128)S(1)} %get-tuple-element.231.slot_in, f32[520,128]{1,0:T(8,128)S(1)} %get-tuple-element.232.weight, ...), custom_call_target="tpu_custom_call" | custom-call | flops 1048576 | bytes 9450000 | tf_op jit(solution)/shard_map/evict/pallas_call | solution.py:496
  134.4 1.3 collective-permute-start.17
  135.7 1.6 %collective-permute-start.18 = (f32[136,128]{1,0:T(8,128)}, f32[136,128]{1,0:T(8,128)S(1)}, u32[]{:S(2)}, u32[]{:S(2)}) collective-permute-start(f32[136,128]{1,0:T(8,128)} %get-tuple-element.315), channel_id=1, source_target_pairs={{0,2},{1,3},{2,0},{3,1},{4,6},{5,7},{6,4},{7,5},{8,10},{9,11},{10,... | collective-permute-start | bytes 208904 | tf_op jit(solution)/shard_map/ppermute | solution.py:27
  137.3 1.6 %collective-permute-start.19 = (f32[136,128]{1,0:T(8,128)}, f32[136,128]{1,0:T(8,128)S(1)}, u32[]{:S(2)}, u32[]{:S(2)}) collective-permute-start(f32[136,128]{1,0:T(8,128)} %get-tuple-element.316), channel_id=1, source_target_pairs={{0,3},{1,0},{2,1},{3,2},{4,7},{5,4},{6,5},{7,6},{8,11},{9,8},{10,9... | collective-permute-start | bytes 208904 | tf_op jit(solution)/shard_map/ppermute | solution.py:27
  138.9 1.2 finish.1
  140.1 4.3 %update.1 = (f32[2048,128]{1,0:T(8,128)}, f32[16,128]{1,0:T(8,128)}) custom-call(f32[1,2048]{1,0:T(1,128)S(1)} %convert_element_type.64.slot_map, bf16[2048,256]{1,0:T(8,128)(2,1)S(1)} %get-tuple-element.310.rhs, f32[2048,128]{1,0:T(8,128)S(1)} %bitcast.33, f32[16,128]{1,0:T(8,128)S(1)} %bitcast.36), custom_call_target="tpu_custom_call" | custom-call | flops 1048576 | bytes 15050000 | tf_op jit(solution)/shard_map/update/pallas_call | solution.py:505
  144.4 1.3 arrive.1
  (64 shorter events, 6.3 us)
Async XLA Ops:
  0.7 1.2 copy-start
  1.9 1.6 %copy-start.3 = (bf16[1024,1024]{1,0:T(8,128)(2,1)S(1)}, bf16[1024,1024]{1,0:T(8,128)(2,1)}, u32[]{:S(2)}) copy-start(bf16[1024,1024]{1,0:T(8,128)(2,1)} %w_up.1) | copy-start | bytes 6291460
  3.5 1.2 copy-start.4
  4.8 9.6 %copy-start.12 = (s32[2,512,8]{1,2,0:T(8,128)S(1)}, s32[2,512,8]{1,2,0:T(8,128)}, u32[]{:S(2)}) copy-start(s32[2,512,8]{1,2,0:T(8,128)} %param.16) | copy-start | bytes 98308
  4.8 9.6 %copy-start.13 = (s32[2,512,8]{1,2,0:T(8,128)S(1)}, s32[2,512,8]{1,2,0:T(8,128)}, u32[]{:S(2)}) copy-start(s32[2,512,8]{1,2,0:T(8,128)} %param.17) | copy-start | bytes 98308
  4.8 9.6 %copy-start.14 = (bf16[2,512,8]{1,2,0:T(8,128)(2,1)S(1)}, bf16[2,512,8]{1,2,0:T(8,128)(2,1)}, u32[]{:S(2)}) copy-start(bf16[2,512,8]{1,2,0:T(8,128)(2,1)} %param.18) | copy-start | bytes 49156
  4.8 9.6 %copy-start.15 = (s32[2,512]{1,0:T(2,128)S(1)}, s32[2,512]{1,0:T(2,128)}, u32[]{:S(2)}) copy-start(s32[2,512]{1,0:T(2,128)} %lens) | copy-start | bytes 12292
  9.3 19.8 %copy-start.1 = (bf16[512,1024]{1,0:T(8,128)(2,1)S(1)}, bf16[512,1024]{1,0:T(8,128)(2,1)}, u32[]{:S(2)}) copy-start(bf16[512,1024]{1,0:T(8,128)(2,1)} %pooled.3) | copy-start | bytes 3145732
  9.3 9.5 %collective-permute-start = (bf16[1024,128]{1,0:T(8,128)(2,1)S(1)}, bf16[1024,128]{1,0:T(8,128)(2,1)S(1)}, u32[]{:S(2)}, u32[]{:S(2)}) collective-permute-start(bf16[1024,128]{1,0:T(8,128)(2,1)S(1)} %get-tuple-element.163), channel_id=1, source_target_pairs={{0,1},{1,2},{2,3},{3,0},{4,5},{5,6},{6,7},{7,4},{8,9},{9,10},{10,1... | collective-permute-start | bytes 786440 | tf_op jit(solution)/shard_map/ppermute | solution.py:27
  11.0 10.7 %collective-permute-start.1 = (bf16[1024,128]{1,0:T(8,128)(2,1)S(1)}, bf16[1024,128]{1,0:T(8,128)(2,1)S(1)}, u32[]{:S(2)}, u32[]{:S(2)}) collective-permute-start(bf16[1024,128]{1,0:T(8,128)(2,1)S(1)} %get-tuple-element.164), channel_id=1, source_target_pairs={{0,2},{1,3},{2,0},{3,1},{4,6},{5,7},{6,4},{7,5},{8,10},{9,11},{10,... | collective-permute-start | bytes 786440 | tf_op jit(solution)/shard_map/ppermute | solution.py:27
  13.6 11.5 %collective-permute-start.2 = (bf16[1024,128]{1,0:T(8,128)(2,1)S(1)}, bf16[1024,128]{1,0:T(8,128)(2,1)S(1)}, u32[]{:S(2)}, u32[]{:S(2)}) collective-permute-start(bf16[1024,128]{1,0:T(8,128)(2,1)S(1)} %get-tuple-element.165), channel_id=1, source_target_pairs={{0,3},{1,0},{2,1},{3,2},{4,7},{5,4},{6,5},{7,6},{8,11},{9,8},{10,9... | collective-permute-start | bytes 786440 | tf_op jit(solution)/shard_map/ppermute | solution.py:27
  25.3 1.7 %collective-permute-start.3 = (bf16[1280,128]{1,0:T(8,128)(2,1)S(1)}, bf16[1280,128]{1,0:T(8,128)(2,1)S(1)}, u32[]{:S(2)}, u32[]{:S(2)}) collective-permute-start(bf16[1280,128]{1,0:T(8,128)(2,1)S(1)} %own.1.refs_0_), channel_id=1, source_target_pairs={{0,4},{4,0},{1,5},{5,1},{2,6},{6,2},{3,7},{7,3},{8,12},{12,8},{9,1... | collective-permute-start | bytes 983048 | tf_op jit(solution)/shard_map/ppermute | solution.py:27
  27.1 14.5 %collective-permute-start.4 = (bf16[2,1280,128]{2,1,0:T(8,128)(2,1)S(1)}, bf16[2,1280,128]{2,1,0:T(8,128)(2,1)S(1)}, u32[]{:S(2)}, u32[]{:S(2)}) collective-permute-start(bf16[2,1280,128]{2,1,0:T(8,128)(2,1)S(1)} %pad_maximum_fusion), channel_id=1, source_target_pairs={{0,32},{32,64},{64,96},{96,128},{128,160},{160,192},{192,224},{224... | collective-permute-start | bytes 1966088 | tf_op jit(solution)/shard_map/ppermute | solution.py:411
  41.6 23.7 %collective-permute-start.5 = (f32[4,8,16,1024]{3,2,1,0:T(8,128)S(1)}, f32[4,8,16,1024]{3,2,1,0:T(8,128)S(1)}, u32[]{:S(2)}, u32[]{:S(2)}) collective-permute-start(f32[4,8,16,1024]{3,2,1,0:T(8,128)S(1)} %get-tuple-element.190), channel_id=1, source_target_pairs={{0,4},{4,0},{1,5},{5,1},{2,6},{6,2},{3,7},{7,3},{8,12},{12,8},{9,1... | collective-permute-start | bytes 6291464 | tf_op jit(solution)/shard_map/ppermute | solution.py:27
  41.6 11.8 %collective-permute-start.6 = (bf16[2,1280,128]{2,1,0:T(8,128)(2,1)S(1)}, bf16[2,1280,128]{2,1,0:T(8,128)(2,1)S(1)}, u32[]{:S(2)}, u32[]{:S(2)}) collective-permute-start(bf16[2,1280,128]{2,1,0:T(8,128)(2,1)S(1)} %collective-permute-done.4.refs_0_), channel_id=1, source_target_pairs={{0,32},{32,64},{64,96},{96,128},{128,160},{160,192},{192,224},{224... | collective-permute-start | bytes 1966088 | tf_op jit(solution)/shard_map/ppermute | solution.py:411
  53.4 11.8 %collective-permute-start.7 = (bf16[2,1280,128]{2,1,0:T(8,128)(2,1)S(1)}, bf16[2,1280,128]{2,1,0:T(8,128)(2,1)S(1)}, u32[]{:S(2)}, u32[]{:S(2)}) collective-permute-start(bf16[2,1280,128]{2,1,0:T(8,128)(2,1)S(1)} %collective-permute-done.6.refs_0_), channel_id=1, source_target_pairs={{0,32},{32,64},{64,96},{96,128},{128,160},{160,192},{192,224},{224... | collective-permute-start | bytes 1966088 | tf_op jit(solution)/shard_map/ppermute | solution.py:411
  65.2 11.8 %collective-permute-start.8 = (bf16[1280,128]{1,0:T(8,128)(2,1)S(1)}, bf16[1280,128]{1,0:T(8,128)(2,1)S(1)}, u32[]{:S(2)}, u32[]{:S(2)}) collective-permute-start(bf16[1280,128]{1,0:T(8,128)(2,1)S(1)} %slice_bitcast_fusion.1), channel_id=1, source_target_pairs={{0,32},{32,64},{64,96},{96,128},{128,160},{160,192},{192,224},{224... | collective-permute-start | bytes 983048 | tf_op jit(solution)/shard_map/ppermute | solution.py:411
  66.1 10.9 %collective-permute-start.10 = (bf16[8,16,1024]{2,1,0:T(8,128)(2,1)S(1)}, bf16[8,16,1024]{2,1,0:T(8,128)(2,1)S(1)}, u32[]{:S(2)}, u32[]{:S(2)}) collective-permute-start(bf16[8,16,1024]{2,1,0:T(8,128)(2,1)S(1)} %get-tuple-element.322), channel_id=1, source_target_pairs={{0,16},{8,24},{16,0},{24,8},{1,17},{9,25},{17,1},{25,9},{2,18},{10... | collective-permute-start | bytes 786440 | tf_op jit(solution)/shard_map/ppermute | solution.py:27
  69.2 12.4 %collective-permute-start.11 = (bf16[8,16,1024]{2,1,0:T(8,128)(2,1)S(1)}, bf16[8,16,1024]{2,1,0:T(8,128)(2,1)S(1)}, u32[]{:S(2)}, u32[]{:S(2)}) collective-permute-start(bf16[8,16,1024]{2,1,0:T(8,128)(2,1)S(1)} %get-tuple-element.321), channel_id=1, source_target_pairs={{0,24},{8,0},{16,8},{24,16},{1,25},{9,1},{17,9},{25,17},{2,26},{10... | collective-permute-start | bytes 786440 | tf_op jit(solution)/shard_map/ppermute | solution.py:27
  70.3 11.2 %collective-permute-start.9 = (bf16[8,16,1024]{2,1,0:T(8,128)(2,1)S(1)}, bf16[8,16,1024]{2,1,0:T(8,128)(2,1)S(1)}, u32[]{:S(2)}, u32[]{:S(2)}) collective-permute-start(bf16[8,16,1024]{2,1,0:T(8,128)(2,1)S(1)} %get-tuple-element.323), channel_id=1, source_target_pairs={{0,8},{8,16},{16,24},{24,0},{1,9},{9,17},{17,25},{25,1},{2,10},{10... | collective-permute-start | bytes 786440 | tf_op jit(solution)/shard_map/ppermute | solution.py:27
  88.3 2.7 %collective-permute-start.13 = (bf16[4,256,512]{2,1,0:T(8,128)(2,1)S(1)}, bf16[4,256,512]{2,1,0:T(8,128)(2,1)S(1)}, u32[]{:S(2)}, u32[]{:S(2)}) collective-permute-start(bf16[4,256,512]{2,1,0:T(8,128)(2,1)S(1)} %send1.1), channel_id=1, source_target_pairs={{0,4},{4,0},{1,5},{5,1},{2,6},{6,2},{3,7},{7,3},{8,12},{12,8},{9,1... | collective-permute-start | bytes 3145736 | tf_op jit(solution)/shard_map/ppermute | solution.py:27
  88.4 4.1 %collective-permute-start.12 = (bf16[4,256,512]{2,1,0:T(8,128)(2,1)S(1)}, bf16[4,256,512]{2,1,0:T(8,128)(2,1)S(1)}, u32[]{:S(2)}, u32[]{:S(2)}) collective-permute-start(bf16[4,256,512]{2,1,0:T(8,128)(2,1)S(1)} %send0.1), channel_id=1, source_target_pairs={{0,4},{4,0},{1,5},{5,1},{2,6},{6,2},{3,7},{7,3},{8,12},{12,8},{9,1... | collective-permute-start | bytes 3145736 | tf_op jit(solution)/shard_map/ppermute | solution.py:27
  98.9 1.0 copy-start.5
  99.9 10.6 %copy-start.17 = (s32[1,1,2048]{2,1,0:T(1,128)S(1)}, s32[1,1,2048]{2,1,0:T(1,128)}, u32[]{:S(2)}) copy-start(s32[1,1,2048]{2,1,0:T(1,128)} %param.20) | copy-start | bytes 24580
  99.9 12.7 %copy-start.18 = (s32[1,1,256]{2,1,0:T(1,128)S(1)}, s32[1,1,256]{2,1,0:T(1,128)}, u32[]{:S(2)}) copy-start(s32[1,1,256]{2,1,0:T(1,128)} %param.24) | copy-start | bytes 3076
  99.9 12.9 %copy-start.2 = (f32[1,1,2048,128]{3,2,1,0:T(8,128)S(1)}, f32[1,1,2048,128]{3,2,1,0:T(8,128)}, u32[]{:S(2)}) copy-start(f32[1,1,2048,128]{3,2,1,0:T(8,128)} %param.21) | copy-start | bytes 3145732
  99.9 13.0 %copy-start.11 = (f32[1,1,2048]{2,1,0:T(1,128)S(1)}, f32[1,1,2048]{2,1,0:T(1,128)}, u32[]{:S(2)}) copy-start(f32[1,1,2048]{2,1,0:T(1,128)} %param.22) | copy-start | bytes 24580
  99.9 13.0 %copy-start.16 = (s32[1,1,256]{2,1,0:T(1,128)S(1)}, s32[1,1,256]{2,1,0:T(1,128)}, u32[]{:S(2)}) copy-start(s32[1,1,256]{2,1,0:T(1,128)} %param.23) | copy-start | bytes 3076
  99.9 15.5 %collective-permute-start.14 = (bf16[512,512]{1,0:T(8,128)(2,1)}, bf16[512,512]{1,0:T(8,128)(2,1)S(1)}, u32[]{:S(2)}, u32[]{:S(2)}) collective-permute-start(bf16[512,512]{1,0:T(8,128)(2,1)} %get-tuple-element.307), channel_id=1, source_target_pairs={{0,8},{8,16},{16,24},{24,0},{1,9},{9,17},{17,25},{25,1},{2,10},{10... | collective-permute-start | bytes 1572872 | tf_op jit(solution)/shard_map/ppermute | solution.py:27
  101.4 26.0 %collective-permute-start.15 = (bf16[512,512]{1,0:T(8,128)(2,1)}, bf16[512,512]{1,0:T(8,128)(2,1)S(1)}, u32[]{:S(2)}, u32[]{:S(2)}) collective-permute-start(bf16[512,512]{1,0:T(8,128)(2,1)} %get-tuple-element.308), channel_id=1, source_target_pairs={{0,16},{8,24},{16,0},{24,8},{1,17},{9,25},{17,1},{25,9},{2,18},{10... | collective-permute-start | bytes 1572872 | tf_op jit(solution)/shard_map/ppermute | solution.py:27
  104.1 24.2 %collective-permute-start.16 = (bf16[512,512]{1,0:T(8,128)(2,1)}, bf16[512,512]{1,0:T(8,128)(2,1)S(1)}, u32[]{:S(2)}, u32[]{:S(2)}) collective-permute-start(bf16[512,512]{1,0:T(8,128)(2,1)} %get-tuple-element.309), channel_id=1, source_target_pairs={{0,24},{8,0},{16,8},{24,16},{1,25},{9,1},{17,9},{25,17},{2,26},{10... | collective-permute-start | bytes 1572872 | tf_op jit(solution)/shard_map/ppermute | solution.py:27
  106.4 32.5 %all-to-all-start = ((bf16[8,16,1024]{2,1,0:T(8,128)(2,1)}), bf16[8,16,1024]{2,1,0:T(8,128)(2,1)S(1)}, u32[]{:S(2)}, u32[]{:S(2)}) async-start(bf16[8,16,1024]{2,1,0:T(8,128)(2,1)} %convert_element_type.60), calls=%async_computation | async-start | bytes 524288 | tf_op jit(solution)/shard_map/all_to_all | solution.py:467
  127.4 0.8 copy-start.7
  128.3 0.8 copy-start.9
  129.1 1.2 copy-start.6
  130.3 1.0 copy-start.8
  131.3 1.0 copy-start.10
  134.4 10.0 %collective-permute-start.17 = (f32[136,128]{1,0:T(8,128)}, f32[136,128]{1,0:T(8,128)S(1)}, u32[]{:S(2)}, u32[]{:S(2)}) collective-permute-start(f32[136,128]{1,0:T(8,128)} %get-tuple-element.314), channel_id=1, source_target_pairs={{0,1},{1,2},{2,3},{3,0},{4,5},{5,6},{6,7},{7,4},{8,9},{9,10},{10,1... | collective-permute-start | bytes 208904 | tf_op jit(solution)/shard_map/ppermute | solution.py:27
  135.7 8.7 %collective-permute-start.18 = (f32[136,128]{1,0:T(8,128)}, f32[136,128]{1,0:T(8,128)S(1)}, u32[]{:S(2)}, u32[]{:S(2)}) collective-permute-start(f32[136,128]{1,0:T(8,128)} %get-tuple-element.315), channel_id=1, source_target_pairs={{0,2},{1,3},{2,0},{3,1},{4,6},{5,7},{6,4},{7,5},{8,10},{9,11},{10,... | collective-permute-start | bytes 208904 | tf_op jit(solution)/shard_map/ppermute | solution.py:27
  137.3 7.1 %collective-permute-start.19 = (f32[136,128]{1,0:T(8,128)}, f32[136,128]{1,0:T(8,128)S(1)}, u32[]{:S(2)}, u32[]{:S(2)}) collective-permute-start(f32[136,128]{1,0:T(8,128)} %get-tuple-element.316), channel_id=1, source_target_pairs={{0,3},{1,0},{2,1},{3,2},{4,7},{5,4},{6,5},{7,6},{8,11},{9,8},{10,9... | collective-permute-start | bytes 208904 | tf_op jit(solution)/shard_map/ppermute | solution.py:27

commit v4 on v2

--- a/solution.py
+++ b/solution.py
@@ -27,14 +27,14 @@
     return lax.ppermute(x, axis, [(i, (i + step) % size) for i in range(size)])
 
 
-def call(body, ins, outs, scratch, flops, moved, name):
+def call(body, ins, outs, scratch, flops, moved, name, limit=20):
     return pl.pallas_call(
         body,
         in_specs=ins,
         out_specs=[VMEM] * len(outs),
         out_shape=outs,
         scratch_shapes=scratch,
-        compiler_params=pltpu.CompilerParams(vmem_limit_bytes=20 << 20),
+        compiler_params=pltpu.CompilerParams(vmem_limit_bytes=limit << 20),
         cost_estimate=pl.CostEstimate(flops=flops, bytes_accessed=moved, transcendentals=0),
         name=name,
     )
@@ -245,10 +245,11 @@
     out[...] = acc
 
 
-def leave_kernel(slots_s, goal_s, accum_s, weight, slot_out, weight_out, accum_out):
-    slot_out[...] = jnp.full_like(slot_out, -1.0)
-    weight_out[...] = jnp.zeros_like(weight_out)
-    accum_out[...] = jnp.zeros_like(accum_out)
+def leave_kernel(slots_s, goal_s, accum_s, weight, out):
+    slot_out, weight_out, accum_out = (out.at[i] for i in range(3))
+    slot_out[...] = jnp.full(slot_out.shape, -1.0, F32)
+    weight_out[...] = jnp.zeros(slot_out.shape, F32)
+    accum_out[...] = jnp.zeros(slot_out.shape, F32)
 
     def leave(i, carry):
         for j in range(4):
@@ -266,7 +267,8 @@
     return lax.broadcasted_iota(I32, (128, 128), 0) == lax.broadcasted_iota(I32, (128, 128), 1)
 
 
-def evict_kernel(slot_map, slot_in, weight, accum, *refs):
+def evict_kernel(slot_map, leaving, *refs):
+    slot_in, weight, accum = (leaving.at[i] for i in range(3))
     parts, rhs, held, pick, sums = refs[:4], refs[4], refs[5:9], refs[9], refs[10]
     for t in range(2):
         at = slice(t * 256, (t + 1) * 256)
@@ -368,6 +370,7 @@
         2 << 30,
         6 << 20,
         "top",
+        60,
     )(pos, pooled, w_up, grad_out)
     got = [shifted(parts[k], H, k) for k in (1, 2, 3)]
 
@@ -422,24 +425,23 @@
         "grad",
     )(pos, pooled, delta)
     near = (up, down)
-    (up, down), (grad, there) = together((up, down), (grad, there))
+    picked = [pick(0, (own,))]
+    near, (grad, there), picked[0] = together(near, (grad, there), picked[0])
+    up, down = near
     there = shifted(there, C, 1)
-    up, down = shifted(up, Z, 1), shifted(down, Z, -1)
-    picked = [pick(0, (own,))]
-    mid = (up, down)
-    (up, down), near, *picked = together((up, down), near, *picked)
-    up, down = shifted(up, Z, 1), shifted(down, Z, -1)
+    mid = (shifted(up, Z, 1), shifted(down, Z, -1))
     grad_x = grad + there
     total, blocks = grad_x[0], [grad_x[k].astype(BF16) for k in (1, 2, 3)]
-    near, (total,), blocks = together(near, (total,), blocks)
+    mid, near, (total,), blocks = together(mid, near, (total,), blocks)
+    up, down = mid
     got_x = [shifted(blocks[k - 1], X, k) for k in (1, 2, 3)]
+    far = (shifted(up, Z, 1), shifted(down, Z, -1))
     picked.append(pick(1, near))
-    far = (up, down)
-    (up, down), mid, picked[1] = together((up, down), mid, picked[1])
+    picked.append(pick(2, mid))
+    far, picked[1], picked[2] = together(far, picked[1], picked[2])
+    up, down = far
     part = bags + 128
     last = (shifted(up[:part], Z, 1), shifted(down[part:], Z, -1))
-    picked.append(pick(2, mid))
-    far, picked[2] = together(far, picked[2])
     picked.append(pick(3, far))
     last, got_x, picked[3] = together(last, got_x, picked[3])
     picked.append(pick(4, last))
@@ -497,16 +499,15 @@
     leaving = call(
         leave_kernel,
         [SMEM] * 3 + [VMEM],
-        [shape((520, 128), F32)] * 3,
+        [shape((3, 520, 128), F32)],
         [],
         1 << 10,
         1 << 20,
         "leave",
     )(evict_slots.reshape(-1), goal, cache_accum.reshape(-1), cache_weight[0, 0])
-    arrived, leaving = together(arrived, leaving)
     rhs, *held = call(
         evict_kernel,
-        [VMEM] * 8,
+        [VMEM] * 6,
         [shape((2048, 256), BF16)] + [shape((HELD, 128), F32)] * 4,
         [pltpu.VMEM((512, 2048), BF16), pltpu.VMEM((512, 256), F32)],
         1 << 29,

time: 133 us -> 132 us (level)
  local copies, waits for them, and re-layouts: 11.2 us -> 5.04 us
  Pallas kernels: 41.4 us -> 43.9 us
  waiting for transfers between devices: 35.1 us -> 37.1 us
    unnamed x38 -> x30, local copies, waits for them, and re-layouts: 9.05 us -> 4.51 us
    all_to_all x1, waiting for transfers between devices: 5.29 us -> 9.34 us  [on_device(): lax.all_to_all(total.astype(BF16), Z, split_axis=0, concat_axis=0, tiled=...]
    pallas_call x1, Pallas kernels: 4.53 us -> 7.23 us  [on_device(): call(top_kernel, [SMEM, VMEM, VMEM, VMEM], [shape((bags, 1024), BF16), sh...]
    ppermute x23, waiting for transfers between devices: 29.8 us -> 27.8 us  [shifted(): return lax.ppermute(x, axis, [(i, (i + step) % size) for i in range(size)])]
    convert_element_type x3, local copies, waits for them, and re-layouts: 2.05 us -> 0.39 us  [on_device(): jnp.swapaxes(slot_map.reshape(2, 256, 4), 1, 2).reshape(1, 2048).astype(F32)]
    all_to_all x1, starting transfers between devices: 4.61 us -> 6.07 us  [on_device(): lax.all_to_all(total.astype(BF16), Z, split_axis=0, concat_axis=0, tiled=...]
  transfers between devices with their start and end apart: 24 -> 24, of which waited for: 10 -> 12; matrix products, arithmetic and copies ran while one was open for 3% -> 2% of each run, Pallas kernels for 15% -> 15%
where the time goes in v4:
time: 132 us
  Pallas kernels  43.9 us (33%)
  starting transfers between devices  41.7 us (32%)
  waiting for transfers between devices  37.1 us (28%)
  local copies, waits for them, and re-layouts  5.04 us (4%)
  other arithmetic  2.11 us (2%)
  between operations  1.57 us (1%)
    ppermute x23, starting transfers between devices, shifted(): return lax.ppermute(x, axis, [(i, (i + step) % size) for i in range(size)])  35.7 us
    ppermute x23, waiting for transfers between devices, shifted(): return lax.ppermute(x, axis, [(i, (i + step) % size) for i in range(size)])  27.8 us
    pallas_call x5, Pallas kernels, pick(): call(functools.partial(pick_kernel, count), [SMEM, VMEM] + [VMEM] * len(b...  11.9 us
    all_to_all x1, waiting for transfers between devices, on_device(): lax.all_to_all(total.astype(BF16), Z, split_axis=0, concat_axis=0, tiled=...  9.34 us
    pallas_call x1, Pallas kernels, on_device(): call(top_kernel, [SMEM, VMEM, VMEM, VMEM], [shape((bags, 1024), BF16), sh...  7.23 us
    pallas_call x1, Pallas kernels, on_device(): call(keep_kernel, [VMEM] * 32, [shape((512, 512), F32)] + [shape((512, 51...  6.26 us
    all_to_all x1, starting transfers between devices, on_device(): lax.all_to_all(total.astype(BF16), Z, split_axis=0, concat_axis=0, tiled=...  6.07 us
    pallas_call x2, Pallas kernels, on_device(): call(send_kernel, [VMEM] * 15, [shape((4, 256, 512), BF16)], work, 4 << 3...  5.04 us
  transfers between devices with their start and end apart: 24, of which 12 were waited for; matrix products, arithmetic and copies ran while one was open for 2% of the time, Pallas kernels for 15%

profile of v4, /device:TPU:8, one launch (start us, length us, event | category | flops | bytes accessed | tf_op | source)
XLA Modules:
  0.0 131.7 jit_solution(11164389260585060364)
XLA Ops:
  1.3 7.2 %top.1 = (bf16[512,1024]{1,0:T(8,128)(2,1)}, f32[1024,128]{1,0:T(8,128)}, bf16[1024,128]{1,0:T(8,128)(2,1)}, bf16[1024,128]{1,0:T(8,128)(2,1)}, bf16[1024,128]{1,0:T(8,128)(2,1)}) custom-call(s32[4]{0:T(128)} %pad_add_fusion.pos, bf16[512,1024]{1,0:T(8,128)(2,1)} %pooled.3, bf16[1024,1024]{1,0:T(8,128)(2,1)} %w_up.1, bf16[512,1024]{1,0:T(8,128)(2,1)} %grad_out.1), custom_call_target="tpu_custom_call" | custom-call | flops 2147483648 | bytes 6291456 | tf_op jit(solution)/shard_map/top/pallas_call | solution.py:365
  8.6 1.6 %collective-permute-start = (bf16[1024,128]{1,0:T(8,128)(2,1)}, bf16[1024,128]{1,0:T(8,128)(2,1)S(1)}, u32[]{:S(2)}, u32[]{:S(2)}) collective-permute-start(bf16[1024,128]{1,0:T(8,128)(2,1)} %get-tuple-element.179), channel_id=1, source_target_pairs={{0,1},{1,2},{2,3},{3,0},{4,5},{5,6},{6,7},{7,4},{8,9},{9,10},{10,1... | collective-permute-start | bytes 786440 | tf_op jit(solution)/shard_map/ppermute | solution.py:27
  10.1 2.7 %collective-permute-start.1 = (bf16[1024,128]{1,0:T(8,128)(2,1)}, bf16[1024,128]{1,0:T(8,128)(2,1)S(1)}, u32[]{:S(2)}, u32[]{:S(2)}) collective-permute-start(bf16[1024,128]{1,0:T(8,128)(2,1)} %get-tuple-element.180), channel_id=1, source_target_pairs={{0,2},{1,3},{2,0},{3,1},{4,6},{5,7},{6,4},{7,5},{8,10},{9,11},{10,... | collective-permute-start | bytes 786440 | tf_op jit(solution)/shard_map/ppermute | solution.py:27
  13.6 4.6 %collective-permute-done.one = bf16[1024,128]{1,0:T(8,128)(2,1)S(1)} collective-permute-done((bf16[1024,128]{1,0:T(8,128)(2,1)}, bf16[1024,128]{1,0:T(8,128)(2,1)S(1)}, u32[]{:S(2)}, u32[]{:S(2)}) %collective-permute-start) | collective-permute-done | bytes 262176 | tf_op jit(solution)/shard_map/ppermute | solution.py:27
  18.2 2.9 %collective-permute-done.1.two = bf16[1024,128]{1,0:T(8,128)(2,1)S(1)} collective-permute-done((bf16[1024,128]{1,0:T(8,128)(2,1)}, bf16[1024,128]{1,0:T(8,128)(2,1)S(1)}, u32[]{:S(2)}, u32[]{:S(2)}) %collective-permute-start.1) | collective-permute-done | bytes 262176 | tf_op jit(solution)/shard_map/ppermute | solution.py:27
  21.1 3.4 %collective-permute-done.2.three = bf16[1024,128]{1,0:T(8,128)(2,1)S(1)} collective-permute-done((bf16[1024,128]{1,0:T(8,128)(2,1)}, bf16[1024,128]{1,0:T(8,128)(2,1)S(1)}, u32[]{:S(2)}, u32[]{:S(2)}) %collective-permute-start.2) | collective-permute-done | bytes 262176 | tf_op jit(solution)/shard_map/ppermute | solution.py:27
  24.5 1.0 copy-done.3
  25.6 2.0 %collective-permute-start.3 = (bf16[1280,128]{1,0:T(8,128)(2,1)S(1)}, bf16[1280,128]{1,0:T(8,128)(2,1)S(1)}, u32[]{:S(2)}, u32[]{:S(2)}) collective-permute-start(bf16[1280,128]{1,0:T(8,128)(2,1)S(1)} %own.1.refs_0_), channel_id=1, source_target_pairs={{0,32},{32,64},{64,96},{96,128},{128,160},{160,192},{192,224},{224... | collective-permute-start | bytes 983048 | tf_op jit(solution)/shard_map/ppermute | solution.py:27
  27.6 4.0 %collective-permute-start.4 = (bf16[1280,128]{1,0:T(8,128)(2,1)S(1)}, bf16[1280,128]{1,0:T(8,128)(2,1)S(1)}, u32[]{:S(2)}, u32[]{:S(2)}) collective-permute-start(bf16[1280,128]{1,0:T(8,128)(2,1)S(1)} %own.1.refs_0_), channel_id=1, source_target_pairs={{0,224},{32,0},{64,32},{96,64},{128,96},{160,128},{192,160},{224,1... | collective-permute-start | bytes 983048 | tf_op jit(solution)/shard_map/ppermute | solution.py:27
  31.7 1.2 copy-done.12
  32.9 2.3 %grad.1 = (f32[4,8,16,1024]{3,2,1,0:T(8,128)S(1)}, f32[4,8,16,1024]{3,2,1,0:T(8,128)S(1)}) custom-call(s32[4]{0:T(128)S(1)} %copy-done.8, bf16[512,1024]{1,0:T(8,128)(2,1)S(1)} %copy-done.11, bf16[512,1024]{1,0:T(8,128)(2,1)S(1)} %copy-done.12), custom_call_target="tpu_custom_call" | custom-call | flops 1073741824 | bytes 6291456 | tf_op jit(solution)/shard_map/grad/pallas_call | solution.py:418
  35.2 1.7 %pick0.1 = (bf16[1,4,128,128]{3,2,1,0:T(8,128)(2,1)S(1)}, bf16[1,4,128,128]{3,2,1,0:T(8,128)(2,1)S(1)}, f32[1,8,128]{2,1,0:T(8,128)S(1)}, bf16[1,4,128,128]{3,2,...) custom-call(s32[4]{0:T(128)S(1)} %copy-done.8, ...), custom_call_target="tpu_custom_call" | custom-call | flops 1073741824 | bytes 4194304 | tf_op jit(solution)/shard_map/pick0/pallas_call | solution.py:400
  36.9 1.7 %collective-permute-done.3.refs_0_ = bf16[1280,128]{1,0:T(8,128)(2,1)S(1)} collective-permute-done((bf16[1280,128]{1,0:T(8,128)(2,1)S(1)}, bf16[1280,128]{1,0:T(8,128)(2,1)S(1)}, u32[]{:S(2)}, u32[]{:S(2)}) %collective-permute-start.3) | collective-permute-done | bytes 327712 | tf_op jit(solution)/shard_map/ppermute | solution.py:27
  38.6 3.2 %collective-permute-start.6 = (bf16[1280,128]{1,0:T(8,128)(2,1)S(1)}, bf16[1280,128]{1,0:T(8,128)(2,1)S(1)}, u32[]{:S(2)}, u32[]{:S(2)}) collective-permute-start(bf16[1280,128]{1,0:T(8,128)(2,1)S(1)} %collective-permute-done.4.refs_1_), channel_id=1, source_target_pairs={{0,224},{32,0},{64,32},{96,64},{128,96},{160,128},{192,160},{224,1... | collective-permute-start | bytes 983048 | tf_op jit(solution)/shard_map/ppermute | solution.py:27
  41.9 0.9 collective-permute-done.7
  43.4 6.6 %collective-permute-done.5.refs_0_ = bf16[1280,128]{1,0:T(8,128)(2,1)S(1)} collective-permute-done((bf16[1280,128]{1,0:T(8,128)(2,1)S(1)}, bf16[1280,128]{1,0:T(8,128)(2,1)S(1)}, u32[]{:S(2)}, u32[]{:S(2)}) %collective-permute-start.5) | collective-permute-done | bytes 327712 | tf_op jit(solution)/shard_map/ppermute | solution.py:27
  50.0 2.4 %collective-permute-start.8 = (bf16[1280,128]{1,0:T(8,128)(2,1)S(1)}, bf16[1280,128]{1,0:T(8,128)(2,1)S(1)}, u32[]{:S(2)}, u32[]{:S(2)}) collective-permute-start(bf16[1280,128]{1,0:T(8,128)(2,1)S(1)} %collective-permute-done.5.refs_0_), channel_id=1, source_target_pairs={{0,32},{32,64},{64,96},{96,128},{128,160},{160,192},{192,224},{224... | collective-permute-start | bytes 983048 | tf_op jit(solution)/shard_map/ppermute | solution.py:27
  52.4 0.9 collective-permute-start.9
  53.3 1.5 %collective-permute-start.12 = (bf16[8,16,1024]{2,1,0:T(8,128)(2,1)S(1)}, bf16[8,16,1024]{2,1,0:T(8,128)(2,1)S(1)}, u32[]{:S(2)}, u32[]{:S(2)}) collective-permute-start(bf16[8,16,1024]{2,1,0:T(8,128)(2,1)S(1)} %get-tuple-element.249), channel_id=1, source_target_pairs={{0,8},{8,16},{16,24},{24,0},{1,9},{9,17},{17,25},{25,1},{2,10},{10... | collective-permute-start | bytes 786440 | tf_op jit(solution)/shard_map/ppermute | solution.py:27
  54.8 2.7 %collective-permute-start.13 = (bf16[8,16,1024]{2,1,0:T(8,128)(2,1)S(1)}, bf16[8,16,1024]{2,1,0:T(8,128)(2,1)S(1)}, u32[]{:S(2)}, u32[]{:S(2)}) collective-permute-start(bf16[8,16,1024]{2,1,0:T(8,128)(2,1)S(1)} %get-tuple-element.250), channel_id=1, source_target_pairs={{0,16},{8,24},{16,0},{24,8},{1,17},{9,25},{17,1},{25,9},{2,18},{10... | collective-permute-start | bytes 786440 | tf_op jit(solution)/shard_map/ppermute | solution.py:27
  57.5 1.4 %collective-permute-start.14 = (bf16[8,16,1024]{2,1,0:T(8,128)(2,1)S(1)}, bf16[8,16,1024]{2,1,0:T(8,128)(2,1)S(1)}, u32[]{:S(2)}, u32[]{:S(2)}) collective-permute-start(bf16[8,16,1024]{2,1,0:T(8,128)(2,1)S(1)} %get-tuple-element.251), channel_id=1, source_target_pairs={{0,24},{8,0},{16,8},{24,16},{1,25},{9,1},{17,9},{25,17},{2,26},{10... | collective-permute-start | bytes 786440 | tf_op jit(solution)/shard_map/ppermute | solution.py:27
  58.9 2.9 %pick2.1 = (bf16[2,4,128,128]{3,2,1,0:T(8,128)(2,1)S(1)}, bf16[2,4,128,128]{3,2,1,0:T(8,128)(2,1)S(1)}, f32[2,8,128]{2,1,0:T(8,128)S(1)}, bf16[2,4,128,128]{3,2,...) custom-call(s32[4]{0:T(128)S(1)} %copy-done.8, ...), custom_call_target="tpu_custom_call" | custom-call | flops 1073741824 | bytes 4194304 | tf_op jit(solution)/shard_map/pick2/pallas_call | solution.py:400
  61.8 2.9 %pick1.1 = (bf16[2,4,128,128]{3,2,1,0:T(8,128)(2,1)S(1)}, bf16[2,4,128,128]{3,2,1,0:T(8,128)(2,1)S(1)}, f32[2,8,128]{2,1,0:T(8,128)S(1)}, bf16[2,4,128,128]{3,2,...) custom-call(s32[4]{0:T(128)S(1)} %copy-done.8, ...), custom_call_target="tpu_custom_call" | custom-call | flops 1073741824 | bytes 4194304 | tf_op jit(solution)/shard_map/pick1/pallas_call | solution.py:400
  64.7 1.2 collective-permute-start.10
  66.0 2.2 %collective-permute-start.11 = (bf16[640,128]{1,0:T(8,128)(2,1)S(1)}, bf16[640,128]{1,0:T(8,128)(2,1)S(1)}, u32[]{:S(2)}, u32[]{:S(2)}) collective-permute-start(bf16[640,128]{1,0:T(8,128)(2,1)S(1)} %slice.26), channel_id=1, source_target_pairs={{0,224},{32,0},{64,32},{96,64},{128,96},{160,128},{192,160},{224,1... | collective-permute-start | bytes 491528 | tf_op jit(solution)/shard_map/ppermute | solution.py:27
  68.1 2.9 %pick3.1 = (bf16[2,4,128,128]{3,2,1,0:T(8,128)(2,1)S(1)}, bf16[2,4,128,128]{3,2,1,0:T(8,128)(2,1)S(1)}, f32[2,8,128]{2,1,0:T(8,128)S(1)}, bf16[2,4,128,128]{3,2,...) custom-call(s32[4]{0:T(128)S(1)} %copy-done.8, ...), custom_call_target="tpu_custom_call" | custom-call | flops 1073741824 | bytes 4194304 | tf_op jit(solution)/shard_map/pick3/pallas_call | solution.py:400
  71.3 1.7 %pick4.1 = (bf16[1,4,128,128]{3,2,1,0:T(8,128)(2,1)S(1)}, bf16[1,4,128,128]{3,2,1,0:T(8,128)(2,1)S(1)}, f32[1,8,128]{2,1,0:T(8,128)S(1)}, bf16[1,4,128,128]{3,2,...) custom-call(s32[4]{0:T(128)S(1)} %copy-done.8, ...), custom_call_target="tpu_custom_call" | custom-call | flops 1073741824 | bytes 4194304 | tf_op jit(solution)/shard_map/pick4/pallas_call | solution.py:400
  73.0 2.5 %send0.1 = bf16[4,256,512]{2,1,0:T(8,128)(2,1)S(1)} custom-call(bf16[1,4,128,128]{3,2,1,0:T(8,128)(2,1)S(1)} %get-tuple-element.206.refs_0_, bf16[1,4,128,128]{3,2,1,0:T(8,128)(2,1)S(1)} %get-tuple-element.207.refs_1_, f32[1,8,128]{2,1,0:T(8,128)S(1)} %get-tuple-element.208.refs_2_, bf16[2,4,128,128]{3,2,1,0:T(8,128)(2,1)S(1)} %get-tuple-element.241.refs_3_, ...), custom_call_target="tpu_custom_call" | custom-call | flops 4294967296 | bytes 5242880 | tf_op jit(solution)/shard_map/send0/pallas_call | solution.py:455
  75.6 2.5 %send1.1 = bf16[4,256,512]{2,1,0:T(8,128)(2,1)S(1)} custom-call(bf16[1,4,128,128]{3,2,1,0:T(8,128)(2,1)S(1)} %get-tuple-element.282.refs_0_, bf16[1,4,128,128]{3,2,1,0:T(8,128)(2,1)S(1)} %get-tuple-element.283.refs_1_, f32[1,8,128]{2,1,0:T(8,128)S(1)} %get-tuple-element.284.refs_2_, bf16[2,4,128,128]{3,2,1,0:T(8,128)(2,1)S(1)} %get-tuple-element.285.refs_3_, ...), custom_call_target="tpu_custom_call" | custom-call | flops 4294967296 | bytes 5242880 | tf_op jit(solution)/shard_map/send1/pallas_call | solution.py:455
  79.5 1.3 collective-permute-done.16.other1
  80.8 1.5 %collective-permute-done.15.other0 = bf16[4,256,512]{2,1,0:T(8,128)(2,1)S(1)} collective-permute-done((bf16[4,256,512]{2,1,0:T(8,128)(2,1)S(1)}, bf16[4,256,512]{2,1,0:T(8,128)(2,1)S(1)}, u32[]{:S(2)}, u32[]{:S(2)}) %collective-permute-start.15) | collective-permute-done | bytes 1048608 | tf_op jit(solution)/shard_map/ppermute | solution.py:27
  82.3 6.3 %keep.1 = (f32[512,512]{1,0:T(8,128)S(1)}, bf16[512,512]{1,0:T(8,128)(2,1)}, bf16[512,512]{1,0:T(8,128)(2,1)}, bf16[512,512]{1,0:T(8,128)(2,1)}) custom-call(bf16[4,256,512]{2,1,0:T(8,128)(2,1)S(1)} %collective-permute-done.15.other0, bf16[4,256,512]{2,1,0:T(8,128)(2,1)S(1)} %collective-permute-done.16.other1, ...), custom_call_target="tpu_custom_call" | custom-call | flops 8589934592 | bytes 10485760 | tf_op jit(solution)/shard_map/keep/pallas_call | solution.py:460
  88.6 1.0 copy-done.1
  90.2 0.9 collective-permute-start.18
  91.0 1.8 %collective-permute-start.19 = (bf16[512,512]{1,0:T(8,128)(2,1)}, bf16[512,512]{1,0:T(8,128)(2,1)}, u32[]{:S(2)}, u32[]{:S(2)}) collective-permute-start(bf16[512,512]{1,0:T(8,128)(2,1)} %get-tuple-element.341), channel_id=1, source_target_pairs={{0,24},{8,0},{16,8},{24,16},{1,25},{9,1},{17,9},{25,17},{2,26},{10... | collective-permute-start | bytes 1572872 | tf_op jit(solution)/shard_map/ppermute | solution.py:27
  92.8 0.7 convert_element_type.60
  93.6 6.1 %all-to-all-start = ((bf16[8,16,1024]{2,1,0:T(8,128)(2,1)}), bf16[8,16,1024]{2,1,0:T(8,128)(2,1)S(1)}, u32[]{:S(2)}, u32[]{:S(2)}) async-start(bf16[8,16,1024]{2,1,0:T(8,128)(2,1)} %convert_element_type.60), calls=%async_computation | async-start | bytes 524288 | tf_op jit(solution)/shard_map/all_to_all | solution.py:477
  100.4 1.6 %leave.1.leaving = f32[3,520,128]{2,1,0:T(8,128)S(1)} custom-call(s32[256]{0:T(256)S(1)} %bitcast.35, s32[256]{0:T(256)S(1)} %fusion.9.goal_s, f32[2048]{0:T(1024)S(1)} %bitcast.33, f32[2048,128]{1,0:T(8,128)S(1)} %bitcast.28), custom_call_target="tpu_custom_call" | custom-call | flops 1024 | bytes 1048576 | tf_op jit(solution)/shard_map/leave/pallas_call | solution.py:499
  101.9 9.3 %all-to-all-done.blocks = bf16[8,16,1024]{2,1,0:T(8,128)(2,1)S(1)} async-done(((bf16[8,16,1024]{2,1,0:T(8,128)(2,1)}), bf16[8,16,1024]{2,1,0:T(8,128)(2,1)S(1)}, u32[]{:S(2)}, u32[]{:S(2)}) %all-to-all-start) | async-done | bytes 262176 | tf_op jit(solution)/shard_map/all_to_all | solution.py:477
  111.3 1.2 finish.1
  112.5 3.7 %collective-permute-done.17.refs_1_ = bf16[512,512]{1,0:T(8,128)(2,1)S(1)} collective-permute-done((bf16[512,512]{1,0:T(8,128)(2,1)}, bf16[512,512]{1,0:T(8,128)(2,1)S(1)}, u32[]{:S(2)}, u32[]{:S(2)}) %collective-permute-start.17) | collective-permute-done | bytes 524320 | tf_op jit(solution)/shard_map/ppermute | solution.py:27
  116.9 1.2 copy-done.2
  118.1 2.6 %evict.1 = (bf16[2048,256]{1,0:T(8,128)(2,1)S(1)}, f32[136,128]{1,0:T(8,128)S(1)}, f32[136,128]{1,0:T(8,128)S(1)}, f32[136,128]{1,0:T(8,128)S(1)}, f32[136,128]{1,0:T(8,128)S(1)}) custom-call(f32[1,2048]{1,0:T(1,128)S(1)} %convert_element_type.64.slot_map, f32[3,520,128]{2,1,0:T(8,128)S(1)} %leave.1.leaving, f32[512,512]{1,0:T(8,128)S(1)} %copy-done.2, ...), custom_call_target="tpu_custom_call" | custom-call | flops 536870912 | bytes 4194304 | tf_op jit(solution)/shard_map/evict/pallas_call | solution.py:508
  120.7 1.0 collective-permute-start.20
  121.7 1.8 %collective-permute-start.21 = (f32[136,128]{1,0:T(8,128)S(1)}, f32[136,128]{1,0:T(8,128)S(1)}, u32[]{:S(2)}, u32[]{:S(2)}) collective-permute-start(f32[136,128]{1,0:T(8,128)S(1)} %get-tuple-element.347), channel_id=1, source_target_pairs={{0,2},{1,3},{2,0},{3,1},{4,6},{5,7},{6,4},{7,5},{8,10},{9,11},{10,... | collective-permute-start | bytes 208904 | tf_op jit(solution)/shard_map/ppermute | solution.py:27
  123.5 2.5 %collective-permute-start.22 = (f32[136,128]{1,0:T(8,128)S(1)}, f32[136,128]{1,0:T(8,128)S(1)}, u32[]{:S(2)}, u32[]{:S(2)}) collective-permute-start(f32[136,128]{1,0:T(8,128)S(1)} %get-tuple-element.348), channel_id=1, source_target_pairs={{0,3},{1,0},{2,1},{3,2},{4,7},{5,4},{6,5},{7,6},{8,11},{9,8},{10,9... | collective-permute-start | bytes 208904 | tf_op jit(solution)/shard_map/ppermute | solution.py:27
  126.1 4.3 %update.1 = (f32[2048,128]{1,0:T(8,128)}, f32[16,128]{1,0:T(8,128)}) custom-call(f32[1,2048]{1,0:T(1,128)S(1)} %convert_element_type.64.slot_map, bf16[2048,256]{1,0:T(8,128)(2,1)S(1)} %get-tuple-element.342.rhs, f32[2048,128]{1,0:T(8,128)S(1)} %bitcast.29, f32[16,128]{1,0:T(8,128)S(1)} %bitcast.34), custom_call_target="tpu_custom_call" | custom-call | flops 2147483648 | bytes 4194304 | tf_op jit(solution)/shard_map/update/pallas_call | solution.py:518
  130.4 1.3 arrive.1
  (62 shorter events, 5.3 us)
Async XLA Ops:
  1.3 12.2 %copy-start.4 = (s32[2,512,8]{1,2,0:T(8,128)S(1)}, s32[2,512,8]{1,2,0:T(8,128)}, u32[]{:S(2)}) copy-start(s32[2,512,8]{1,2,0:T(8,128)} %param.16) | copy-start | bytes 98308
  1.3 12.2 %copy-start.5 = (s32[2,512,8]{1,2,0:T(8,128)S(1)}, s32[2,512,8]{1,2,0:T(8,128)}, u32[]{:S(2)}) copy-start(s32[2,512,8]{1,2,0:T(8,128)} %param.17) | copy-start | bytes 98308
  1.3 12.2 %copy-start.6 = (bf16[2,512,8]{1,2,0:T(8,128)(2,1)S(1)}, bf16[2,512,8]{1,2,0:T(8,128)(2,1)}, u32[]{:S(2)}) copy-start(bf16[2,512,8]{1,2,0:T(8,128)(2,1)} %param.18) | copy-start | bytes 49156
  1.3 12.2 %copy-start.9 = (s32[2,512]{1,0:T(2,128)S(1)}, s32[2,512]{1,0:T(2,128)}, u32[]{:S(2)}) copy-start(s32[2,512]{1,0:T(2,128)} %lens) | copy-start | bytes 12292
  1.3 30.4 %copy-start.8 = (s32[4]{0:T(128)S(1)}, s32[4]{0:T(128)}, u32[]{:S(2)}) copy-start(s32[4]{0:T(128)} %pad_add_fusion.pos) | copy-start | bytes 52
  1.3 30.3 %copy-start.11 = (bf16[512,1024]{1,0:T(8,128)(2,1)S(1)}, bf16[512,1024]{1,0:T(8,128)(2,1)}, u32[]{:S(2)}) copy-start(bf16[512,1024]{1,0:T(8,128)(2,1)} %pooled.3) | copy-start | bytes 3145732
  8.6 9.6 %collective-permute-start = (bf16[1024,128]{1,0:T(8,128)(2,1)}, bf16[1024,128]{1,0:T(8,128)(2,1)S(1)}, u32[]{:S(2)}, u32[]{:S(2)}) collective-permute-start(bf16[1024,128]{1,0:T(8,128)(2,1)} %get-tuple-element.179), channel_id=1, source_target_pairs={{0,1},{1,2},{2,3},{3,0},{4,5},{5,6},{6,7},{7,4},{8,9},{9,10},{10,1... | collective-permute-start | bytes 786440 | tf_op jit(solution)/shard_map/ppermute | solution.py:27
  10.1 10.9 %collective-permute-start.1 = (bf16[1024,128]{1,0:T(8,128)(2,1)}, bf16[1024,128]{1,0:T(8,128)(2,1)S(1)}, u32[]{:S(2)}, u32[]{:S(2)}) collective-permute-start(bf16[1024,128]{1,0:T(8,128)(2,1)} %get-tuple-element.180), channel_id=1, source_target_pairs={{0,2},{1,3},{2,0},{3,1},{4,6},{5,7},{6,4},{7,5},{8,10},{9,11},{10,... | collective-permute-start | bytes 786440 | tf_op jit(solution)/shard_map/ppermute | solution.py:27
  12.8 11.6 %collective-permute-start.2 = (bf16[1024,128]{1,0:T(8,128)(2,1)}, bf16[1024,128]{1,0:T(8,128)(2,1)S(1)}, u32[]{:S(2)}, u32[]{:S(2)}) collective-permute-start(bf16[1024,128]{1,0:T(8,128)(2,1)} %get-tuple-element.181), channel_id=1, source_target_pairs={{0,3},{1,0},{2,1},{3,2},{4,7},{5,4},{6,5},{7,6},{8,11},{9,8},{10,9... | collective-permute-start | bytes 786440 | tf_op jit(solution)/shard_map/ppermute | solution.py:27
  24.5 1.0 copy-start.3
  25.6 13.0 %collective-permute-start.3 = (bf16[1280,128]{1,0:T(8,128)(2,1)S(1)}, bf16[1280,128]{1,0:T(8,128)(2,1)S(1)}, u32[]{:S(2)}, u32[]{:S(2)}) collective-permute-start(bf16[1280,128]{1,0:T(8,128)(2,1)S(1)} %own.1.refs_0_), channel_id=1, source_target_pairs={{0,32},{32,64},{64,96},{96,128},{128,160},{160,192},{192,224},{224... | collective-permute-start | bytes 983048 | tf_op jit(solution)/shard_map/ppermute | solution.py:27
  27.6 11.0 %collective-permute-start.4 = (bf16[1280,128]{1,0:T(8,128)(2,1)S(1)}, bf16[1280,128]{1,0:T(8,128)(2,1)S(1)}, u32[]{:S(2)}, u32[]{:S(2)}) collective-permute-start(bf16[1280,128]{1,0:T(8,128)(2,1)S(1)} %own.1.refs_0_), channel_id=1, source_target_pairs={{0,224},{32,0},{64,32},{96,64},{128,96},{160,128},{192,160},{224,1... | collective-permute-start | bytes 983048 | tf_op jit(solution)/shard_map/ppermute | solution.py:27
  31.7 1.2 copy-start.12
  38.6 4.2 %collective-permute-start.7 = (f32[4,8,16,1024]{3,2,1,0:T(8,128)S(1)}, f32[4,8,16,1024]{3,2,1,0:T(8,128)S(1)}, u32[]{:S(2)}, u32[]{:S(2)}) collective-permute-start(f32[4,8,16,1024]{3,2,1,0:T(8,128)S(1)} %get-tuple-element.212), channel_id=1, source_target_pairs={{0,4},{4,0},{1,5},{5,1},{2,6},{6,2},{3,7},{7,3},{8,12},{12,8},{9,1... | collective-permute-start | bytes 6291464 | tf_op jit(solution)/shard_map/ppermute | solution.py:27
  38.6 11.4 %collective-permute-start.5 = (bf16[1280,128]{1,0:T(8,128)(2,1)S(1)}, bf16[1280,128]{1,0:T(8,128)(2,1)S(1)}, u32[]{:S(2)}, u32[]{:S(2)}) collective-permute-start(bf16[1280,128]{1,0:T(8,128)(2,1)S(1)} %collective-permute-done.3.refs_0_), channel_id=1, source_target_pairs={{0,32},{32,64},{64,96},{96,128},{128,160},{160,192},{192,224},{224... | collective-permute-start | bytes 983048 | tf_op jit(solution)/shard_map/ppermute | solution.py:27
  38.6 11.4 %collective-permute-start.6 = (bf16[1280,128]{1,0:T(8,128)(2,1)S(1)}, bf16[1280,128]{1,0:T(8,128)(2,1)S(1)}, u32[]{:S(2)}, u32[]{:S(2)}) collective-permute-start(bf16[1280,128]{1,0:T(8,128)(2,1)S(1)} %collective-permute-done.4.refs_1_), channel_id=1, source_target_pairs={{0,224},{32,0},{64,32},{96,64},{128,96},{160,128},{192,160},{224,1... | collective-permute-start | bytes 983048 | tf_op jit(solution)/shard_map/ppermute | solution.py:27
  50.0 14.6 %collective-permute-start.8 = (bf16[1280,128]{1,0:T(8,128)(2,1)S(1)}, bf16[1280,128]{1,0:T(8,128)(2,1)S(1)}, u32[]{:S(2)}, u32[]{:S(2)}) collective-permute-start(bf16[1280,128]{1,0:T(8,128)(2,1)S(1)} %collective-permute-done.5.refs_0_), channel_id=1, source_target_pairs={{0,32},{32,64},{64,96},{96,128},{128,160},{160,192},{192,224},{224... | collective-permute-start | bytes 983048 | tf_op jit(solution)/shard_map/ppermute | solution.py:27
  52.4 12.3 %collective-permute-start.9 = (bf16[1280,128]{1,0:T(8,128)(2,1)S(1)}, bf16[1280,128]{1,0:T(8,128)(2,1)S(1)}, u32[]{:S(2)}, u32[]{:S(2)}) collective-permute-start(bf16[1280,128]{1,0:T(8,128)(2,1)S(1)} %collective-permute-done.6.refs_1_), channel_id=1, source_target_pairs={{0,224},{32,0},{64,32},{96,64},{128,96},{160,128},{192,160},{224,1... | collective-permute-start | bytes 983048 | tf_op jit(solution)/shard_map/ppermute | solution.py:27
  53.3 17.7 %collective-permute-start.12 = (bf16[8,16,1024]{2,1,0:T(8,128)(2,1)S(1)}, bf16[8,16,1024]{2,1,0:T(8,128)(2,1)S(1)}, u32[]{:S(2)}, u32[]{:S(2)}) collective-permute-start(bf16[8,16,1024]{2,1,0:T(8,128)(2,1)S(1)} %get-tuple-element.249), channel_id=1, source_target_pairs={{0,8},{8,16},{16,24},{24,0},{1,9},{9,17},{17,25},{25,1},{2,10},{10... | collective-permute-start | bytes 786440 | tf_op jit(solution)/shard_map/ppermute | solution.py:27
  54.8 16.2 %collective-permute-start.13 = (bf16[8,16,1024]{2,1,0:T(8,128)(2,1)S(1)}, bf16[8,16,1024]{2,1,0:T(8,128)(2,1)S(1)}, u32[]{:S(2)}, u32[]{:S(2)}) collective-permute-start(bf16[8,16,1024]{2,1,0:T(8,128)(2,1)S(1)} %get-tuple-element.250), channel_id=1, source_target_pairs={{0,16},{8,24},{16,0},{24,8},{1,17},{9,25},{17,1},{25,9},{2,18},{10... | collective-permute-start | bytes 786440 | tf_op jit(solution)/shard_map/ppermute | solution.py:27
  57.5 13.5 %collective-permute-start.14 = (bf16[8,16,1024]{2,1,0:T(8,128)(2,1)S(1)}, bf16[8,16,1024]{2,1,0:T(8,128)(2,1)S(1)}, u32[]{:S(2)}, u32[]{:S(2)}) collective-permute-start(bf16[8,16,1024]{2,1,0:T(8,128)(2,1)S(1)} %get-tuple-element.251), channel_id=1, source_target_pairs={{0,24},{8,0},{16,8},{24,16},{1,25},{9,1},{17,9},{25,17},{2,26},{10... | collective-permute-start | bytes 786440 | tf_op jit(solution)/shard_map/ppermute | solution.py:27
  64.7 6.6 %collective-permute-start.10 = (bf16[640,128]{1,0:T(8,128)(2,1)S(1)}, bf16[640,128]{1,0:T(8,128)(2,1)S(1)}, u32[]{:S(2)}, u32[]{:S(2)}) collective-permute-start(bf16[640,128]{1,0:T(8,128)(2,1)S(1)} %slice.25), channel_id=1, source_target_pairs={{0,32},{32,64},{64,96},{96,128},{128,160},{160,192},{192,224},{224... | collective-permute-start | bytes 491528 | tf_op jit(solution)/shard_map/ppermute | solution.py:27
  66.0 5.4 %collective-permute-start.11 = (bf16[640,128]{1,0:T(8,128)(2,1)S(1)}, bf16[640,128]{1,0:T(8,128)(2,1)S(1)}, u32[]{:S(2)}, u32[]{:S(2)}) collective-permute-start(bf16[640,128]{1,0:T(8,128)(2,1)S(1)} %slice.26), channel_id=1, source_target_pairs={{0,224},{32,0},{64,32},{96,64},{128,96},{160,128},{192,160},{224,1... | collective-permute-start | bytes 491528 | tf_op jit(solution)/shard_map/ppermute | solution.py:27
  78.1 2.7 %collective-permute-start.16 = (bf16[4,256,512]{2,1,0:T(8,128)(2,1)S(1)}, bf16[4,256,512]{2,1,0:T(8,128)(2,1)S(1)}, u32[]{:S(2)}, u32[]{:S(2)}) collective-permute-start(bf16[4,256,512]{2,1,0:T(8,128)(2,1)S(1)} %send1.1), channel_id=1, source_target_pairs={{0,4},{4,0},{1,5},{5,1},{2,6},{6,2},{3,7},{7,3},{8,12},{12,8},{9,1... | collective-permute-start | bytes 3145736 | tf_op jit(solution)/shard_map/ppermute | solution.py:27
  78.2 4.1 %collective-permute-start.15 = (bf16[4,256,512]{2,1,0:T(8,128)(2,1)S(1)}, bf16[4,256,512]{2,1,0:T(8,128)(2,1)S(1)}, u32[]{:S(2)}, u32[]{:S(2)}) collective-permute-start(bf16[4,256,512]{2,1,0:T(8,128)(2,1)S(1)} %send0.1), channel_id=1, source_target_pairs={{0,4},{4,0},{1,5},{5,1},{2,6},{6,2},{3,7},{7,3},{8,12},{12,8},{9,1... | collective-permute-start | bytes 3145736 | tf_op jit(solution)/shard_map/ppermute | solution.py:27
  79.5 20.2 %copy-start.13 = (s32[1,1,2048]{2,1,0:T(1,128)S(1)}, s32[1,1,2048]{2,1,0:T(1,128)}, u32[]{:S(2)}) copy-start(s32[1,1,2048]{2,1,0:T(1,128)} %param.20) | copy-start | bytes 24580
  79.5 20.6 %copy-start.14 = (s32[1,1,256]{2,1,0:T(1,128)S(1)}, s32[1,1,256]{2,1,0:T(1,128)}, u32[]{:S(2)}) copy-start(s32[1,1,256]{2,1,0:T(1,128)} %param.24) | copy-start | bytes 3076
  79.5 20.8 %copy-start.7 = (f32[1,1,2048]{2,1,0:T(1,128)S(1)}, f32[1,1,2048]{2,1,0:T(1,128)}, u32[]{:S(2)}) copy-start(f32[1,1,2048]{2,1,0:T(1,128)} %param.22) | copy-start | bytes 24580
  79.5 20.8 %copy-start.10 = (s32[1,1,256]{2,1,0:T(1,128)S(1)}, s32[1,1,256]{2,1,0:T(1,128)}, u32[]{:S(2)}) copy-start(s32[1,1,256]{2,1,0:T(1,128)} %param.23) | copy-start | bytes 3076
  88.6 1.0 copy-start.1
  89.6 10.8 %copy-start = (f32[1,1,2048,128]{3,2,1,0:T(8,128)S(1)}, f32[1,1,2048,128]{3,2,1,0:T(8,128)}, u32[]{:S(2)}) copy-start(f32[1,1,2048,128]{3,2,1,0:T(8,128)} %param.21) | copy-start | bytes 3145732
  89.6 26.6 %collective-permute-start.17 = (bf16[512,512]{1,0:T(8,128)(2,1)}, bf16[512,512]{1,0:T(8,128)(2,1)S(1)}, u32[]{:S(2)}, u32[]{:S(2)}) collective-permute-start(bf16[512,512]{1,0:T(8,128)(2,1)} %get-tuple-element.339), channel_id=1, source_target_pairs={{0,8},{8,16},{16,24},{24,0},{1,9},{9,17},{17,25},{25,1},{2,10},{10... | collective-permute-start | bytes 1572872 | tf_op jit(solution)/shard_map/ppermute | solution.py:27
  90.2 26.0 %collective-permute-start.18 = (bf16[512,512]{1,0:T(8,128)(2,1)}, bf16[512,512]{1,0:T(8,128)(2,1)}, u32[]{:S(2)}, u32[]{:S(2)}) collective-permute-start(bf16[512,512]{1,0:T(8,128)(2,1)} %get-tuple-element.340), channel_id=1, source_target_pairs={{0,16},{8,24},{16,0},{24,8},{1,17},{9,25},{17,1},{25,9},{2,18},{10... | collective-permute-start | bytes 1572872 | tf_op jit(solution)/shard_map/ppermute | solution.py:27
  91.0 25.9 %collective-permute-start.19 = (bf16[512,512]{1,0:T(8,128)(2,1)}, bf16[512,512]{1,0:T(8,128)(2,1)}, u32[]{:S(2)}, u32[]{:S(2)}) collective-permute-start(bf16[512,512]{1,0:T(8,128)(2,1)} %get-tuple-element.341), channel_id=1, source_target_pairs={{0,24},{8,0},{16,8},{24,16},{1,25},{9,1},{17,9},{25,17},{2,26},{10... | collective-permute-start | bytes 1572872 | tf_op jit(solution)/shard_map/ppermute | solution.py:27
  93.6 17.7 %all-to-all-start = ((bf16[8,16,1024]{2,1,0:T(8,128)(2,1)}), bf16[8,16,1024]{2,1,0:T(8,128)(2,1)S(1)}, u32[]{:S(2)}, u32[]{:S(2)}) async-start(bf16[8,16,1024]{2,1,0:T(8,128)(2,1)} %convert_element_type.60), calls=%async_computation | async-start | bytes 524288 | tf_op jit(solution)/shard_map/all_to_all | solution.py:477
  116.9 1.2 copy-start.2
  120.7 9.6 %collective-permute-start.20 = (f32[136,128]{1,0:T(8,128)S(1)}, f32[136,128]{1,0:T(8,128)S(1)}, u32[]{:S(2)}, u32[]{:S(2)}) collective-permute-start(f32[136,128]{1,0:T(8,128)S(1)} %get-tuple-element.346), channel_id=1, source_target_pairs={{0,1},{1,2},{2,3},{3,0},{4,5},{5,6},{6,7},{7,4},{8,9},{9,10},{10,1... | collective-permute-start | bytes 208904 | tf_op jit(solution)/shard_map/ppermute | solution.py:27
  121.7 8.7 %collective-permute-start.21 = (f32[136,128]{1,0:T(8,128)S(1)}, f32[136,128]{1,0:T(8,128)S(1)}, u32[]{:S(2)}, u32[]{:S(2)}) collective-permute-start(f32[136,128]{1,0:T(8,128)S(1)} %get-tuple-element.347), channel_id=1, source_target_pairs={{0,2},{1,3},{2,0},{3,1},{4,6},{5,7},{6,4},{7,5},{8,10},{9,11},{10,... | collective-permute-start | bytes 208904 | tf_op jit(solution)/shard_map/ppermute | solution.py:27
  123.5 6.8 %collective-permute-start.22 = (f32[136,128]{1,0:T(8,128)S(1)}, f32[136,128]{1,0:T(8,128)S(1)}, u32[]{:S(2)}, u32[]{:S(2)}) collective-permute-start(f32[136,128]{1,0:T(8,128)S(1)} %get-tuple-element.348), channel_id=1, source_target_pairs={{0,3},{1,0},{2,1},{3,2},{4,7},{5,4},{6,5},{7,6},{8,11},{9,8},{10,9... | collective-permute-start | bytes 208904 | tf_op jit(solution)/shard_map/ppermute | solution.py:27

commit v5 on v4

--- a/solution.py
+++ b/solution.py
@@ -272,7 +272,7 @@
     parts, rhs, held, pick, sums = refs[:4], refs[4], refs[5:9], refs[9], refs[10]
     for t in range(2):
         at = slice(t * 256, (t + 1) * 256)
-        own = parts[0][at, :]
+        own = parts[0][at, :].astype(F32)
         for k in range(1, 4):
             own = own + parts[k][at, :].astype(F32)
         high = own.astype(BF16)
@@ -460,7 +460,7 @@
     outs = call(
         keep_kernel,
         [VMEM] * 32,
-        [shape((512, 512), F32)] + [shape((512, 512), BF16)] * 3,
+        [shape((512, 512), BF16)] * 4,
         work + [pltpu.VMEM((4, 256, 512), F32)],
         8 << 30,
         10 << 20,

time: 132 us -> 130 us (0.985)
  local copies, waits for them, and re-layouts: 5.04 us -> 2.84 us
    unnamed x30 -> x26, local copies, waits for them, and re-layouts: 4.51 us -> 2.32 us
  transfers between devices with their start and end apart: 24 -> 24, of which waited for: 12 -> 13; matrix products, arithmetic and copies ran while one was open for 2% -> 2% of each run, Pallas kernels for 15% -> 15%
where the time goes in v5:
time: 130 us
  Pallas kernels  44.2 us (34%)
  starting transfers between devices  41.8 us (32%)
  waiting for transfers between devices  37.1 us (29%)
  local copies, waits for them, and re-layouts  2.84 us (2%)
  other arithmetic  2.03 us (2%)
  between operations  1.57 us (1%)
    ppermute x23, starting transfers between devices, shifted(): return lax.ppermute(x, axis, [(i, (i + step) % size) for i in range(size)])  35.7 us
    ppermute x23, waiting for transfers between devices, shifted(): return lax.ppermute(x, axis, [(i, (i + step) % size) for i in range(size)])  27.8 us
    pallas_call x5, Pallas kernels, pick(): call(functools.partial(pick_kernel, count), [SMEM, VMEM] + [VMEM] * len(b...  11.9 us
    all_to_all x1, waiting for transfers between devices, on_device(): lax.all_to_all(total.astype(BF16), Z, split_axis=0, concat_axis=0, tiled=...  9.33 us
    pallas_call x1, Pallas kernels, on_device(): call(top_kernel, [SMEM, VMEM, VMEM, VMEM], [shape((bags, 1024), BF16), sh...  7.24 us
    pallas_call x1, Pallas kernels, on_device(): call(keep_kernel, [VMEM] * 32, [shape((512, 512), BF16)] * 4, work + [plt...  6.29 us
    all_to_all x1, starting transfers between devices, on_device(): lax.all_to_all(total.astype(BF16), Z, split_axis=0, concat_axis=0, tiled=...  6.09 us
    pallas_call x2, Pallas kernels, on_device(): call(send_kernel, [VMEM] * 15, [shape((4, 256, 512), BF16)], work, 4 << 3...  5.05 us
  transfers between devices with their start and end apart: 24, of which 13 were waited for; matrix products, arithmetic and copies ran while one was open for 2% of the time, Pallas kernels for 15%

profile of v5, /device:TPU:8, one launch (start us, length us, event | category | flops | bytes accessed | tf_op | source)
XLA Modules:
  0.0 129.7 jit_solution(10262000221527334818)
XLA Ops:
  1.3 7.2 %top.1 = (bf16[512,1024]{1,0:T(8,128)(2,1)}, f32[1024,128]{1,0:T(8,128)}, bf16[1024,128]{1,0:T(8,128)(2,1)}, bf16[1024,128]{1,0:T(8,128)(2,1)}, bf16[1024,128]{1,0:T(8,128)(2,1)}) custom-call(s32[4]{0:T(128)} %pad_add_fusion.pos, bf16[512,1024]{1,0:T(8,128)(2,1)} %pooled.3, bf16[1024,1024]{1,0:T(8,128)(2,1)} %w_up.1, bf16[512,1024]{1,0:T(8,128)(2,1)} %grad_out.1), custom_call_target="tpu_custom_call" | custom-call | flops 2147483648 | bytes 6291456 | tf_op jit(solution)/shard_map/top/pallas_call | solution.py:365
  8.5 1.6 %collective-permute-start = (bf16[1024,128]{1,0:T(8,128)(2,1)}, bf16[1024,128]{1,0:T(8,128)(2,1)S(1)}, u32[]{:S(2)}, u32[]{:S(2)}) collective-permute-start(bf16[1024,128]{1,0:T(8,128)(2,1)} %get-tuple-element.179), channel_id=1, source_target_pairs={{0,1},{1,2},{2,3},{3,0},{4,5},{5,6},{6,7},{7,4},{8,9},{9,10},{10,1... | collective-permute-start | bytes 786440 | tf_op jit(solution)/shard_map/ppermute | solution.py:27
  10.1 2.7 %collective-permute-start.1 = (bf16[1024,128]{1,0:T(8,128)(2,1)}, bf16[1024,128]{1,0:T(8,128)(2,1)S(1)}, u32[]{:S(2)}, u32[]{:S(2)}) collective-permute-start(bf16[1024,128]{1,0:T(8,128)(2,1)} %get-tuple-element.180), channel_id=1, source_target_pairs={{0,2},{1,3},{2,0},{3,1},{4,6},{5,7},{6,4},{7,5},{8,10},{9,11},{10,... | collective-permute-start | bytes 786440 | tf_op jit(solution)/shard_map/ppermute | solution.py:27
  12.8 0.7 collective-permute-start.2
  13.5 4.6 %collective-permute-done.one = bf16[1024,128]{1,0:T(8,128)(2,1)S(1)} collective-permute-done((bf16[1024,128]{1,0:T(8,128)(2,1)}, bf16[1024,128]{1,0:T(8,128)(2,1)S(1)}, u32[]{:S(2)}, u32[]{:S(2)}) %collective-permute-start) | collective-permute-done | bytes 262176 | tf_op jit(solution)/shard_map/ppermute | solution.py:27
  18.1 2.9 %collective-permute-done.1.two = bf16[1024,128]{1,0:T(8,128)(2,1)S(1)} collective-permute-done((bf16[1024,128]{1,0:T(8,128)(2,1)}, bf16[1024,128]{1,0:T(8,128)(2,1)S(1)}, u32[]{:S(2)}, u32[]{:S(2)}) %collective-permute-start.1) | collective-permute-done | bytes 262176 | tf_op jit(solution)/shard_map/ppermute | solution.py:27
  21.0 3.4 %collective-permute-done.2.three = bf16[1024,128]{1,0:T(8,128)(2,1)S(1)} collective-permute-done((bf16[1024,128]{1,0:T(8,128)(2,1)}, bf16[1024,128]{1,0:T(8,128)(2,1)S(1)}, u32[]{:S(2)}, u32[]{:S(2)}) %collective-permute-start.2) | collective-permute-done | bytes 262176 | tf_op jit(solution)/shard_map/ppermute | solution.py:27
  24.4 1.0 copy-done.1
  25.6 2.0 %collective-permute-start.3 = (bf16[1280,128]{1,0:T(8,128)(2,1)S(1)}, bf16[1280,128]{1,0:T(8,128)(2,1)S(1)}, u32[]{:S(2)}, u32[]{:S(2)}) collective-permute-start(bf16[1280,128]{1,0:T(8,128)(2,1)S(1)} %own.1.refs_0_), channel_id=1, source_target_pairs={{0,32},{32,64},{64,96},{96,128},{128,160},{160,192},{192,224},{224... | collective-permute-start | bytes 983048 | tf_op jit(solution)/shard_map/ppermute | solution.py:27
  27.6 4.0 %collective-permute-start.4 = (bf16[1280,128]{1,0:T(8,128)(2,1)S(1)}, bf16[1280,128]{1,0:T(8,128)(2,1)S(1)}, u32[]{:S(2)}, u32[]{:S(2)}) collective-permute-start(bf16[1280,128]{1,0:T(8,128)(2,1)S(1)} %own.1.refs_0_), channel_id=1, source_target_pairs={{0,224},{32,0},{64,32},{96,64},{128,96},{160,128},{192,160},{224,1... | collective-permute-start | bytes 983048 | tf_op jit(solution)/shard_map/ppermute | solution.py:27
  31.6 1.2 copy-done.10
  32.8 2.3 %grad.1 = (f32[4,8,16,1024]{3,2,1,0:T(8,128)S(1)}, f32[4,8,16,1024]{3,2,1,0:T(8,128)S(1)}) custom-call(s32[4]{0:T(128)S(1)} %copy-done.6, bf16[512,1024]{1,0:T(8,128)(2,1)S(1)} %copy-done.9, bf16[512,1024]{1,0:T(8,128)(2,1)S(1)} %copy-done.10), custom_call_target="tpu_custom_call" | custom-call | flops 1073741824 | bytes 6291456 | tf_op jit(solution)/shard_map/grad/pallas_call | solution.py:418
  35.2 1.7 %pick0.1 = (bf16[1,4,128,128]{3,2,1,0:T(8,128)(2,1)S(1)}, bf16[1,4,128,128]{3,2,1,0:T(8,128)(2,1)S(1)}, f32[1,8,128]{2,1,0:T(8,128)S(1)}, bf16[1,4,128,128]{3,2,...) custom-call(s32[4]{0:T(128)S(1)} %copy-done.6, ...), custom_call_target="tpu_custom_call" | custom-call | flops 1073741824 | bytes 4194304 | tf_op jit(solution)/shard_map/pick0/pallas_call | solution.py:400
  36.8 1.7 %collective-permute-done.3.refs_0_ = bf16[1280,128]{1,0:T(8,128)(2,1)S(1)} collective-permute-done((bf16[1280,128]{1,0:T(8,128)(2,1)S(1)}, bf16[1280,128]{1,0:T(8,128)(2,1)S(1)}, u32[]{:S(2)}, u32[]{:S(2)}) %collective-permute-start.3) | collective-permute-done | bytes 327712 | tf_op jit(solution)/shard_map/ppermute | solution.py:27
  38.6 3.2 %collective-permute-start.6 = (bf16[1280,128]{1,0:T(8,128)(2,1)S(1)}, bf16[1280,128]{1,0:T(8,128)(2,1)S(1)}, u32[]{:S(2)}, u32[]{:S(2)}) collective-permute-start(bf16[1280,128]{1,0:T(8,128)(2,1)S(1)} %collective-permute-done.4.refs_1_), channel_id=1, source_target_pairs={{0,224},{32,0},{64,32},{96,64},{128,96},{160,128},{192,160},{224,1... | collective-permute-start | bytes 983048 | tf_op jit(solution)/shard_map/ppermute | solution.py:27
  41.8 0.9 collective-permute-done.7
  43.4 6.6 %collective-permute-done.5.refs_0_ = bf16[1280,128]{1,0:T(8,128)(2,1)S(1)} collective-permute-done((bf16[1280,128]{1,0:T(8,128)(2,1)S(1)}, bf16[1280,128]{1,0:T(8,128)(2,1)S(1)}, u32[]{:S(2)}, u32[]{:S(2)}) %collective-permute-start.5) | collective-permute-done | bytes 327712 | tf_op jit(solution)/shard_map/ppermute | solution.py:27
  50.0 2.4 %collective-permute-start.8 = (bf16[1280,128]{1,0:T(8,128)(2,1)S(1)}, bf16[1280,128]{1,0:T(8,128)(2,1)S(1)}, u32[]{:S(2)}, u32[]{:S(2)}) collective-permute-start(bf16[1280,128]{1,0:T(8,128)(2,1)S(1)} %collective-permute-done.5.refs_0_), channel_id=1, source_target_pairs={{0,32},{32,64},{64,96},{96,128},{128,160},{160,192},{192,224},{224... | collective-permute-start | bytes 983048 | tf_op jit(solution)/shard_map/ppermute | solution.py:27
  52.3 0.9 collective-permute-start.9
  53.2 1.5 %collective-permute-start.12 = (bf16[8,16,1024]{2,1,0:T(8,128)(2,1)S(1)}, bf16[8,16,1024]{2,1,0:T(8,128)(2,1)S(1)}, u32[]{:S(2)}, u32[]{:S(2)}) collective-permute-start(bf16[8,16,1024]{2,1,0:T(8,128)(2,1)S(1)} %get-tuple-element.249), channel_id=1, source_target_pairs={{0,8},{8,16},{16,24},{24,0},{1,9},{9,17},{17,25},{25,1},{2,10},{10... | collective-permute-start | bytes 786440 | tf_op jit(solution)/shard_map/ppermute | solution.py:27
  54.7 2.7 %collective-permute-start.13 = (bf16[8,16,1024]{2,1,0:T(8,128)(2,1)S(1)}, bf16[8,16,1024]{2,1,0:T(8,128)(2,1)S(1)}, u32[]{:S(2)}, u32[]{:S(2)}) collective-permute-start(bf16[8,16,1024]{2,1,0:T(8,128)(2,1)S(1)} %get-tuple-element.250), channel_id=1, source_target_pairs={{0,16},{8,24},{16,0},{24,8},{1,17},{9,25},{17,1},{25,9},{2,18},{10... | collective-permute-start | bytes 786440 | tf_op jit(solution)/shard_map/ppermute | solution.py:27
  57.4 1.4 %collective-permute-start.14 = (bf16[8,16,1024]{2,1,0:T(8,128)(2,1)S(1)}, bf16[8,16,1024]{2,1,0:T(8,128)(2,1)S(1)}, u32[]{:S(2)}, u32[]{:S(2)}) collective-permute-start(bf16[8,16,1024]{2,1,0:T(8,128)(2,1)S(1)} %get-tuple-element.251), channel_id=1, source_target_pairs={{0,24},{8,0},{16,8},{24,16},{1,25},{9,1},{17,9},{25,17},{2,26},{10... | collective-permute-start | bytes 786440 | tf_op jit(solution)/shard_map/ppermute | solution.py:27
  58.9 2.9 %pick2.1 = (bf16[2,4,128,128]{3,2,1,0:T(8,128)(2,1)S(1)}, bf16[2,4,128,128]{3,2,1,0:T(8,128)(2,1)S(1)}, f32[2,8,128]{2,1,0:T(8,128)S(1)}, bf16[2,4,128,128]{3,2,...) custom-call(s32[4]{0:T(128)S(1)} %copy-done.6, ...), custom_call_target="tpu_custom_call" | custom-call | flops 1073741824 | bytes 4194304 | tf_op jit(solution)/shard_map/pick2/pallas_call | solution.py:400
  61.7 2.9 %pick1.1 = (bf16[2,4,128,128]{3,2,1,0:T(8,128)(2,1)S(1)}, bf16[2,4,128,128]{3,2,1,0:T(8,128)(2,1)S(1)}, f32[2,8,128]{2,1,0:T(8,128)S(1)}, bf16[2,4,128,128]{3,2,...) custom-call(s32[4]{0:T(128)S(1)} %copy-done.6, ...), custom_call_target="tpu_custom_call" | custom-call | flops 1073741824 | bytes 4194304 | tf_op jit(solution)/shard_map/pick1/pallas_call | solution.py:400
  64.6 1.3 collective-permute-start.10
  65.9 2.1 %collective-permute-start.11 = (bf16[640,128]{1,0:T(8,128)(2,1)S(1)}, bf16[640,128]{1,0:T(8,128)(2,1)S(1)}, u32[]{:S(2)}, u32[]{:S(2)}) collective-permute-start(bf16[640,128]{1,0:T(8,128)(2,1)S(1)} %slice.26), channel_id=1, source_target_pairs={{0,224},{32,0},{64,32},{96,64},{128,96},{160,128},{192,160},{224,1... | collective-permute-start | bytes 491528 | tf_op jit(solution)/shard_map/ppermute | solution.py:27
  68.0 2.9 %pick3.1 = (bf16[2,4,128,128]{3,2,1,0:T(8,128)(2,1)S(1)}, bf16[2,4,128,128]{3,2,1,0:T(8,128)(2,1)S(1)}, f32[2,8,128]{2,1,0:T(8,128)S(1)}, bf16[2,4,128,128]{3,2,...) custom-call(s32[4]{0:T(128)S(1)} %copy-done.6, ...), custom_call_target="tpu_custom_call" | custom-call | flops 1073741824 | bytes 4194304 | tf_op jit(solution)/shard_map/pick3/pallas_call | solution.py:400
  71.3 1.7 %pick4.1 = (bf16[1,4,128,128]{3,2,1,0:T(8,128)(2,1)S(1)}, bf16[1,4,128,128]{3,2,1,0:T(8,128)(2,1)S(1)}, f32[1,8,128]{2,1,0:T(8,128)S(1)}, bf16[1,4,128,128]{3,2,...) custom-call(s32[4]{0:T(128)S(1)} %copy-done.6, ...), custom_call_target="tpu_custom_call" | custom-call | flops 1073741824 | bytes 4194304 | tf_op jit(solution)/shard_map/pick4/pallas_call | solution.py:400
  72.9 2.5 %send0.1 = bf16[4,256,512]{2,1,0:T(8,128)(2,1)S(1)} custom-call(bf16[1,4,128,128]{3,2,1,0:T(8,128)(2,1)S(1)} %get-tuple-element.206.refs_0_, bf16[1,4,128,128]{3,2,1,0:T(8,128)(2,1)S(1)} %get-tuple-element.207.refs_1_, f32[1,8,128]{2,1,0:T(8,128)S(1)} %get-tuple-element.208.refs_2_, bf16[2,4,128,128]{3,2,1,0:T(8,128)(2,1)S(1)} %get-tuple-element.241.refs_3_, ...), custom_call_target="tpu_custom_call" | custom-call | flops 4294967296 | bytes 5242880 | tf_op jit(solution)/shard_map/send0/pallas_call | solution.py:455
  75.5 2.5 %send1.1 = bf16[4,256,512]{2,1,0:T(8,128)(2,1)S(1)} custom-call(bf16[1,4,128,128]{3,2,1,0:T(8,128)(2,1)S(1)} %get-tuple-element.282.refs_0_, bf16[1,4,128,128]{3,2,1,0:T(8,128)(2,1)S(1)} %get-tuple-element.283.refs_1_, f32[1,8,128]{2,1,0:T(8,128)S(1)} %get-tuple-element.284.refs_2_, bf16[2,4,128,128]{3,2,1,0:T(8,128)(2,1)S(1)} %get-tuple-element.285.refs_3_, ...), custom_call_target="tpu_custom_call" | custom-call | flops 4294967296 | bytes 5242880 | tf_op jit(solution)/shard_map/send1/pallas_call | solution.py:455
  79.5 1.3 %collective-permute-done.16.other1 = bf16[4,256,512]{2,1,0:T(8,128)(2,1)S(1)} collective-permute-done((bf16[4,256,512]{2,1,0:T(8,128)(2,1)S(1)}, bf16[4,256,512]{2,1,0:T(8,128)(2,1)S(1)}, u32[]{:S(2)}, u32[]{:S(2)}) %collective-permute-start.16) | collective-permute-done | bytes 1048608 | tf_op jit(solution)/shard_map/ppermute | solution.py:27
  80.8 1.5 %collective-permute-done.15.other0 = bf16[4,256,512]{2,1,0:T(8,128)(2,1)S(1)} collective-permute-done((bf16[4,256,512]{2,1,0:T(8,128)(2,1)S(1)}, bf16[4,256,512]{2,1,0:T(8,128)(2,1)S(1)}, u32[]{:S(2)}, u32[]{:S(2)}) %collective-permute-start.15) | collective-permute-done | bytes 1048608 | tf_op jit(solution)/shard_map/ppermute | solution.py:27
  82.3 6.3 %keep.1 = (bf16[512,512]{1,0:T(8,128)(2,1)S(1)}, bf16[512,512]{1,0:T(8,128)(2,1)}, bf16[512,512]{1,0:T(8,128)(2,1)}, bf16[512,512]{1,0:T(8,128)(2,1)}) custom-call(bf16[4,256,512]{2,1,0:T(8,128)(2,1)S(1)} %collective-permute-done.15.other0, bf16[4,256,512]{2,1,0:T(8,128)(2,1)S(1)} %collective-permute-done.16.other1, ...), custom_call_target="tpu_custom_call" | custom-call | flops 8589934592 | bytes 10485760 | tf_op jit(solution)/shard_map/keep/pallas_call | solution.py:460
  89.2 0.9 collective-permute-start.18
  90.0 1.8 %collective-permute-start.19 = (bf16[512,512]{1,0:T(8,128)(2,1)}, bf16[512,512]{1,0:T(8,128)(2,1)}, u32[]{:S(2)}, u32[]{:S(2)}) collective-permute-start(bf16[512,512]{1,0:T(8,128)(2,1)} %get-tuple-element.341), channel_id=1, source_target_pairs={{0,24},{8,0},{16,8},{24,16},{1,25},{9,1},{17,9},{25,17},{2,26},{10... | collective-permute-start | bytes 1572872 | tf_op jit(solution)/shard_map/ppermute | solution.py:27
  91.8 0.7 convert_element_type.60
  92.6 6.1 %all-to-all-start = ((bf16[8,16,1024]{2,1,0:T(8,128)(2,1)}), bf16[8,16,1024]{2,1,0:T(8,128)(2,1)S(1)}, u32[]{:S(2)}, u32[]{:S(2)}) async-start(bf16[8,16,1024]{2,1,0:T(8,128)(2,1)} %convert_element_type.60), calls=%async_computation | async-start | bytes 524288 | tf_op jit(solution)/shard_map/all_to_all | solution.py:477
  99.4 1.6 %leave.1.leaving = f32[3,520,128]{2,1,0:T(8,128)S(1)} custom-call(s32[256]{0:T(256)S(1)} %bitcast.35, s32[256]{0:T(256)S(1)} %fusion.9.goal_s, f32[2048]{0:T(1024)S(1)} %bitcast.33, f32[2048,128]{1,0:T(8,128)S(1)} %bitcast.28), custom_call_target="tpu_custom_call" | custom-call | flops 1024 | bytes 1048576 | tf_op jit(solution)/shard_map/leave/pallas_call | solution.py:499
  100.9 9.3 %all-to-all-done.blocks = bf16[8,16,1024]{2,1,0:T(8,128)(2,1)S(1)} async-done(((bf16[8,16,1024]{2,1,0:T(8,128)(2,1)}), bf16[8,16,1024]{2,1,0:T(8,128)(2,1)S(1)}, u32[]{:S(2)}, u32[]{:S(2)}) %all-to-all-start) | async-done | bytes 262176 | tf_op jit(solution)/shard_map/all_to_all | solution.py:477
  110.3 1.2 finish.1
  111.5 3.8 %collective-permute-done.17.refs_1_ = bf16[512,512]{1,0:T(8,128)(2,1)} collective-permute-done((bf16[512,512]{1,0:T(8,128)(2,1)}, bf16[512,512]{1,0:T(8,128)(2,1)}, u32[]{:S(2)}, u32[]{:S(2)}) %collective-permute-start.17) | collective-permute-done | bytes 524320 | tf_op jit(solution)/shard_map/ppermute | solution.py:27
  115.3 0.6 collective-permute-done.19.refs_3_
  115.9 2.8 %evict.1 = (bf16[2048,256]{1,0:T(8,128)(2,1)S(1)}, f32[136,128]{1,0:T(8,128)S(1)}, f32[136,128]{1,0:T(8,128)S(1)}, f32[136,128]{1,0:T(8,128)S(1)}, f32[136,128]{1,0:T(8,128)S(1)}) custom-call(f32[1,2048]{1,0:T(1,128)S(1)} %convert_element_type.64.slot_map, f32[3,520,128]{2,1,0:T(8,128)S(1)} %leave.1.leaving, ...), custom_call_target="tpu_custom_call" | custom-call | flops 536870912 | bytes 4194304 | tf_op jit(solution)/shard_map/evict/pallas_call | solution.py:508
  118.7 1.0 collective-permute-start.20
  119.7 1.8 %collective-permute-start.21 = (f32[136,128]{1,0:T(8,128)S(1)}, f32[136,128]{1,0:T(8,128)S(1)}, u32[]{:S(2)}, u32[]{:S(2)}) collective-permute-start(f32[136,128]{1,0:T(8,128)S(1)} %get-tuple-element.347), channel_id=1, source_target_pairs={{0,2},{1,3},{2,0},{3,1},{4,6},{5,7},{6,4},{7,5},{8,10},{9,11},{10,... | collective-permute-start | bytes 208904 | tf_op jit(solution)/shard_map/ppermute | solution.py:27
  121.5 2.5 %collective-permute-start.22 = (f32[136,128]{1,0:T(8,128)S(1)}, f32[136,128]{1,0:T(8,128)S(1)}, u32[]{:S(2)}, u32[]{:S(2)}) collective-permute-start(f32[136,128]{1,0:T(8,128)S(1)} %get-tuple-element.348), channel_id=1, source_target_pairs={{0,3},{1,0},{2,1},{3,2},{4,7},{5,4},{6,5},{7,6},{8,11},{9,8},{10,9... | collective-permute-start | bytes 208904 | tf_op jit(solution)/shard_map/ppermute | solution.py:27
  124.1 4.3 %update.1 = (f32[2048,128]{1,0:T(8,128)}, f32[16,128]{1,0:T(8,128)}) custom-call(f32[1,2048]{1,0:T(1,128)S(1)} %convert_element_type.64.slot_map, bf16[2048,256]{1,0:T(8,128)(2,1)S(1)} %get-tuple-element.342.rhs, f32[2048,128]{1,0:T(8,128)S(1)} %bitcast.29, f32[16,128]{1,0:T(8,128)S(1)} %bitcast.34), custom_call_target="tpu_custom_call" | custom-call | flops 2147483648 | bytes 4194304 | tf_op jit(solution)/shard_map/update/pallas_call | solution.py:518
  128.4 1.3 arrive.1
  (58 shorter events, 3.9 us)
Async XLA Ops:
  1.2 12.2 %copy-start.2 = (s32[2,512,8]{1,2,0:T(8,128)S(1)}, s32[2,512,8]{1,2,0:T(8,128)}, u32[]{:S(2)}) copy-start(s32[2,512,8]{1,2,0:T(8,128)} %param.16) | copy-start | bytes 98308
  1.2 12.2 %copy-start.3 = (s32[2,512,8]{1,2,0:T(8,128)S(1)}, s32[2,512,8]{1,2,0:T(8,128)}, u32[]{:S(2)}) copy-start(s32[2,512,8]{1,2,0:T(8,128)} %param.17) | copy-start | bytes 98308
  1.2 12.2 %copy-start.4 = (bf16[2,512,8]{1,2,0:T(8,128)(2,1)S(1)}, bf16[2,512,8]{1,2,0:T(8,128)(2,1)}, u32[]{:S(2)}) copy-start(bf16[2,512,8]{1,2,0:T(8,128)(2,1)} %param.18) | copy-start | bytes 49156
  1.2 12.2 %copy-start.7 = (s32[2,512]{1,0:T(2,128)S(1)}, s32[2,512]{1,0:T(2,128)}, u32[]{:S(2)}) copy-start(s32[2,512]{1,0:T(2,128)} %lens) | copy-start | bytes 12292
  1.2 30.4 %copy-start.6 = (s32[4]{0:T(128)S(1)}, s32[4]{0:T(128)}, u32[]{:S(2)}) copy-start(s32[4]{0:T(128)} %pad_add_fusion.pos) | copy-start | bytes 52
  1.3 30.4 %copy-start.9 = (bf16[512,1024]{1,0:T(8,128)(2,1)S(1)}, bf16[512,1024]{1,0:T(8,128)(2,1)}, u32[]{:S(2)}) copy-start(bf16[512,1024]{1,0:T(8,128)(2,1)} %pooled.3) | copy-start | bytes 3145732
  8.5 9.6 %collective-permute-start = (bf16[1024,128]{1,0:T(8,128)(2,1)}, bf16[1024,128]{1,0:T(8,128)(2,1)S(1)}, u32[]{:S(2)}, u32[]{:S(2)}) collective-permute-start(bf16[1024,128]{1,0:T(8,128)(2,1)} %get-tuple-element.179), channel_id=1, source_target_pairs={{0,1},{1,2},{2,3},{3,0},{4,5},{5,6},{6,7},{7,4},{8,9},{9,10},{10,1... | collective-permute-start | bytes 786440 | tf_op jit(solution)/shard_map/ppermute | solution.py:27
  10.1 10.9 %collective-permute-start.1 = (bf16[1024,128]{1,0:T(8,128)(2,1)}, bf16[1024,128]{1,0:T(8,128)(2,1)S(1)}, u32[]{:S(2)}, u32[]{:S(2)}) collective-permute-start(bf16[1024,128]{1,0:T(8,128)(2,1)} %get-tuple-element.180), channel_id=1, source_target_pairs={{0,2},{1,3},{2,0},{3,1},{4,6},{5,7},{6,4},{7,5},{8,10},{9,11},{10,... | collective-permute-start | bytes 786440 | tf_op jit(solution)/shard_map/ppermute | solution.py:27
  12.8 11.6 %collective-permute-start.2 = (bf16[1024,128]{1,0:T(8,128)(2,1)}, bf16[1024,128]{1,0:T(8,128)(2,1)S(1)}, u32[]{:S(2)}, u32[]{:S(2)}) collective-permute-start(bf16[1024,128]{1,0:T(8,128)(2,1)} %get-tuple-element.181), channel_id=1, source_target_pairs={{0,3},{1,0},{2,1},{3,2},{4,7},{5,4},{6,5},{7,6},{8,11},{9,8},{10,9... | collective-permute-start | bytes 786440 | tf_op jit(solution)/shard_map/ppermute | solution.py:27
  24.4 1.0 copy-start.1
  25.6 13.0 %collective-permute-start.3 = (bf16[1280,128]{1,0:T(8,128)(2,1)S(1)}, bf16[1280,128]{1,0:T(8,128)(2,1)S(1)}, u32[]{:S(2)}, u32[]{:S(2)}) collective-permute-start(bf16[1280,128]{1,0:T(8,128)(2,1)S(1)} %own.1.refs_0_), channel_id=1, source_target_pairs={{0,32},{32,64},{64,96},{96,128},{128,160},{160,192},{192,224},{224... | collective-permute-start | bytes 983048 | tf_op jit(solution)/shard_map/ppermute | solution.py:27
  27.6 11.0 %collective-permute-start.4 = (bf16[1280,128]{1,0:T(8,128)(2,1)S(1)}, bf16[1280,128]{1,0:T(8,128)(2,1)S(1)}, u32[]{:S(2)}, u32[]{:S(2)}) collective-permute-start(bf16[1280,128]{1,0:T(8,128)(2,1)S(1)} %own.1.refs_0_), channel_id=1, source_target_pairs={{0,224},{32,0},{64,32},{96,64},{128,96},{160,128},{192,160},{224,1... | collective-permute-start | bytes 983048 | tf_op jit(solution)/shard_map/ppermute | solution.py:27
  31.6 1.2 copy-start.10
  38.6 4.2 %collective-permute-start.7 = (f32[4,8,16,1024]{3,2,1,0:T(8,128)S(1)}, f32[4,8,16,1024]{3,2,1,0:T(8,128)S(1)}, u32[]{:S(2)}, u32[]{:S(2)}) collective-permute-start(f32[4,8,16,1024]{3,2,1,0:T(8,128)S(1)} %get-tuple-element.212), channel_id=1, source_target_pairs={{0,4},{4,0},{1,5},{5,1},{2,6},{6,2},{3,7},{7,3},{8,12},{12,8},{9,1... | collective-permute-start | bytes 6291464 | tf_op jit(solution)/shard_map/ppermute | solution.py:27
  38.6 11.4 %collective-permute-start.5 = (bf16[1280,128]{1,0:T(8,128)(2,1)S(1)}, bf16[1280,128]{1,0:T(8,128)(2,1)S(1)}, u32[]{:S(2)}, u32[]{:S(2)}) collective-permute-start(bf16[1280,128]{1,0:T(8,128)(2,1)S(1)} %collective-permute-done.3.refs_0_), channel_id=1, source_target_pairs={{0,32},{32,64},{64,96},{96,128},{128,160},{160,192},{192,224},{224... | collective-permute-start | bytes 983048 | tf_op jit(solution)/shard_map/ppermute | solution.py:27
  38.6 11.4 %collective-permute-start.6 = (bf16[1280,128]{1,0:T(8,128)(2,1)S(1)}, bf16[1280,128]{1,0:T(8,128)(2,1)S(1)}, u32[]{:S(2)}, u32[]{:S(2)}) collective-permute-start(bf16[1280,128]{1,0:T(8,128)(2,1)S(1)} %collective-permute-done.4.refs_1_), channel_id=1, source_target_pairs={{0,224},{32,0},{64,32},{96,64},{128,96},{160,128},{192,160},{224,1... | collective-permute-start | bytes 983048 | tf_op jit(solution)/shard_map/ppermute | solution.py:27
  50.0 14.6 %collective-permute-start.8 = (bf16[1280,128]{1,0:T(8,128)(2,1)S(1)}, bf16[1280,128]{1,0:T(8,128)(2,1)S(1)}, u32[]{:S(2)}, u32[]{:S(2)}) collective-permute-start(bf16[1280,128]{1,0:T(8,128)(2,1)S(1)} %collective-permute-done.5.refs_0_), channel_id=1, source_target_pairs={{0,32},{32,64},{64,96},{96,128},{128,160},{160,192},{192,224},{224... | collective-permute-start | bytes 983048 | tf_op jit(solution)/shard_map/ppermute | solution.py:27
  52.3 12.2 %collective-permute-start.9 = (bf16[1280,128]{1,0:T(8,128)(2,1)S(1)}, bf16[1280,128]{1,0:T(8,128)(2,1)S(1)}, u32[]{:S(2)}, u32[]{:S(2)}) collective-permute-start(bf16[1280,128]{1,0:T(8,128)(2,1)S(1)} %collective-permute-done.6.refs_1_), channel_id=1, source_target_pairs={{0,224},{32,0},{64,32},{96,64},{128,96},{160,128},{192,160},{224,1... | collective-permute-start | bytes 983048 | tf_op jit(solution)/shard_map/ppermute | solution.py:27
  53.2 17.7 %collective-permute-start.12 = (bf16[8,16,1024]{2,1,0:T(8,128)(2,1)S(1)}, bf16[8,16,1024]{2,1,0:T(8,128)(2,1)S(1)}, u32[]{:S(2)}, u32[]{:S(2)}) collective-permute-start(bf16[8,16,1024]{2,1,0:T(8,128)(2,1)S(1)} %get-tuple-element.249), channel_id=1, source_target_pairs={{0,8},{8,16},{16,24},{24,0},{1,9},{9,17},{17,25},{25,1},{2,10},{10... | collective-permute-start | bytes 786440 | tf_op jit(solution)/shard_map/ppermute | solution.py:27
  54.7 16.2 %collective-permute-start.13 = (bf16[8,16,1024]{2,1,0:T(8,128)(2,1)S(1)}, bf16[8,16,1024]{2,1,0:T(8,128)(2,1)S(1)}, u32[]{:S(2)}, u32[]{:S(2)}) collective-permute-start(bf16[8,16,1024]{2,1,0:T(8,128)(2,1)S(1)} %get-tuple-element.250), channel_id=1, source_target_pairs={{0,16},{8,24},{16,0},{24,8},{1,17},{9,25},{17,1},{25,9},{2,18},{10... | collective-permute-start | bytes 786440 | tf_op jit(solution)/shard_map/ppermute | solution.py:27
  57.4 13.5 %collective-permute-start.14 = (bf16[8,16,1024]{2,1,0:T(8,128)(2,1)S(1)}, bf16[8,16,1024]{2,1,0:T(8,128)(2,1)S(1)}, u32[]{:S(2)}, u32[]{:S(2)}) collective-permute-start(bf16[8,16,1024]{2,1,0:T(8,128)(2,1)S(1)} %get-tuple-element.251), channel_id=1, source_target_pairs={{0,24},{8,0},{16,8},{24,16},{1,25},{9,1},{17,9},{25,17},{2,26},{10... | collective-permute-start | bytes 786440 | tf_op jit(solution)/shard_map/ppermute | solution.py:27
  64.6 6.6 %collective-permute-start.10 = (bf16[640,128]{1,0:T(8,128)(2,1)S(1)}, bf16[640,128]{1,0:T(8,128)(2,1)S(1)}, u32[]{:S(2)}, u32[]{:S(2)}) collective-permute-start(bf16[640,128]{1,0:T(8,128)(2,1)S(1)} %slice.25), channel_id=1, source_target_pairs={{0,32},{32,64},{64,96},{96,128},{128,160},{160,192},{192,224},{224... | collective-permute-start | bytes 491528 | tf_op jit(solution)/shard_map/ppermute | solution.py:27
  65.9 5.4 %collective-permute-start.11 = (bf16[640,128]{1,0:T(8,128)(2,1)S(1)}, bf16[640,128]{1,0:T(8,128)(2,1)S(1)}, u32[]{:S(2)}, u32[]{:S(2)}) collective-permute-start(bf16[640,128]{1,0:T(8,128)(2,1)S(1)} %slice.26), channel_id=1, source_target_pairs={{0,224},{32,0},{64,32},{96,64},{128,96},{160,128},{192,160},{224,1... | collective-permute-start | bytes 491528 | tf_op jit(solution)/shard_map/ppermute | solution.py:27
  78.0 2.7 %collective-permute-start.16 = (bf16[4,256,512]{2,1,0:T(8,128)(2,1)S(1)}, bf16[4,256,512]{2,1,0:T(8,128)(2,1)S(1)}, u32[]{:S(2)}, u32[]{:S(2)}) collective-permute-start(bf16[4,256,512]{2,1,0:T(8,128)(2,1)S(1)} %send1.1), channel_id=1, source_target_pairs={{0,4},{4,0},{1,5},{5,1},{2,6},{6,2},{3,7},{7,3},{8,12},{12,8},{9,1... | collective-permute-start | bytes 3145736 | tf_op jit(solution)/shard_map/ppermute | solution.py:27
  78.1 4.1 %collective-permute-start.15 = (bf16[4,256,512]{2,1,0:T(8,128)(2,1)S(1)}, bf16[4,256,512]{2,1,0:T(8,128)(2,1)S(1)}, u32[]{:S(2)}, u32[]{:S(2)}) collective-permute-start(bf16[4,256,512]{2,1,0:T(8,128)(2,1)S(1)} %send0.1), channel_id=1, source_target_pairs={{0,4},{4,0},{1,5},{5,1},{2,6},{6,2},{3,7},{7,3},{8,12},{12,8},{9,1... | collective-permute-start | bytes 3145736 | tf_op jit(solution)/shard_map/ppermute | solution.py:27
  79.4 19.3 %copy-start.11 = (s32[1,1,2048]{2,1,0:T(1,128)S(1)}, s32[1,1,2048]{2,1,0:T(1,128)}, u32[]{:S(2)}) copy-start(s32[1,1,2048]{2,1,0:T(1,128)} %param.20) | copy-start | bytes 24580
  79.4 19.7 %copy-start.12 = (s32[1,1,256]{2,1,0:T(1,128)S(1)}, s32[1,1,256]{2,1,0:T(1,128)}, u32[]{:S(2)}) copy-start(s32[1,1,256]{2,1,0:T(1,128)} %param.24) | copy-start | bytes 3076
  79.4 19.9 %copy-start.5 = (f32[1,1,2048]{2,1,0:T(1,128)S(1)}, f32[1,1,2048]{2,1,0:T(1,128)}, u32[]{:S(2)}) copy-start(f32[1,1,2048]{2,1,0:T(1,128)} %param.22) | copy-start | bytes 24580
  79.4 19.9 %copy-start.8 = (s32[1,1,256]{2,1,0:T(1,128)S(1)}, s32[1,1,256]{2,1,0:T(1,128)}, u32[]{:S(2)}) copy-start(s32[1,1,256]{2,1,0:T(1,128)} %param.23) | copy-start | bytes 3076
  88.6 10.8 %copy-start = (f32[1,1,2048,128]{3,2,1,0:T(8,128)S(1)}, f32[1,1,2048,128]{3,2,1,0:T(8,128)}, u32[]{:S(2)}) copy-start(f32[1,1,2048,128]{3,2,1,0:T(8,128)} %param.21) | copy-start | bytes 3145732
  88.6 26.7 %collective-permute-start.17 = (bf16[512,512]{1,0:T(8,128)(2,1)}, bf16[512,512]{1,0:T(8,128)(2,1)}, u32[]{:S(2)}, u32[]{:S(2)}) collective-permute-start(bf16[512,512]{1,0:T(8,128)(2,1)} %get-tuple-element.339), channel_id=1, source_target_pairs={{0,8},{8,16},{16,24},{24,0},{1,9},{9,17},{17,25},{25,1},{2,10},{10... | collective-permute-start | bytes 1572872 | tf_op jit(solution)/shard_map/ppermute | solution.py:27
  89.2 26.1 %collective-permute-start.18 = (bf16[512,512]{1,0:T(8,128)(2,1)}, bf16[512,512]{1,0:T(8,128)(2,1)}, u32[]{:S(2)}, u32[]{:S(2)}) collective-permute-start(bf16[512,512]{1,0:T(8,128)(2,1)} %get-tuple-element.340), channel_id=1, source_target_pairs={{0,16},{8,24},{16,0},{24,8},{1,17},{9,25},{17,1},{25,9},{2,18},{10... | collective-permute-start | bytes 1572872 | tf_op jit(solution)/shard_map/ppermute | solution.py:27
  90.0 25.9 %collective-permute-start.19 = (bf16[512,512]{1,0:T(8,128)(2,1)}, bf16[512,512]{1,0:T(8,128)(2,1)}, u32[]{:S(2)}, u32[]{:S(2)}) collective-permute-start(bf16[512,512]{1,0:T(8,128)(2,1)} %get-tuple-element.341), channel_id=1, source_target_pairs={{0,24},{8,0},{16,8},{24,16},{1,25},{9,1},{17,9},{25,17},{2,26},{10... | collective-permute-start | bytes 1572872 | tf_op jit(solution)/shard_map/ppermute | solution.py:27
  92.6 17.7 %all-to-all-start = ((bf16[8,16,1024]{2,1,0:T(8,128)(2,1)}), bf16[8,16,1024]{2,1,0:T(8,128)(2,1)S(1)}, u32[]{:S(2)}, u32[]{:S(2)}) async-start(bf16[8,16,1024]{2,1,0:T(8,128)(2,1)} %convert_element_type.60), calls=%async_computation | async-start | bytes 524288 | tf_op jit(solution)/shard_map/all_to_all | solution.py:477
  118.7 9.7 %collective-permute-start.20 = (f32[136,128]{1,0:T(8,128)S(1)}, f32[136,128]{1,0:T(8,128)S(1)}, u32[]{:S(2)}, u32[]{:S(2)}) collective-permute-start(f32[136,128]{1,0:T(8,128)S(1)} %get-tuple-element.346), channel_id=1, source_target_pairs={{0,1},{1,2},{2,3},{3,0},{4,5},{5,6},{6,7},{7,4},{8,9},{9,10},{10,1... | collective-permute-start | bytes 208904 | tf_op jit(solution)/shard_map/ppermute | solution.py:27
  119.7 8.7 %collective-permute-start.21 = (f32[136,128]{1,0:T(8,128)S(1)}, f32[136,128]{1,0:T(8,128)S(1)}, u32[]{:S(2)}, u32[]{:S(2)}) collective-permute-start(f32[136,128]{1,0:T(8,128)S(1)} %get-tuple-element.347), channel_id=1, source_target_pairs={{0,2},{1,3},{2,0},{3,1},{4,6},{5,7},{6,4},{7,5},{8,10},{9,11},{10,... | collective-permute-start | bytes 208904 | tf_op jit(solution)/shard_map/ppermute | solution.py:27
  121.5 6.8 %collective-permute-start.22 = (f32[136,128]{1,0:T(8,128)S(1)}, f32[136,128]{1,0:T(8,128)S(1)}, u32[]{:S(2)}, u32[]{:S(2)}) collective-permute-start(f32[136,128]{1,0:T(8,128)S(1)} %get-tuple-element.348), channel_id=1, source_target_pairs={{0,3},{1,0},{2,1},{3,2},{4,7},{5,4},{6,5},{7,6},{8,11},{9,8},{10,9... | collective-permute-start | bytes 208904 | tf_op jit(solution)/shard_map/ppermute | solution.py:27

commit v6 on v5

--- a/solution.py
+++ b/solution.py
@@ -432,11 +432,12 @@
     mid = (shifted(up, Z, 1), shifted(down, Z, -1))
     grad_x = grad + there
     total, blocks = grad_x[0], [grad_x[k].astype(BF16) for k in (1, 2, 3)]
-    mid, near, (total,), blocks = together(mid, near, (total,), blocks)
+    early = pick(1, near)
+    mid, near, (total,), blocks, early = together(mid, near, (total,), blocks, early)
     up, down = mid
     got_x = [shifted(blocks[k - 1], X, k) for k in (1, 2, 3)]
     far = (shifted(up, Z, 1), shifted(down, Z, -1))
-    picked.append(pick(1, near))
+    picked.append(early)
     picked.append(pick(2, mid))
     far, picked[1], picked[2] = together(far, picked[1], picked[2])
     up, down = far
@@ -474,17 +475,6 @@
         (arrived[0], total, slot_map, evict_slots, evict_dest)
     )
     arrived[0] = first
-    blocks = lax.all_to_all(total.astype(BF16), Z, split_axis=0, concat_axis=0, tiled=True)
-    (grad_up,) = call(
-        finish_kernel,
-        [SMEM, VMEM, VMEM],
-        [shape((16, 1024), F32)],
-        [],
-        1 << 10,
-        1 << 18,
-        "finish",
-    )(pos, total, blocks)
-
     list_len = evict_slots.shape[-1]
     departure = evict_dest[0, 0]
     list_ids = jnp.arange(list_len, dtype=I32)
@@ -505,6 +495,17 @@
         1 << 20,
         "leave",
     )(evict_slots.reshape(-1), goal, cache_accum.reshape(-1), cache_weight[0, 0])
+    (total,), _ = together((total,), leaving)
+    blocks = lax.all_to_all(total.astype(BF16), Z, split_axis=0, concat_axis=0, tiled=True)
+    (grad_up,) = call(
+        finish_kernel,
+        [SMEM, VMEM, VMEM],
+        [shape((16, 1024), F32)],
+        [],
+        1 << 10,
+        1 << 18,
+        "finish",
+    )(pos, total, blocks)
     rhs, *held = call(
         evict_kernel,
         [VMEM] * 6,

time: 130 us -> 130 us (level)
  blocking collectives: 0 us -> 14.3 us
  waiting for transfers between devices: 37.1 us -> 29.1 us
  starting transfers between devices: 41.8 us -> 36.8 us
    all_to_all x0 -> x1, blocking collectives: none -> 14.3 us  [on_device(): lax.all_to_all(total.astype(BF16), Z, split_axis=0, concat_axis=0, tiled=...]
    all_to_all x1 -> x0, waiting for transfers between devices: 9.33 us -> none  [on_device(): lax.all_to_all(total.astype(BF16), Z, split_axis=0, concat_axis=0, tiled=...]
    all_to_all x1 -> x0, starting transfers between devices: 6.09 us -> none  [on_device(): lax.all_to_all(total.astype(BF16), Z, split_axis=0, concat_axis=0, tiled=...]
    ppermute x23, waiting for transfers between devices: 27.8 us -> 29.1 us  [shifted(): return lax.ppermute(x, axis, [(i, (i + step) % size) for i in range(size)])]
  transfers between devices with their start and end apart: 24 -> 23, of which waited for: 13 -> 10; matrix products, arithmetic and copies ran while one was open for 2% -> 1% of each run, Pallas kernels for 15% -> 17%
where the time goes in v6:
time: 130 us
  Pallas kernels  43.8 us (34%)
  starting transfers between devices  36.8 us (28%)
  waiting for transfers between devices  29.1 us (22%)
  blocking collectives  14.3 us (11%)
  local copies, waits for them, and re-layouts  2.84 us (2%)
  between operations  1.59 us (1%)
  other arithmetic  1.36 us (1%)
    ppermute x23, starting transfers between devices, shifted(): return lax.ppermute(x, axis, [(i, (i + step) % size) for i in range(size)])  36.8 us
    ppermute x23, waiting for transfers between devices, shifted(): return lax.ppermute(x, axis, [(i, (i + step) % size) for i in range(size)])  29.1 us
    all_to_all x1, blocking collectives, on_device(): lax.all_to_all(total.astype(BF16), Z, split_axis=0, concat_axis=0, tiled=...  14.3 us
    pallas_call x5, Pallas kernels, pick(): call(functools.partial(pick_kernel, count), [SMEM, VMEM] + [VMEM] * len(b...  11.9 us
    pallas_call x1, Pallas kernels, on_device(): call(top_kernel, [SMEM, VMEM, VMEM, VMEM], [shape((bags, 1024), BF16), sh...  7.23 us
    pallas_call x1, Pallas kernels, on_device(): call(keep_kernel, [VMEM] * 32, [shape((512, 512), BF16)] * 4, work + [plt...  6.3 us
    pallas_call x2, Pallas kernels, on_device(): call(send_kernel, [VMEM] * 15, [shape((4, 256, 512), BF16)], work, 4 << 3...  5.03 us
    pallas_call x1, Pallas kernels, on_device(): call(update_kernel, [VMEM] * 4, [shape((2048, 128), F32), shape((16, 128)...  4.31 us
  transfers between devices with their start and end apart: 23, of which 10 were waited for; matrix products, arithmetic and copies ran while one was open for 1% of the time, Pallas kernels for 17%

profile of v6, /device:TPU:8, one launch (start us, length us, event | category | flops | bytes accessed | tf_op | source)
XLA Modules:
  0.0 130.0 jit_solution(17079945455133583470)
XLA Ops:
  0.6 0.6 pad_add_fusion.pos
  1.3 7.2 %top.1 = (bf16[512,1024]{1,0:T(8,128)(2,1)}, f32[1024,128]{1,0:T(8,128)}, bf16[1024,128]{1,0:T(8,128)(2,1)}, bf16[1024,128]{1,0:T(8,128)(2,1)}, bf16[1024,128]{1,0:T(8,128)(2,1)}) custom-call(s32[4]{0:T(128)} %pad_add_fusion.pos, bf16[512,1024]{1,0:T(8,128)(2,1)} %pooled.3, bf16[1024,1024]{1,0:T(8,128)(2,1)} %w_up.1, bf16[512,1024]{1,0:T(8,128)(2,1)} %grad_out.1), custom_call_target="tpu_custom_call" | custom-call | flops 2147483648 | bytes 6291456 | tf_op jit(solution)/shard_map/top/pallas_call | solution.py:365
  8.5 1.6 %collective-permute-start = (bf16[1024,128]{1,0:T(8,128)(2,1)}, bf16[1024,128]{1,0:T(8,128)(2,1)S(1)}, u32[]{:S(2)}, u32[]{:S(2)}) collective-permute-start(bf16[1024,128]{1,0:T(8,128)(2,1)} %get-tuple-element.190), channel_id=1, source_target_pairs={{0,1},{1,2},{2,3},{3,0},{4,5},{5,6},{6,7},{7,4},{8,9},{9,10},{10,1... | collective-permute-start | bytes 786440 | tf_op jit(solution)/shard_map/ppermute | solution.py:27
  10.1 2.7 %collective-permute-start.1 = (bf16[1024,128]{1,0:T(8,128)(2,1)}, bf16[1024,128]{1,0:T(8,128)(2,1)S(1)}, u32[]{:S(2)}, u32[]{:S(2)}) collective-permute-start(bf16[1024,128]{1,0:T(8,128)(2,1)} %get-tuple-element.191), channel_id=1, source_target_pairs={{0,2},{1,3},{2,0},{3,1},{4,6},{5,7},{6,4},{7,5},{8,10},{9,11},{10,... | collective-permute-start | bytes 786440 | tf_op jit(solution)/shard_map/ppermute | solution.py:27
  12.8 0.7 collective-permute-start.2
  13.5 4.6 %collective-permute-done.one = bf16[1024,128]{1,0:T(8,128)(2,1)S(1)} collective-permute-done((bf16[1024,128]{1,0:T(8,128)(2,1)}, bf16[1024,128]{1,0:T(8,128)(2,1)S(1)}, u32[]{:S(2)}, u32[]{:S(2)}) %collective-permute-start) | collective-permute-done | bytes 262176 | tf_op jit(solution)/shard_map/ppermute | solution.py:27
  18.1 2.9 %collective-permute-done.1.two = bf16[1024,128]{1,0:T(8,128)(2,1)S(1)} collective-permute-done((bf16[1024,128]{1,0:T(8,128)(2,1)}, bf16[1024,128]{1,0:T(8,128)(2,1)S(1)}, u32[]{:S(2)}, u32[]{:S(2)}) %collective-permute-start.1) | collective-permute-done | bytes 262176 | tf_op jit(solution)/shard_map/ppermute | solution.py:27
  21.1 3.4 %collective-permute-done.2.three = bf16[1024,128]{1,0:T(8,128)(2,1)S(1)} collective-permute-done((bf16[1024,128]{1,0:T(8,128)(2,1)}, bf16[1024,128]{1,0:T(8,128)(2,1)S(1)}, u32[]{:S(2)}, u32[]{:S(2)}) %collective-permute-start.2) | collective-permute-done | bytes 262176 | tf_op jit(solution)/shard_map/ppermute | solution.py:27
  24.4 1.0 copy-done.1
  25.6 5.9 %collective-permute-start.4 = (bf16[1280,128]{1,0:T(8,128)(2,1)S(1)}, bf16[1280,128]{1,0:T(8,128)(2,1)S(1)}, u32[]{:S(2)}, u32[]{:S(2)}) collective-permute-start(bf16[1280,128]{1,0:T(8,128)(2,1)S(1)} %own.1.refs_0_), channel_id=1, source_target_pairs={{0,224},{32,0},{64,32},{96,64},{128,96},{160,128},{192,160},{224,1... | collective-permute-start | bytes 983048 | tf_op jit(solution)/shard_map/ppermute | solution.py:27
  31.6 1.2 copy-done.10
  32.8 2.3 %grad.1 = (f32[4,8,16,1024]{3,2,1,0:T(8,128)S(1)}, f32[4,8,16,1024]{3,2,1,0:T(8,128)S(1)}) custom-call(s32[4]{0:T(128)S(1)} %copy-done.6, bf16[512,1024]{1,0:T(8,128)(2,1)S(1)} %copy-done.9, bf16[512,1024]{1,0:T(8,128)(2,1)S(1)} %copy-done.10), custom_call_target="tpu_custom_call" | custom-call | flops 1073741824 | bytes 6291456 | tf_op jit(solution)/shard_map/grad/pallas_call | solution.py:418
  35.1 1.7 %pick0.1 = (bf16[1,4,128,128]{3,2,1,0:T(8,128)(2,1)S(1)}, bf16[1,4,128,128]{3,2,1,0:T(8,128)(2,1)S(1)}, f32[1,8,128]{2,1,0:T(8,128)S(1)}, bf16[1,4,128,128]{3,2,...) custom-call(s32[4]{0:T(128)S(1)} %copy-done.6, ...), custom_call_target="tpu_custom_call" | custom-call | flops 1073741824 | bytes 4194304 | tf_op jit(solution)/shard_map/pick0/pallas_call | solution.py:400
  36.8 1.1 collective-permute-done.4.refs_1_
  37.8 3.4 %collective-permute-done.3.refs_0_ = bf16[1280,128]{1,0:T(8,128)(2,1)S(1)} collective-permute-done((bf16[1280,128]{1,0:T(8,128)(2,1)S(1)}, bf16[1280,128]{1,0:T(8,128)(2,1)S(1)}, u32[]{:S(2)}, u32[]{:S(2)}) %collective-permute-start.3) | collective-permute-done | bytes 327712 | tf_op jit(solution)/shard_map/ppermute | solution.py:27
  41.3 3.2 %collective-permute-start.6 = (bf16[1280,128]{1,0:T(8,128)(2,1)S(1)}, bf16[1280,128]{1,0:T(8,128)(2,1)S(1)}, u32[]{:S(2)}, u32[]{:S(2)}) collective-permute-start(bf16[1280,128]{1,0:T(8,128)(2,1)S(1)} %collective-permute-done.4.refs_1_), channel_id=1, source_target_pairs={{0,224},{32,0},{64,32},{96,64},{128,96},{160,128},{192,160},{224,1... | collective-permute-start | bytes 983048 | tf_op jit(solution)/shard_map/ppermute | solution.py:27
  44.5 2.9 %pick1.1 = (bf16[2,4,128,128]{3,2,1,0:T(8,128)(2,1)S(1)}, bf16[2,4,128,128]{3,2,1,0:T(8,128)(2,1)S(1)}, f32[2,8,128]{2,1,0:T(8,128)S(1)}, bf16[2,4,128,128]{3,2,...) custom-call(s32[4]{0:T(128)S(1)} %copy-done.6, ...), custom_call_target="tpu_custom_call" | custom-call | flops 1073741824 | bytes 4194304 | tf_op jit(solution)/shard_map/pick1/pallas_call | solution.py:400
  47.3 0.5 fusion.10
  48.0 4.6 %collective-permute-done.5.refs_0_ = bf16[1280,128]{1,0:T(8,128)(2,1)S(1)} collective-permute-done((bf16[1280,128]{1,0:T(8,128)(2,1)S(1)}, bf16[1280,128]{1,0:T(8,128)(2,1)S(1)}, u32[]{:S(2)}, u32[]{:S(2)}) %collective-permute-start.5) | collective-permute-done | bytes 327712 | tf_op jit(solution)/shard_map/ppermute | solution.py:27
  52.6 3.2 %collective-permute-start.9 = (bf16[1280,128]{1,0:T(8,128)(2,1)S(1)}, bf16[1280,128]{1,0:T(8,128)(2,1)S(1)}, u32[]{:S(2)}, u32[]{:S(2)}) collective-permute-start(bf16[1280,128]{1,0:T(8,128)(2,1)S(1)} %collective-permute-done.6.refs_1_), channel_id=1, source_target_pairs={{0,224},{32,0},{64,32},{96,64},{128,96},{160,128},{192,160},{224,1... | collective-permute-start | bytes 983048 | tf_op jit(solution)/shard_map/ppermute | solution.py:27
  55.8 1.5 %collective-permute-start.12 = (bf16[8,16,1024]{2,1,0:T(8,128)(2,1)S(1)}, bf16[8,16,1024]{2,1,0:T(8,128)(2,1)S(1)}, u32[]{:S(2)}, u32[]{:S(2)}) collective-permute-start(bf16[8,16,1024]{2,1,0:T(8,128)(2,1)S(1)} %get-tuple-element.270), channel_id=1, source_target_pairs={{0,8},{8,16},{16,24},{24,0},{1,9},{9,17},{17,25},{25,1},{2,10},{10... | collective-permute-start | bytes 786440 | tf_op jit(solution)/shard_map/ppermute | solution.py:27
  57.3 2.7 %collective-permute-start.13 = (bf16[8,16,1024]{2,1,0:T(8,128)(2,1)S(1)}, bf16[8,16,1024]{2,1,0:T(8,128)(2,1)S(1)}, u32[]{:S(2)}, u32[]{:S(2)}) collective-permute-start(bf16[8,16,1024]{2,1,0:T(8,128)(2,1)S(1)} %get-tuple-element.271), channel_id=1, source_target_pairs={{0,16},{8,24},{16,0},{24,8},{1,17},{9,25},{17,1},{25,9},{2,18},{10... | collective-permute-start | bytes 786440 | tf_op jit(solution)/shard_map/ppermute | solution.py:27
  60.0 1.4 %collective-permute-start.14 = (bf16[8,16,1024]{2,1,0:T(8,128)(2,1)S(1)}, bf16[8,16,1024]{2,1,0:T(8,128)(2,1)S(1)}, u32[]{:S(2)}, u32[]{:S(2)}) collective-permute-start(bf16[8,16,1024]{2,1,0:T(8,128)(2,1)S(1)} %get-tuple-element.272), channel_id=1, source_target_pairs={{0,24},{8,0},{16,8},{24,16},{1,25},{9,1},{17,9},{25,17},{2,26},{10... | collective-permute-start | bytes 786440 | tf_op jit(solution)/shard_map/ppermute | solution.py:27
  61.5 2.9 %pick2.1 = (bf16[2,4,128,128]{3,2,1,0:T(8,128)(2,1)S(1)}, bf16[2,4,128,128]{3,2,1,0:T(8,128)(2,1)S(1)}, f32[2,8,128]{2,1,0:T(8,128)S(1)}, bf16[2,4,128,128]{3,2,...) custom-call(s32[4]{0:T(128)S(1)} %copy-done.6, ...), custom_call_target="tpu_custom_call" | custom-call | flops 1073741824 | bytes 4194304 | tf_op jit(solution)/shard_map/pick2/pallas_call | solution.py:400
  64.4 1.8 %collective-permute-start.11 = (bf16[640,128]{1,0:T(8,128)(2,1)S(1)}, bf16[640,128]{1,0:T(8,128)(2,1)S(1)}, u32[]{:S(2)}, u32[]{:S(2)}) collective-permute-start(bf16[640,128]{1,0:T(8,128)(2,1)S(1)} %slice.26), channel_id=1, source_target_pairs={{0,224},{32,0},{64,32},{96,64},{128,96},{160,128},{192,160},{224,1... | collective-permute-start | bytes 491528 | tf_op jit(solution)/shard_map/ppermute | solution.py:27
  66.2 0.3 collective-permute-start.10
  66.5 2.9 %pick3.1 = (bf16[2,4,128,128]{3,2,1,0:T(8,128)(2,1)S(1)}, bf16[2,4,128,128]{3,2,1,0:T(8,128)(2,1)S(1)}, f32[2,8,128]{2,1,0:T(8,128)S(1)}, bf16[2,4,128,128]{3,2,...) custom-call(s32[4]{0:T(128)S(1)} %copy-done.6, ...), custom_call_target="tpu_custom_call" | custom-call | flops 1073741824 | bytes 4194304 | tf_op jit(solution)/shard_map/pick3/pallas_call | solution.py:400
  69.4 1.6 %collective-permute-done.13 = bf16[8,16,1024]{2,1,0:T(8,128)(2,1)S(1)} collective-permute-done((bf16[8,16,1024]{2,1,0:T(8,128)(2,1)S(1)}, bf16[8,16,1024]{2,1,0:T(8,128)(2,1)S(1)}, u32[]{:S(2)}, u32[]{:S(2)}) %collective-permute-start.13) | collective-permute-done | bytes 262176 | tf_op jit(solution)/shard_map/ppermute | solution.py:27
  71.0 1.7 %collective-permute-done.10.refs_0_ = bf16[640,128]{1,0:T(8,128)(2,1)S(1)} collective-permute-done((bf16[640,128]{1,0:T(8,128)(2,1)S(1)}, bf16[640,128]{1,0:T(8,128)(2,1)S(1)}, u32[]{:S(2)}, u32[]{:S(2)}) %collective-permute-start.10) | collective-permute-done | bytes 163872 | tf_op jit(solution)/shard_map/ppermute | solution.py:27
  72.7 1.7 %pick4.1 = (bf16[1,4,128,128]{3,2,1,0:T(8,128)(2,1)S(1)}, bf16[1,4,128,128]{3,2,1,0:T(8,128)(2,1)S(1)}, f32[1,8,128]{2,1,0:T(8,128)S(1)}, bf16[1,4,128,128]{3,2,...) custom-call(s32[4]{0:T(128)S(1)} %copy-done.6, ...), custom_call_target="tpu_custom_call" | custom-call | flops 1073741824 | bytes 4194304 | tf_op jit(solution)/shard_map/pick4/pallas_call | solution.py:400
  74.4 2.5 %send0.1 = bf16[4,256,512]{2,1,0:T(8,128)(2,1)S(1)} custom-call(bf16[1,4,128,128]{3,2,1,0:T(8,128)(2,1)S(1)} %get-tuple-element.217.refs_0_, bf16[1,4,128,128]{3,2,1,0:T(8,128)(2,1)S(1)} %get-tuple-element.218.refs_1_, f32[1,8,128]{2,1,0:T(8,128)S(1)} %get-tuple-element.219.refs_2_, bf16[2,4,128,128]{3,2,1,0:T(8,128)(2,1)S(1)} %get-tuple-element.262.refs_3_, ...), custom_call_target="tpu_custom_call" | custom-call | flops 4294967296 | bytes 5242880 | tf_op jit(solution)/shard_map/send0/pallas_call | solution.py:456
  77.0 2.5 %send1.1 = bf16[4,256,512]{2,1,0:T(8,128)(2,1)S(1)} custom-call(bf16[1,4,128,128]{3,2,1,0:T(8,128)(2,1)S(1)} %get-tuple-element.303.refs_0_, bf16[1,4,128,128]{3,2,1,0:T(8,128)(2,1)S(1)} %get-tuple-element.304.refs_1_, f32[1,8,128]{2,1,0:T(8,128)S(1)} %get-tuple-element.305.refs_2_, bf16[2,4,128,128]{3,2,1,0:T(8,128)(2,1)S(1)} %get-tuple-element.306.refs_3_, ...), custom_call_target="tpu_custom_call" | custom-call | flops 4294967296 | bytes 5242880 | tf_op jit(solution)/shard_map/send1/pallas_call | solution.py:456
  79.5 0.6 collective-permute-start.16
  81.0 1.4 %collective-permute-done.16.other1 = bf16[4,256,512]{2,1,0:T(8,128)(2,1)S(1)} collective-permute-done((bf16[4,256,512]{2,1,0:T(8,128)(2,1)S(1)}, bf16[4,256,512]{2,1,0:T(8,128)(2,1)S(1)}, u32[]{:S(2)}, u32[]{:S(2)}) %collective-permute-start.16) | collective-permute-done | bytes 1048608 | tf_op jit(solution)/shard_map/ppermute | solution.py:27
  82.4 6.3 %keep.1 = (bf16[512,512]{1,0:T(8,128)(2,1)S(1)}, bf16[512,512]{1,0:T(8,128)(2,1)}, bf16[512,512]{1,0:T(8,128)(2,1)}, bf16[512,512]{1,0:T(8,128)(2,1)}) custom-call(bf16[4,256,512]{2,1,0:T(8,128)(2,1)S(1)} %collective-permute-done.15.other0, bf16[4,256,512]{2,1,0:T(8,128)(2,1)S(1)} %collective-permute-done.16.other1, ...), custom_call_target="tpu_custom_call" | custom-call | flops 8589934592 | bytes 10485760 | tf_op jit(solution)/shard_map/keep/pallas_call | solution.py:461
  88.7 1.5 %collective-permute-start.17 = (bf16[512,512]{1,0:T(8,128)(2,1)}, bf16[512,512]{1,0:T(8,128)(2,1)S(1)}, u32[]{:S(2)}, u32[]{:S(2)}) collective-permute-start(bf16[512,512]{1,0:T(8,128)(2,1)} %get-tuple-element.361), channel_id=1, source_target_pairs={{0,8},{8,16},{16,24},{24,0},{1,9},{9,17},{17,25},{25,1},{2,10},{10... | collective-permute-start | bytes 1572872 | tf_op jit(solution)/shard_map/ppermute | solution.py:27
  90.2 2.7 %collective-permute-start.18 = (bf16[512,512]{1,0:T(8,128)(2,1)}, bf16[512,512]{1,0:T(8,128)(2,1)S(1)}, u32[]{:S(2)}, u32[]{:S(2)}) collective-permute-start(bf16[512,512]{1,0:T(8,128)(2,1)} %get-tuple-element.362), channel_id=1, source_target_pairs={{0,16},{8,24},{16,0},{24,8},{1,17},{9,25},{17,1},{25,9},{2,18},{10... | collective-permute-start | bytes 1572872 | tf_op jit(solution)/shard_map/ppermute | solution.py:27
  92.9 1.5 %collective-permute-start.19 = (bf16[512,512]{1,0:T(8,128)(2,1)}, bf16[512,512]{1,0:T(8,128)(2,1)}, u32[]{:S(2)}, u32[]{:S(2)}) collective-permute-start(bf16[512,512]{1,0:T(8,128)(2,1)} %get-tuple-element.363), channel_id=1, source_target_pairs={{0,24},{8,0},{16,8},{24,16},{1,25},{9,1},{17,9},{25,17},{2,26},{10... | collective-permute-start | bytes 1572872 | tf_op jit(solution)/shard_map/ppermute | solution.py:27
  95.1 1.6 %leave.1.leaving = f32[3,520,128]{2,1,0:T(8,128)S(1)} custom-call(s32[256]{0:T(256)S(1)} %bitcast.35, s32[256]{0:T(256)S(1)} %fusion.9.goal_s, f32[2048]{0:T(1024)S(1)} %bitcast.33, f32[2048,128]{1,0:T(8,128)S(1)} %bitcast.28), custom_call_target="tpu_custom_call" | custom-call | flops 1024 | bytes 1048576 | tf_op jit(solution)/shard_map/leave/pallas_call | solution.py:489
  96.7 14.3 %all_to_all.5.blocks = bf16[8,16,1024]{2,1,0:T(8,128)(2,1)S(1)} all-to-all(bf16[8,16,1024]{2,1,0:T(8,128)(2,1)S(1)} %convert_element_type.67), channel_id=1, replica_groups=mesh['tbl_0'=8,'tbl_1'=4,'tbl_2'=2,'hst'=4] {'tbl_0'}, dimensions={0} | all-to-all | bytes 524288 | tf_op jit(solution)/shard_map/all_to_all | solution.py:499
  111.0 1.2 finish.1
  112.2 4.3 %collective-permute-done.18.refs_2_ = bf16[512,512]{1,0:T(8,128)(2,1)S(1)} collective-permute-done((bf16[512,512]{1,0:T(8,128)(2,1)}, bf16[512,512]{1,0:T(8,128)(2,1)S(1)}, u32[]{:S(2)}, u32[]{:S(2)}) %collective-permute-start.18) | collective-permute-done | bytes 524320 | tf_op jit(solution)/shard_map/ppermute | solution.py:27
  116.5 2.5 %evict.1 = (bf16[2048,256]{1,0:T(8,128)(2,1)S(1)}, f32[136,128]{1,0:T(8,128)S(1)}, f32[136,128]{1,0:T(8,128)S(1)}, f32[136,128]{1,0:T(8,128)S(1)}, f32[136,128]{1,0:T(8,128)S(1)}) custom-call(f32[1,2048]{1,0:T(1,128)S(1)} %convert_element_type.63.slot_map, f32[3,520,128]{2,1,0:T(8,128)S(1)} %leave.1.leaving, ...), custom_call_target="tpu_custom_call" | custom-call | flops 536870912 | bytes 4194304 | tf_op jit(solution)/shard_map/evict/pallas_call | solution.py:509
  119.0 1.0 collective-permute-start.20
  120.0 1.8 %collective-permute-start.21 = (f32[136,128]{1,0:T(8,128)S(1)}, f32[136,128]{1,0:T(8,128)S(1)}, u32[]{:S(2)}, u32[]{:S(2)}) collective-permute-start(f32[136,128]{1,0:T(8,128)S(1)} %get-tuple-element.369), channel_id=1, source_target_pairs={{0,2},{1,3},{2,0},{3,1},{4,6},{5,7},{6,4},{7,5},{8,10},{9,11},{10,... | collective-permute-start | bytes 208904 | tf_op jit(solution)/shard_map/ppermute | solution.py:27
  121.8 2.5 %collective-permute-start.22 = (f32[136,128]{1,0:T(8,128)S(1)}, f32[136,128]{1,0:T(8,128)S(1)}, u32[]{:S(2)}, u32[]{:S(2)}) collective-permute-start(f32[136,128]{1,0:T(8,128)S(1)} %get-tuple-element.370), channel_id=1, source_target_pairs={{0,3},{1,0},{2,1},{3,2},{4,7},{5,4},{6,5},{7,6},{8,11},{9,8},{10,9... | collective-permute-start | bytes 208904 | tf_op jit(solution)/shard_map/ppermute | solution.py:27
  124.4 4.3 %update.1 = (f32[2048,128]{1,0:T(8,128)}, f32[16,128]{1,0:T(8,128)}) custom-call(f32[1,2048]{1,0:T(1,128)S(1)} %convert_element_type.63.slot_map, bf16[2048,256]{1,0:T(8,128)(2,1)S(1)} %get-tuple-element.364.rhs, f32[2048,128]{1,0:T(8,128)S(1)} %bitcast.29, f32[16,128]{1,0:T(8,128)S(1)} %bitcast.34), custom_call_target="tpu_custom_call" | custom-call | flops 2147483648 | bytes 4194304 | tf_op jit(solution)/shard_map/update/pallas_call | solution.py:519
  128.7 1.3 arrive.1
  (57 shorter events, 1.3 us)
Async XLA Ops:
  1.3 12.2 %copy-start.2 = (s32[2,512,8]{1,2,0:T(8,128)S(1)}, s32[2,512,8]{1,2,0:T(8,128)}, u32[]{:S(2)}) copy-start(s32[2,512,8]{1,2,0:T(8,128)} %param.16) | copy-start | bytes 98308
  1.3 12.2 %copy-start.3 = (s32[2,512,8]{1,2,0:T(8,128)S(1)}, s32[2,512,8]{1,2,0:T(8,128)}, u32[]{:S(2)}) copy-start(s32[2,512,8]{1,2,0:T(8,128)} %param.17) | copy-start | bytes 98308
  1.3 12.2 %copy-start.4 = (bf16[2,512,8]{1,2,0:T(8,128)(2,1)S(1)}, bf16[2,512,8]{1,2,0:T(8,128)(2,1)}, u32[]{:S(2)}) copy-start(bf16[2,512,8]{1,2,0:T(8,128)(2,1)} %param.18) | copy-start | bytes 49156
  1.3 12.2 %copy-start.7 = (s32[2,512]{1,0:T(2,128)S(1)}, s32[2,512]{1,0:T(2,128)}, u32[]{:S(2)}) copy-start(s32[2,512]{1,0:T(2,128)} %lens) | copy-start | bytes 12292
  1.3 30.3 %copy-start.6 = (s32[4]{0:T(128)S(1)}, s32[4]{0:T(128)}, u32[]{:S(2)}) copy-start(s32[4]{0:T(128)} %pad_add_fusion.pos) | copy-start | bytes 52
  1.3 30.3 %copy-start.9 = (bf16[512,1024]{1,0:T(8,128)(2,1)S(1)}, bf16[512,1024]{1,0:T(8,128)(2,1)}, u32[]{:S(2)}) copy-start(bf16[512,1024]{1,0:T(8,128)(2,1)} %pooled.3) | copy-start | bytes 3145732
  8.5 9.6 %collective-permute-start = (bf16[1024,128]{1,0:T(8,128)(2,1)}, bf16[1024,128]{1,0:T(8,128)(2,1)S(1)}, u32[]{:S(2)}, u32[]{:S(2)}) collective-permute-start(bf16[1024,128]{1,0:T(8,128)(2,1)} %get-tuple-element.190), channel_id=1, source_target_pairs={{0,1},{1,2},{2,3},{3,0},{4,5},{5,6},{6,7},{7,4},{8,9},{9,10},{10,1... | collective-permute-start | bytes 786440 | tf_op jit(solution)/shard_map/ppermute | solution.py:27
  10.1 10.9 %collective-permute-start.1 = (bf16[1024,128]{1,0:T(8,128)(2,1)}, bf16[1024,128]{1,0:T(8,128)(2,1)S(1)}, u32[]{:S(2)}, u32[]{:S(2)}) collective-permute-start(bf16[1024,128]{1,0:T(8,128)(2,1)} %get-tuple-element.191), channel_id=1, source_target_pairs={{0,2},{1,3},{2,0},{3,1},{4,6},{5,7},{6,4},{7,5},{8,10},{9,11},{10,... | collective-permute-start | bytes 786440 | tf_op jit(solution)/shard_map/ppermute | solution.py:27
  12.8 11.6 %collective-permute-start.2 = (bf16[1024,128]{1,0:T(8,128)(2,1)}, bf16[1024,128]{1,0:T(8,128)(2,1)S(1)}, u32[]{:S(2)}, u32[]{:S(2)}) collective-permute-start(bf16[1024,128]{1,0:T(8,128)(2,1)} %get-tuple-element.192), channel_id=1, source_target_pairs={{0,3},{1,0},{2,1},{3,2},{4,7},{5,4},{6,5},{7,6},{8,11},{9,8},{10,9... | collective-permute-start | bytes 786440 | tf_op jit(solution)/shard_map/ppermute | solution.py:27
  24.4 1.0 copy-start.1
  25.6 12.2 %collective-permute-start.4 = (bf16[1280,128]{1,0:T(8,128)(2,1)S(1)}, bf16[1280,128]{1,0:T(8,128)(2,1)S(1)}, u32[]{:S(2)}, u32[]{:S(2)}) collective-permute-start(bf16[1280,128]{1,0:T(8,128)(2,1)S(1)} %own.1.refs_0_), channel_id=1, source_target_pairs={{0,224},{32,0},{64,32},{96,64},{128,96},{160,128},{192,160},{224,1... | collective-permute-start | bytes 983048 | tf_op jit(solution)/shard_map/ppermute | solution.py:27
  31.5 9.7 %collective-permute-start.3 = (bf16[1280,128]{1,0:T(8,128)(2,1)S(1)}, bf16[1280,128]{1,0:T(8,128)(2,1)S(1)}, u32[]{:S(2)}, u32[]{:S(2)}) collective-permute-start(bf16[1280,128]{1,0:T(8,128)(2,1)S(1)} %own.1.refs_0_), channel_id=1, source_target_pairs={{0,32},{32,64},{64,96},{96,128},{128,160},{160,192},{192,224},{224... | collective-permute-start | bytes 983048 | tf_op jit(solution)/shard_map/ppermute | solution.py:27
  31.5 1.2 copy-start.10
  41.2 6.1 %collective-permute-start.7 = (f32[4,8,16,1024]{3,2,1,0:T(8,128)S(1)}, f32[4,8,16,1024]{3,2,1,0:T(8,128)S(1)}, u32[]{:S(2)}, u32[]{:S(2)}) collective-permute-start(f32[4,8,16,1024]{3,2,1,0:T(8,128)S(1)} %get-tuple-element.223), channel_id=1, source_target_pairs={{0,4},{4,0},{1,5},{5,1},{2,6},{6,2},{3,7},{7,3},{8,12},{12,8},{9,1... | collective-permute-start | bytes 6291464 | tf_op jit(solution)/shard_map/ppermute | solution.py:27
  41.2 11.3 %collective-permute-start.5 = (bf16[1280,128]{1,0:T(8,128)(2,1)S(1)}, bf16[1280,128]{1,0:T(8,128)(2,1)S(1)}, u32[]{:S(2)}, u32[]{:S(2)}) collective-permute-start(bf16[1280,128]{1,0:T(8,128)(2,1)S(1)} %collective-permute-done.3.refs_0_), channel_id=1, source_target_pairs={{0,32},{32,64},{64,96},{96,128},{128,160},{160,192},{192,224},{224... | collective-permute-start | bytes 983048 | tf_op jit(solution)/shard_map/ppermute | solution.py:27
  41.3 11.3 %collective-permute-start.6 = (bf16[1280,128]{1,0:T(8,128)(2,1)S(1)}, bf16[1280,128]{1,0:T(8,128)(2,1)S(1)}, u32[]{:S(2)}, u32[]{:S(2)}) collective-permute-start(bf16[1280,128]{1,0:T(8,128)(2,1)S(1)} %collective-permute-done.4.refs_1_), channel_id=1, source_target_pairs={{0,224},{32,0},{64,32},{96,64},{128,96},{160,128},{192,160},{224,1... | collective-permute-start | bytes 983048 | tf_op jit(solution)/shard_map/ppermute | solution.py:27
  52.6 11.8 %collective-permute-start.8 = (bf16[1280,128]{1,0:T(8,128)(2,1)S(1)}, bf16[1280,128]{1,0:T(8,128)(2,1)S(1)}, u32[]{:S(2)}, u32[]{:S(2)}) collective-permute-start(bf16[1280,128]{1,0:T(8,128)(2,1)S(1)} %collective-permute-done.5.refs_0_), channel_id=1, source_target_pairs={{0,32},{32,64},{64,96},{96,128},{128,160},{160,192},{192,224},{224... | collective-permute-start | bytes 983048 | tf_op jit(solution)/shard_map/ppermute | solution.py:27
  52.6 11.8 %collective-permute-start.9 = (bf16[1280,128]{1,0:T(8,128)(2,1)S(1)}, bf16[1280,128]{1,0:T(8,128)(2,1)S(1)}, u32[]{:S(2)}, u32[]{:S(2)}) collective-permute-start(bf16[1280,128]{1,0:T(8,128)(2,1)S(1)} %collective-permute-done.6.refs_1_), channel_id=1, source_target_pairs={{0,224},{32,0},{64,32},{96,64},{128,96},{160,128},{192,160},{224,1... | collective-permute-start | bytes 983048 | tf_op jit(solution)/shard_map/ppermute | solution.py:27
  55.8 13.5 %collective-permute-start.12 = (bf16[8,16,1024]{2,1,0:T(8,128)(2,1)S(1)}, bf16[8,16,1024]{2,1,0:T(8,128)(2,1)S(1)}, u32[]{:S(2)}, u32[]{:S(2)}) collective-permute-start(bf16[8,16,1024]{2,1,0:T(8,128)(2,1)S(1)} %get-tuple-element.270), channel_id=1, source_target_pairs={{0,8},{8,16},{16,24},{24,0},{1,9},{9,17},{17,25},{25,1},{2,10},{10... | collective-permute-start | bytes 786440 | tf_op jit(solution)/shard_map/ppermute | solution.py:27
  57.3 13.7 %collective-permute-start.13 = (bf16[8,16,1024]{2,1,0:T(8,128)(2,1)S(1)}, bf16[8,16,1024]{2,1,0:T(8,128)(2,1)S(1)}, u32[]{:S(2)}, u32[]{:S(2)}) collective-permute-start(bf16[8,16,1024]{2,1,0:T(8,128)(2,1)S(1)} %get-tuple-element.271), channel_id=1, source_target_pairs={{0,16},{8,24},{16,0},{24,8},{1,17},{9,25},{17,1},{25,9},{2,18},{10... | collective-permute-start | bytes 786440 | tf_op jit(solution)/shard_map/ppermute | solution.py:27
  60.0 11.0 %collective-permute-start.14 = (bf16[8,16,1024]{2,1,0:T(8,128)(2,1)S(1)}, bf16[8,16,1024]{2,1,0:T(8,128)(2,1)S(1)}, u32[]{:S(2)}, u32[]{:S(2)}) collective-permute-start(bf16[8,16,1024]{2,1,0:T(8,128)(2,1)S(1)} %get-tuple-element.272), channel_id=1, source_target_pairs={{0,24},{8,0},{16,8},{24,16},{1,25},{9,1},{17,9},{25,17},{2,26},{10... | collective-permute-start | bytes 786440 | tf_op jit(solution)/shard_map/ppermute | solution.py:27
  64.4 6.6 %collective-permute-start.11 = (bf16[640,128]{1,0:T(8,128)(2,1)S(1)}, bf16[640,128]{1,0:T(8,128)(2,1)S(1)}, u32[]{:S(2)}, u32[]{:S(2)}) collective-permute-start(bf16[640,128]{1,0:T(8,128)(2,1)S(1)} %slice.26), channel_id=1, source_target_pairs={{0,224},{32,0},{64,32},{96,64},{128,96},{160,128},{192,160},{224,1... | collective-permute-start | bytes 491528 | tf_op jit(solution)/shard_map/ppermute | solution.py:27
  66.2 6.5 %collective-permute-start.10 = (bf16[640,128]{1,0:T(8,128)(2,1)S(1)}, bf16[640,128]{1,0:T(8,128)(2,1)S(1)}, u32[]{:S(2)}, u32[]{:S(2)}) collective-permute-start(bf16[640,128]{1,0:T(8,128)(2,1)S(1)} %slice.25), channel_id=1, source_target_pairs={{0,32},{32,64},{64,96},{96,128},{128,160},{160,192},{192,224},{224... | collective-permute-start | bytes 491528 | tf_op jit(solution)/shard_map/ppermute | solution.py:27
  76.9 4.1 %collective-permute-start.15 = (bf16[4,256,512]{2,1,0:T(8,128)(2,1)S(1)}, bf16[4,256,512]{2,1,0:T(8,128)(2,1)S(1)}, u32[]{:S(2)}, u32[]{:S(2)}) collective-permute-start(bf16[4,256,512]{2,1,0:T(8,128)(2,1)S(1)} %send0.1), channel_id=1, source_target_pairs={{0,4},{4,0},{1,5},{5,1},{2,6},{6,2},{3,7},{7,3},{8,12},{12,8},{9,1... | collective-permute-start | bytes 3145736 | tf_op jit(solution)/shard_map/ppermute | solution.py:27
  79.5 2.9 %collective-permute-start.16 = (bf16[4,256,512]{2,1,0:T(8,128)(2,1)S(1)}, bf16[4,256,512]{2,1,0:T(8,128)(2,1)S(1)}, u32[]{:S(2)}, u32[]{:S(2)}) collective-permute-start(bf16[4,256,512]{2,1,0:T(8,128)(2,1)S(1)} %send1.1), channel_id=1, source_target_pairs={{0,4},{4,0},{1,5},{5,1},{2,6},{6,2},{3,7},{7,3},{8,12},{12,8},{9,1... | collective-permute-start | bytes 3145736 | tf_op jit(solution)/shard_map/ppermute | solution.py:27
  80.9 13.4 %copy-start.12 = (s32[1,1,256]{2,1,0:T(1,128)S(1)}, s32[1,1,256]{2,1,0:T(1,128)}, u32[]{:S(2)}) copy-start(s32[1,1,256]{2,1,0:T(1,128)} %param.24) | copy-start | bytes 3076
  81.0 13.7 %copy-start.11 = (s32[1,1,2048]{2,1,0:T(1,128)S(1)}, s32[1,1,2048]{2,1,0:T(1,128)}, u32[]{:S(2)}) copy-start(s32[1,1,2048]{2,1,0:T(1,128)} %param.20) | copy-start | bytes 24580
  81.0 14.1 %copy-start = (f32[1,1,2048,128]{3,2,1,0:T(8,128)S(1)}, f32[1,1,2048,128]{3,2,1,0:T(8,128)}, u32[]{:S(2)}) copy-start(f32[1,1,2048,128]{3,2,1,0:T(8,128)} %param.21) | copy-start | bytes 3145732
  81.0 14.1 %copy-start.5 = (f32[1,1,2048]{2,1,0:T(1,128)S(1)}, f32[1,1,2048]{2,1,0:T(1,128)}, u32[]{:S(2)}) copy-start(f32[1,1,2048]{2,1,0:T(1,128)} %param.22) | copy-start | bytes 24580
  81.0 14.1 %copy-start.8 = (s32[1,1,256]{2,1,0:T(1,128)S(1)}, s32[1,1,256]{2,1,0:T(1,128)}, u32[]{:S(2)}) copy-start(s32[1,1,256]{2,1,0:T(1,128)} %param.23) | copy-start | bytes 3076
  88.7 23.5 %collective-permute-start.17 = (bf16[512,512]{1,0:T(8,128)(2,1)}, bf16[512,512]{1,0:T(8,128)(2,1)S(1)}, u32[]{:S(2)}, u32[]{:S(2)}) collective-permute-start(bf16[512,512]{1,0:T(8,128)(2,1)} %get-tuple-element.361), channel_id=1, source_target_pairs={{0,8},{8,16},{16,24},{24,0},{1,9},{9,17},{17,25},{25,1},{2,10},{10... | collective-permute-start | bytes 1572872 | tf_op jit(solution)/shard_map/ppermute | solution.py:27
  90.2 26.3 %collective-permute-start.18 = (bf16[512,512]{1,0:T(8,128)(2,1)}, bf16[512,512]{1,0:T(8,128)(2,1)S(1)}, u32[]{:S(2)}, u32[]{:S(2)}) collective-permute-start(bf16[512,512]{1,0:T(8,128)(2,1)} %get-tuple-element.362), channel_id=1, source_target_pairs={{0,16},{8,24},{16,0},{24,8},{1,17},{9,25},{17,1},{25,9},{2,18},{10... | collective-permute-start | bytes 1572872 | tf_op jit(solution)/shard_map/ppermute | solution.py:27
  92.9 23.6 %collective-permute-start.19 = (bf16[512,512]{1,0:T(8,128)(2,1)}, bf16[512,512]{1,0:T(8,128)(2,1)}, u32[]{:S(2)}, u32[]{:S(2)}) collective-permute-start(bf16[512,512]{1,0:T(8,128)(2,1)} %get-tuple-element.363), channel_id=1, source_target_pairs={{0,24},{8,0},{16,8},{24,16},{1,25},{9,1},{17,9},{25,17},{2,26},{10... | collective-permute-start | bytes 1572872 | tf_op jit(solution)/shard_map/ppermute | solution.py:27
  119.0 9.7 %collective-permute-start.20 = (f32[136,128]{1,0:T(8,128)S(1)}, f32[136,128]{1,0:T(8,128)S(1)}, u32[]{:S(2)}, u32[]{:S(2)}) collective-permute-start(f32[136,128]{1,0:T(8,128)S(1)} %get-tuple-element.368), channel_id=1, source_target_pairs={{0,1},{1,2},{2,3},{3,0},{4,5},{5,6},{6,7},{7,4},{8,9},{9,10},{10,1... | collective-permute-start | bytes 208904 | tf_op jit(solution)/shard_map/ppermute | solution.py:27
  120.0 8.7 %collective-permute-start.21 = (f32[136,128]{1,0:T(8,128)S(1)}, f32[136,128]{1,0:T(8,128)S(1)}, u32[]{:S(2)}, u32[]{:S(2)}) collective-permute-start(f32[136,128]{1,0:T(8,128)S(1)} %get-tuple-element.369), channel_id=1, source_target_pairs={{0,2},{1,3},{2,0},{3,1},{4,6},{5,7},{6,4},{7,5},{8,10},{9,11},{10,... | collective-permute-start | bytes 208904 | tf_op jit(solution)/shard_map/ppermute | solution.py:27
  121.8 6.8 %collective-permute-start.22 = (f32[136,128]{1,0:T(8,128)S(1)}, f32[136,128]{1,0:T(8,128)S(1)}, u32[]{:S(2)}, u32[]{:S(2)}) collective-permute-start(f32[136,128]{1,0:T(8,128)S(1)} %get-tuple-element.370), channel_id=1, source_target_pairs={{0,3},{1,0},{2,1},{3,2},{4,7},{5,4},{6,5},{7,6},{8,11},{9,8},{10,9... | collective-permute-start | bytes 208904 | tf_op jit(solution)/shard_map/ppermute | solution.py:27
